TPU v7x, 32 devices: a whole 2x2x4 slice. The times are simulated.
32 devices in a mesh: gx: 4 (over x, core), gy: 8 (over z, y).
Axes of the slice: x: 2, y: 2, z: 4, core: 2. Of those that a mesh axis runs over, the one named last changes fastest.
Arguments:
- field: float32 [5, 1, 128, 1024], P(None, None, 'gx', 'gy'), may hold values from -6 to 6
- cotangent: float32 [5, 1, 128, 1024], P(None, None, 'gx', 'gy'), may hold values from -6 to 6
- lift: float32 [15, 32], replicated, may hold values from -1.5 to 1.5
- spectral: float32 [2, 2, 64, 32, 32], replicated, may hold values from -6 to 6
- pointwise: float32 [2, 32, 32], replicated, may hold values from -1 to 1
- project: float32 [32, 5], replicated, may hold values from -1 to 1
Outputs:
- field_grad: float32 [5, 1, 128, 1024], P(None, None, 'gx', 'gy')
All inputs are finite; a program needn't handle non-finite values.
Results may differ from a plain program's by a relative error of at most 0.0003.
Values sent between devices are 32-bit elements; how exact they have to be, the bound alone decides.
No kernel may reach another device: no remote copies, remote signals or barrier semaphores. Data moves between devices by JAX's collectives and lax.ppermute only.
A program may use at most 64 MiB of HBM per device.

v0:
```python
import functools

import jax
import jax.numpy as jnp
import numpy as np
from jax import lax
from jax.experimental import pallas as pl
from jax.experimental.pallas import tpu as pltpu
from jax.sharding import PartitionSpec as P

MODES = 8
F32 = jnp.float32
BF16 = jnp.bfloat16
HIGHEST = lax.Precision.HIGHEST
SQRT_HALF = float(np.sqrt(0.5))
INV_SQRT_2PI = float(1.0 / np.sqrt(2.0 * np.pi))


class Ring:
    def __init__(self, count):
        self.count = count
        self.whole = count <= 7
        self.offsets = list(range(count)) if self.whole else [0, 1, 2, 3, -3, -2, -1]

    def place(self, offset):
        if self.whole:
            return offset % self.count
        return self.offsets.index(max(-3, min(3, offset)))


def split(value):
    high = value.astype(BF16)
    return high, (value - high.astype(F32)).astype(BF16)


def dot(left, right):
    return jnp.dot(left, right, preferred_element_type=F32)


def dot_t(left, right):
    return lax.dot_general(left, right, (((1,), (1,)), ((), ())), precision=HIGHEST, preferred_element_type=F32)


def exact_dot(left, right):
    return jnp.dot(left, right, precision=HIGHEST, preferred_element_type=F32)


def stacked(value):
    high, low = split(value)
    top = jnp.concatenate([high, high], axis=1)
    bottom = jnp.concatenate([low, jnp.zeros_like(low)], axis=1)
    return jnp.concatenate([top, bottom], axis=0)


def halves(value):
    rows = value.shape[0] // 2
    return value[:rows] + value[rows:]


def row_pool_matrix(cols):
    half = cols // 2
    out = np.zeros((2 * cols, cols), np.float32)
    for j in range(cols):
        out[j, j // 2] = 0.25
        out[cols + j, half + j // 2] = 0.25
    return out


def quarter_matrix(cols):
    half, quarter, eighth = cols // 2, cols // 4, cols // 8
    out = np.zeros((5 * cols, cols), np.float32)
    for lane in range(cols):
        coarse = lane - eighth * 3
        d, t = coarse // quarter, coarse % quarter
        for m in (2 * t, 2 * t + 1, half + 2 * t, half + 2 * t + 1):
            out[(d + 2) * cols + m, lane] = 0.25
    return out


def angle_tables(rows, cols):
    m = np.arange(MODES * MODES)
    wave_x, wave_y = m // MODES - MODES // 2, m % MODES
    a = 2.0 * np.pi * ((np.arange(rows)[:, None] * wave_x[None]) % rows) / rows
    b = 2.0 * np.pi * ((np.arange(cols)[:, None] * wave_y[None]) % cols) / cols
    scale = 1.0 / np.sqrt(rows * cols)
    x = np.concatenate([np.cos(a), -np.sin(a)], 1)
    y = np.concatenate([-np.sin(a), -np.cos(a)], 1)
    b1 = np.concatenate([np.cos(b), np.cos(b)], 1) * scale
    b2 = np.concatenate([np.sin(b), np.sin(b)], 1) * scale
    return [v.astype(np.float32) for v in (x, y, b1, b2)]


def table_kernel(x_ref, y_ref, b1_ref, b2_ref, xt_ref, yt_ref, b1t_ref, b2t_ref, table_ref, flipped_ref):
    rows = x_ref.shape[0]
    cols, modes = b1_ref.shape
    for i in range(rows):
        piece = x_ref[i : i + 1, :] * b1_ref[...] + y_ref[i : i + 1, :] * b2_ref[...]
        high, low = split(piece)
        table_ref[i * cols : (i + 1) * cols, :modes] = high
        table_ref[i * cols : (i + 1) * cols, modes:] = low
        piece = xt_ref[:, i : i + 1] * b1t_ref[...] + yt_ref[:, i : i + 1] * b2t_ref[...]
        high, low = split(piece)
        flipped_ref[:modes, i * cols : (i + 1) * cols] = high
        flipped_ref[modes:, i * cols : (i + 1) * cols] = low


def pool_kernel(field_ref, pool_ref, out_ref):
    count = field_ref.shape[0] // 4
    rows = [field_ref[pl.ds(k, count, stride=4), :] for k in range(4)]
    pairs = jnp.concatenate([rows[0] + rows[1], rows[2] + rows[3]], axis=1)
    out_ref[...] = exact_dot(pairs, pool_ref[...])


def mix(weights, layer, coefficients, swap_ref):
    width, lanes = coefficients.shape
    half = lanes // 2
    lane = lax.broadcasted_iota(jnp.int32, (width, lanes), 1)
    swapped = pltpu.roll(coefficients, half, 1)
    signed = jnp.where(lane < half, coefficients, -coefficients)
    total_real = jnp.zeros((width, lanes), F32)
    total_imag = jnp.zeros((width, lanes), F32)
    for w in range(width):
        block = weights[layer, w]
        total_real += block * signed[w : w + 1]
        total_imag += block * swapped[w : w + 1]
    total_real += pltpu.roll(total_real, half, 1)
    total_imag += pltpu.roll(total_imag, half, 1)
    return jnp.where(lane < half, total_real, total_imag)


def unmix(weights, layer, grads, swap_ref):
    width, lanes = grads.shape
    half = lanes // 2
    lane = lax.broadcasted_iota(jnp.int32, (width, lanes), 1)
    turned = pltpu.roll(grads, half, 1)
    turned = jnp.where(lane < half, turned, -turned)
    for w in range(width):
        block = weights[layer, w]
        swap_ref[0, w : w + 1, :] = jnp.sum(block * grads, axis=0, keepdims=True)
        swap_ref[1, w : w + 1, :] = jnp.sum(block * turned, axis=0, keepdims=True)
    real, imag = swap_ref[0], swap_ref[1]
    real += pltpu.roll(real, half, 1)
    imag += pltpu.roll(imag, half, 1)
    return jnp.where(lane < half, real, imag)


def contract(pair_ref, table_ref):
    both = dot(pair_ref[...], table_ref[...])
    rows, modes = both.shape[0] // 2, both.shape[1] // 2
    return both[:rows, :modes] + both[:rows, modes:] + both[rows:, :modes]


def network_kernel(
    ring, chunk,
    core_ref, field_ref, blocks_ref, near_a, near_b, swap_a, swap_b, cotangent_ref, lift_ref, lift_t_ref, weights,
    pointwise_ref, pointwise_t_ref, project_ref, quarter_ref, quarter_t_ref, table_ref, flipped_ref,
    own_ref, center_ref, keep_a, keep_b, give_a, give_b,
    x_ref, window_ref, feature_pair, hidden_pair, grad_pair, target_pair, slope_one, swap_ref, target_ref, grad_x_ref,
):
    channels, rows, cols = field_ref.shape
    tall = rows // 4
    half, quarter = cols // 2, cols // 4
    cells = rows * cols
    width = pointwise_ref.shape[1]
    padded = x_ref.shape[0] // rows
    odd = core_ref[0] == 1
    lane = lax.broadcasted_iota(jnp.int32, (1, 1, cols), 2)

    for d in range(-2, 3):
        for e in range(-2, 3):
            here = ring.place(e)
            if d == 0:
                block = blocks_ref[here]
            else:
                there = jnp.where(odd, ring.place(e + 1), ring.place(e - 1))
                direct, swapped = (near_a, swap_a) if d > 0 else (near_b, swap_b)
                block = jnp.where(odd == (abs(d) == 1), direct[here], swapped[there])
            if e == -2:
                window_ref[d + 2, :, : tall // 2, :] = block[:, tall // 2 :, :]
            elif e == 2:
                window_ref[d + 2, :, 4 * tall - tall // 2 :, :] = block[:, : tall // 2, :]
            else:
                first = tall // 2 + (e + 1) * tall
                window_ref[d + 2, :, first : first + tall, :] = block

    for c in range(channels):
        x_ref[c * rows : (c + 1) * rows, :] = field_ref[c]
    previous, own, following = (window_ref[d, :, tall : 3 * tall, :] for d in (1, 2, 3))

    def turn(value, steps):
        flat = value.reshape(channels * 2 * tall, cols)
        return pltpu.roll(flat, steps % cols, 1).reshape(value.shape)

    def three(a, b, c):
        return jnp.where(lane < quarter, a, jnp.where(lane < 3 * quarter, b, c))

    even_rows = three(turn(previous, -quarter), turn(own, quarter), turn(following, -quarter))
    odd_rows = three(turn(previous, quarter), turn(own, -quarter), turn(following, quarter))
    for c in range(channels):
        first = (channels + c) * rows
        x_ref[pl.ds(first, 2 * tall, stride=2), :] = even_rows[c]
        x_ref[pl.ds(first + 1, 2 * tall, stride=2), :] = odd_rows[c]
    pieces = []
    for d in range(5):
        high, low = split(window_ref[d].reshape(channels * rows, cols))
        pieces.append(jnp.concatenate([high, low], axis=0))
    far = halves(dot(jnp.concatenate(pieces, axis=1), quarter_ref[...]))
    x_ref[2 * channels * rows : 3 * channels * rows, :] = far
    for c in range(3 * channels, padded):
        x_ref[c * rows : (c + 1) * rows, :] = jnp.zeros((rows, cols), F32)

    target_ref[channels * rows :, :] = jnp.zeros((target_ref.shape[0] - channels * rows, cols), F32)
    for c in range(channels):
        target_ref[c * rows : (c + 1) * rows, :] = cotangent_ref[c]
    small = target_ref.shape[0] // rows
    for i in range(rows):
        at = slice(i * cols, (i + 1) * cols)
        high, low = split(x_ref[pl.ds(i, padded, stride=rows), :])
        feature_pair[:padded, at] = high
        feature_pair[padded:, at] = low
        value = target_ref[pl.ds(i, small, stride=rows), :]
        high = value.astype(BF16).astype(F32)
        target_pair[:, at] = jnp.concatenate([high, value - high], axis=0).astype(BF16)

    lift = lift_ref[...]
    lift_t = lift_t_ref[...]
    steps = [slice(k, k + chunk) for k in range(0, cells, chunk)]

    mixed = mix(weights, 0, exact_dot(lift_t, contract(feature_pair, table_ref)), swap_ref)
    wave = stacked(mixed)
    local = stacked(exact_dot(pointwise_t_ref[0], lift_t))
    for at in steps:
        u = halves(dot(wave, flipped_ref[:, at]) + dot(local, feature_pair[:, at]))
        cdf = 0.5 + 0.5 * lax.erf(u * SQRT_HALF)
        slope_one[:, at] = cdf + u * (INV_SQRT_2PI * jnp.exp(-0.5 * u * u))
        high, low = split(u * cdf)
        hidden_pair[:width, at] = high
        hidden_pair[width:, at] = low

    mixed = mix(weights, 1, contract(hidden_pair, table_ref), swap_ref)
    wave = stacked(mixed)
    local = stacked(pointwise_t_ref[1])
    out = stacked(project_ref[...])
    for at in steps:
        u = halves(dot(wave, flipped_ref[:, at]) + dot(local, hidden_pair[:, at]))
        cdf = 0.5 + 0.5 * lax.erf(u * SQRT_HALF)
        slope = cdf + u * (INV_SQRT_2PI * jnp.exp(-0.5 * u * u))
        high, low = split(slope * halves(dot(out, target_pair[:, at])))
        grad_pair[:width, at] = high
        grad_pair[width:, at] = low
    wave = stacked(unmix(weights, 1, contract(grad_pair, table_ref), swap_ref))
    local = stacked(pointwise_ref[1])
    for at in steps:
        g = halves(dot(wave, flipped_ref[:, at]) + dot(local, grad_pair[:, at]))
        high, low = split(g * slope_one[:, at])
        hidden_pair[:width, at] = high
        hidden_pair[width:, at] = low

    wave = stacked(exact_dot(lift, unmix(weights, 0, contract(hidden_pair, table_ref), swap_ref)))
    local = stacked(exact_dot(lift, pointwise_ref[0]))
    for k, at in enumerate(steps):
        g = halves(dot(wave, flipped_ref[:, at]) + dot(local, hidden_pair[:, at]))
        for n in range(chunk // cols):
            grad_x_ref[pl.ds(k * (chunk // cols) + n, padded, stride=rows), :] = g[:, n * cols : (n + 1) * cols]

    for c in range(channels):
        own_ref[c] = grad_x_ref[c * rows : (c + 1) * rows, :]

    even_grads, odd_grads = [], []
    for c in range(channels):
        first = (channels + c) * rows
        even_grads.append(grad_x_ref[pl.ds(first, 2 * tall, stride=2), :][None])
        odd_grads.append(grad_x_ref[pl.ds(first + 1, 2 * tall, stride=2), :][None])
    even_grads = jnp.concatenate(even_grads, axis=0)
    odd_grads = jnp.concatenate(odd_grads, axis=0)
    even_up, even_down = turn(even_grads, quarter), turn(even_grads, -quarter)
    odd_up, odd_down = turn(odd_grads, quarter), turn(odd_grads, -quarter)
    zero = jnp.zeros_like(even_grads)

    def four(a, b, c, d):
        return jnp.where(lane < quarter, a, jnp.where(lane < half, b, jnp.where(lane < 3 * quarter, c, d)))

    near = {
        -1: four(zero, even_up, zero, odd_down),
        0: four(even_down, even_down, odd_up, odd_up),
        1: four(even_up, zero, odd_down, zero),
    }
    high, low = split(grad_x_ref[2 * channels * rows : 3 * channels * rows, :])
    spread = halves(dot(jnp.concatenate([high, low], axis=0), quarter_t_ref[...]))
    for d in range(5):
        window_ref[d] = spread[:, d * cols : (d + 1) * cols].reshape(channels, rows, cols)
    for d in (-1, 0, 1):
        window_ref[d + 2, :, tall : 3 * tall, :] += near[d]

    def block_of(d, e):
        if abs(e) < 2:
            first = tall // 2 + (e + 1) * tall
            return window_ref[d + 2, :, first : first + tall, :]
        low_part = window_ref[d + 2, :, 4 * tall - tall // 2 :, :]
        high_part = window_ref[d + 2, :, : tall // 2, :]
        if not (ring.whole and ring.count == 4):
            low_part, high_part = (low_part, jnp.zeros_like(low_part)) if e > 0 else (jnp.zeros_like(low_part), high_part)
        return jnp.concatenate([low_part, high_part], axis=1)

    reached = {}
    for e in range(-2, 3):
        reached[ring.place(e)] = e
    for place in range(len(ring.offsets)):
        if place not in reached:
            for ref in (center_ref, keep_a, keep_b, give_a, give_b):
                ref[place] = jnp.zeros((channels, tall, cols), F32)
            continue
        e = reached[place]
        center_ref[place] = block_of(0, e)
        for one, two, keep, give in ((-1, -2, keep_a, give_a), (1, 2, keep_b, give_b)):
            near_block, far_block = block_of(one, e), block_of(two, e)
            keep[place] = jnp.where(odd, near_block, far_block)
            give[place] = jnp.where(odd, far_block, near_block)


def join_kernel(ring, core_ref, keep_a, keep_b, got_a, got_b, out_a, out_b):
    odd = core_ref[0] == 1
    for offset in ring.offsets:
        here = ring.place(offset)
        there = jnp.where(odd, ring.place(offset + 1), ring.place(offset - 1))
        out_a[here] = keep_a[here] + got_a[there]
        out_b[here] = keep_b[here] + got_b[there]


def gather_kernel(center_ref, a_ref, b_ref, *outs):
    for place, out in enumerate(outs):
        out[...] = center_ref[place] + a_ref[place] + b_ref[place]


def final_kernel(channels, own_ref, pool_ref, *refs):
    out_ref = refs[-1]
    total = refs[0][...]
    for ref in refs[1:-1]:
        total = total + ref[...]
    cols = total.shape[2]
    spread = dot_t(total.reshape(-1, cols), pool_ref[...])
    count = spread.shape[0]
    for k in range(4):
        part = spread[:, :cols] if k < 2 else spread[:, cols:]
        at = pl.ds(k, count, stride=4)
        out_ref[at, :] = own_ref[at, :] + part


def in_vmem(count):
    return [pl.BlockSpec(memory_space=pltpu.VMEM)] * count


SCALAR = pl.BlockSpec(memory_space=pltpu.SMEM)


def call(kernel, shapes, *operands, scalars=0, scratch=(), name=None):
    single = not isinstance(shapes, (list, tuple))
    outs = [shapes] if single else list(shapes)
    result = pl.pallas_call(
        kernel,
        out_shape=outs,
        in_specs=[SCALAR] * scalars + in_vmem(len(operands) - scalars),
        out_specs=in_vmem(len(outs)),
        scratch_shapes=list(scratch),
        compiler_params=pltpu.CompilerParams(vmem_limit_bytes=48 << 20),
        name=name,
    )(*operands)
    return result[0] if single else result


def body(field, cotangent, lift, spectral, pointwise, project):
    channels, levels, rows, cols = field.shape
    width = lift.shape[1]
    layers = spectral.shape[0]
    modes = spectral.shape[2]
    features = lift.shape[0]
    cells = rows * cols
    tall = rows // 4
    gx, gy = lax.axis_size("gx"), lax.axis_size("gy")
    ring = Ring(gx)
    blocks = len(ring.offsets)
    core = (lax.axis_index("gx") % 2).astype(jnp.int32).reshape(1)

    def shape(*dims, dtype=F32):
        return jax.ShapeDtypeStruct(dims, dtype)

    def along_x(value, steps):
        return lax.ppermute(value, "gx", [(s, (s + steps) % gx) for s in range(gx)])

    def along_y(value, even_steps, odd_steps):
        pairs = []
        for a in range(gx):
            for b in range(gy):
                steps = odd_steps if a % 2 else even_steps
                pairs.append((a * gy + b, a * gy + (b + steps) % gy))
        return lax.ppermute(value, ("gx", "gy"), pairs)

    def swap(value):
        return lax.ppermute(value, "gx", [(s, s ^ 1) for s in range(gx)])

    flat_field = field.reshape(channels * rows, cols)
    pool = jnp.asarray(row_pool_matrix(cols))
    quarter = quarter_matrix(cols)
    packed = call(pool_kernel, shape(channels * tall, cols), flat_field, pool, name="pool")
    packed = packed.reshape(channels, tall, cols)

    held = [packed] + [along_x(packed, -offset) for offset in ring.offsets[1:]]
    x, y, b1, b2 = angle_tables(rows, cols)
    table, flipped = call(
        table_kernel,
        (shape(cells, 4 * modes, dtype=BF16), shape(4 * modes, cells, dtype=BF16)),
        *(jnp.asarray(v) for v in (x, y, b1, b2, x.T.copy(), y.T.copy(), b1.T.copy(), b2.T.copy())),
        name="table",
    )
    by_mode = jnp.transpose(spectral, (0, 1, 3, 4, 2))
    weights = jnp.concatenate([by_mode[:, 0], by_mode[:, 1]], axis=-1)
    held = jnp.stack(held)
    from_a = along_y(held, -2, -1)
    from_b = along_y(held, 2, 1)
    swap_a, swap_b = swap(from_a), swap(from_b)

    padded = -(-features // 16) * 16
    lift_rows = jnp.pad(lift, ((0, padded - features), (0, 0)))
    small = -(-channels // 8) * 8
    project_cols = jnp.pad(project, ((0, 0), (0, small - channels)))
    group = shape(blocks, channels, tall, cols)
    chunk = 4 * cols
    own, center, keep_a, keep_b, give_a, give_b = call(
        functools.partial(network_kernel, ring, chunk),
        (shape(channels, rows, cols), group, group, group, group, group),
        core, field.reshape(channels, rows, cols), held, from_a, from_b, swap_a, swap_b,
        cotangent.reshape(channels, rows, cols), lift_rows, lift_rows.T, weights,
        pointwise, jnp.transpose(pointwise, (0, 2, 1)), project_cols,
        jnp.asarray(quarter, BF16), jnp.asarray(quarter.T.copy(), BF16), table, flipped,
        scalars=1,
        scratch=(
            pltpu.VMEM((padded * rows, cols), F32),
            pltpu.VMEM((5, channels, rows, cols), F32),
            pltpu.VMEM((2 * padded, cells), BF16),
            pltpu.VMEM((2 * width, cells), BF16),
            pltpu.VMEM((2 * width, cells), BF16),
            pltpu.VMEM((2 * small, cells), BF16),
            pltpu.VMEM((width, cells), F32),
            pltpu.VMEM((2, width, 2 * modes), F32),
            pltpu.VMEM((small * rows, cols), F32),
            pltpu.VMEM((padded * rows, cols), F32),
        ),
        name="network",
    )

    got_a, got_b = swap(give_a), swap(give_b)
    sum_a, sum_b = call(
        functools.partial(join_kernel, ring), (group, group), core, keep_a, keep_b, got_a, got_b, scalars=1, name="join"
    )
    sum_a, sum_b = along_y(sum_a, -2, -1), along_y(sum_b, 2, 1)
    piece = shape(channels, tall, cols)
    parts = call(gather_kernel, [piece] * blocks, center, sum_a, sum_b, name="gather")
    parts = [parts[0]] + [along_x(part, offset) for part, offset in zip(parts[1:], ring.offsets[1:])]
    out = call(
        functools.partial(final_kernel, channels),
        shape(channels * rows, cols),
        own.reshape(channels * rows, cols), pool, *parts,
        name="final",
    )
    return out.reshape(field.shape)


def solution(mesh):
    return jax.shard_map(
        body,
        mesh=mesh,
        in_specs=(P(None, None, "gx", "gy"), P(None, None, "gx", "gy"), P(), P(), P(), P()),
        out_specs=P(None, None, "gx", "gy"),
        check_vma=False,
    )
```

profile of v0, /device:TPU:0, one launch (start us, length us, event | category | flops | bytes accessed | tf_op | source)
XLA Modules:
  0.0 46.3 jit_solution(11334025263598047044)
XLA Ops:
  0.0 0.9 %copy-done.1 = f32[256,128]{1,0:T(8,128)S(1)} copy-done((f32[256,128]{1,0:T(8,128)S(1)}, f32[256,128]{1,0:T(8,128)}, u32[]{:S(2)}) %copy-start.1) | copy-done | bytes 131096
  0.9 0.9 %copy-done.3 = f32[5,1,32,128]{3,2,1,0:T(8,128)S(1)} copy-done((f32[5,1,32,128]{3,2,1,0:T(8,128)S(1)}, f32[5,1,32,128]{3,2,1,0:T(8,128)}, u32[]{:S(2)}) %copy-start.3) | copy-done | bytes 81944
  1.8 0.2 pool.1
  2.0 0.5 %collective-permute-start.2 = (f32[5,8,128]{2,1,0:T(8,128)S(1)}, f32[5,8,128]{2,1,0:T(8,128)S(1)}, u32[]{:S(2)}, u32[]{:S(2)}) collective-permute-start(f32[5,8,128]{2,1,0:T(8,128)S(1)} %bitcast.26), channel_id=1, source_target_pairs={{0,8},{8,16},{16,24},{24,0},{1,9},{9,17},{17,25},{25,1},{2,10},{10... | collective-permute-start | bytes 61448 | tf_op jit(solution)/shard_map/ppermute | solution.py:388
  2.5 2.6 %collective-permute-start.1 = (f32[5,8,128]{2,1,0:T(8,128)S(1)}, f32[5,8,128]{2,1,0:T(8,128)S(1)}, u32[]{:S(2)}, u32[]{:S(2)}) collective-permute-start(f32[5,8,128]{2,1,0:T(8,128)S(1)} %bitcast.27), channel_id=1, source_target_pairs={{0,16},{8,24},{16,0},{24,8},{1,17},{9,25},{17,1},{25,9},{2,18},{10... | collective-permute-start | bytes 61448 | tf_op jit(solution)/shard_map/ppermute | solution.py:388
  5.1 1.4 %collective-permute-start = (f32[5,8,128]{2,1,0:T(8,128)S(1)}, f32[5,8,128]{2,1,0:T(8,128)S(1)}, u32[]{:S(2)}, u32[]{:S(2)}) collective-permute-start(f32[5,8,128]{2,1,0:T(8,128)S(1)} %bitcast.28), channel_id=1, source_target_pairs={{0,24},{8,0},{16,8},{24,16},{1,25},{9,1},{17,9},{25,17},{2,26},{10... | collective-permute-start | bytes 61448 | tf_op jit(solution)/shard_map/ppermute | solution.py:388
  6.5 1.8 %copy.26 = f32[2,2,64,32,32]{2,4,3,0,1:T(8,128)S(1)} copy(f32[2,2,64,32,32]{2,4,3,1,0:T(8,128)} %param.20) | data formatting | bytes 2097152 | tf_op args[3]
  8.4 0.2 slice_bitcast_fusion.1
  8.7 0.3 copy-done.17
  9.4 1.8 %table.1 = (bf16[4096,256]{1,0:T(8,128)(2,1)S(1)}, bf16[256,4096]{1,0:T(8,128)(2,1)S(1)}) custom-call(f32[32,128]{1,0:T(8,128)S(1)} %copy-done.16, f32[32,128]{1,0:T(8,128)S(1)} %copy-done.15, f32[128,128]{1,0:T(8,128)S(1)} %copy-done.14, f32[128,128]{1,0:T(8,128)S(1)} %copy-done.13, f32[128,32]{1,0:T(8,128)S(1)} %copy-done.12, f32[128,32]{1,0:T(8,128)S(1)} %copy-done.11, ...), custom_call_target="tpu_custom_call" | custom-call | tf_op jit(solution)/shard_map/table/pallas_call | solution.py:359
  11.2 1.3 %copy-done = bf16[256,4096]{1,0:T(8,128)(2,1)} copy-done((bf16[256,4096]{1,0:T(8,128)(2,1)}, bf16[256,4096]{1,0:T(8,128)(2,1)S(1)}, u32[]{:S(2)}) %copy-start) | copy-done | bytes 2097176
  12.6 1.6 %collective-permute-start.4 = (f32[4,5,8,128]{3,2,1,0:T(8,128)S(1)}, f32[4,5,8,128]{3,2,1,0:T(8,128)S(1)}, u32[]{:S(2)}, u32[]{:S(2)}) collective-permute-start(f32[4,5,8,128]{3,2,1,0:T(8,128)S(1)} %pad_maximum_fusion.1.blocks_ref), channel_id=1, source_target_pairs={{0,2},{1,3},{2,4},{3,5},{4,6},{5,7},{6,0},{7,1},{8,9},{9,10},{10,1... | collective-permute-start | bytes 245768 | tf_op jit(solution)/shard_map/ppermute | solution.py:396
  14.2 2.2 %collective-permute-start.3 = (f32[4,5,8,128]{3,2,1,0:T(8,128)S(1)}, f32[4,5,8,128]{3,2,1,0:T(8,128)S(1)}, u32[]{:S(2)}, u32[]{:S(2)}) collective-permute-start(f32[4,5,8,128]{3,2,1,0:T(8,128)S(1)} %pad_maximum_fusion.1.blocks_ref), channel_id=1, source_target_pairs={{0,6},{1,7},{2,0},{3,1},{4,2},{5,3},{6,4},{7,5},{8,15},{9,8},{10,9... | collective-permute-start | bytes 245768 | tf_op jit(solution)/shard_map/ppermute | solution.py:396
  16.5 0.3 pad_maximum_fusion.weights
  16.8 2.4 %collective-permute-done.4.near_b = f32[4,5,8,128]{3,2,1,0:T(8,128)S(1)} collective-permute-done((f32[4,5,8,128]{3,2,1,0:T(8,128)S(1)}, f32[4,5,8,128]{3,2,1,0:T(8,128)S(1)}, u32[]{:S(2)}, u32[]{:S(2)}) %collective-permute-start.4) | collective-permute-done | bytes 81952 | tf_op jit(solution)/shard_map/ppermute | solution.py:396
  19.2 0.3 collective-permute-done.3.near_a
  19.5 0.2 collective-permute-start.5
  19.7 0.8 %collective-permute-done.6.swap_b = f32[4,5,8,128]{3,2,1,0:T(8,128)S(1)} collective-permute-done((f32[4,5,8,128]{3,2,1,0:T(8,128)S(1)}, f32[4,5,8,128]{3,2,1,0:T(8,128)S(1)}, u32[]{:S(2)}, u32[]{:S(2)}) %collective-permute-start.6) | collective-permute-done | bytes 81952 | tf_op jit(solution)/shard_map/ppermute | solution.py:399
  20.5 0.4 collective-permute-done.5.swap_a
  20.8 8.1 %network.1 = (f32[5,32,128]{2,1,0:T(8,128)S(1)}, f32[4,5,8,128]{3,2,1,0:T(8,128)S(1)}, f32[4,5,8,128]{3,2,1,0:T(8,128)S(1)}, f32[4,5,8,128]{3,2,1,0:T(8,128)S(1)...) custom-call(s32[1]{0:T(128)} %bitcast.core_ref, f32[5,32,128]{2,1,0:T(8,128)S(1)} %bitcast.24, ...), custom_call_target="tpu_custom_call" | custom-call | tf_op jit(solution)/shard_map/network/pallas_call | solution.py:359
  29.0 0.2 collective-permute-start.7
  29.2 0.3 collective-permute-start.8
  29.5 0.8 %collective-permute-done.7.got_a = f32[4,5,8,128]{3,2,1,0:T(8,128)S(1)} collective-permute-done((f32[4,5,8,128]{3,2,1,0:T(8,128)S(1)}, f32[4,5,8,128]{3,2,1,0:T(8,128)S(1)}, u32[]{:S(2)}, u32[]{:S(2)}) %collective-permute-start.7) | collective-permute-done | bytes 81952 | tf_op jit(solution)/shard_map/ppermute | solution.py:399
  30.3 0.2 collective-permute-done.8.got_b
  30.5 3.2 %collective-permute-start.9 = (f32[4,5,8,128]{3,2,1,0:T(8,128)S(1)}, f32[4,5,8,128]{3,2,1,0:T(8,128)S(1)}, u32[]{:S(2)}, u32[]{:S(2)}) collective-permute-start(f32[4,5,8,128]{3,2,1,0:T(8,128)S(1)} %get-tuple-element.27), channel_id=1, source_target_pairs={{0,6},{1,7},{2,0},{3,1},{4,2},{5,3},{6,4},{7,5},{8,15},{9,8},{10,9... | collective-permute-start | bytes 245768 | tf_op jit(solution)/shard_map/ppermute | solution.py:396
  33.7 2.5 %collective-permute-done.9.a_ref = f32[4,5,8,128]{3,2,1,0:T(8,128)S(1)} collective-permute-done((f32[4,5,8,128]{3,2,1,0:T(8,128)S(1)}, f32[4,5,8,128]{3,2,1,0:T(8,128)S(1)}, u32[]{:S(2)}, u32[]{:S(2)}) %collective-permute-start.9) | collective-permute-done | bytes 81952 | tf_op jit(solution)/shard_map/ppermute | solution.py:396
  36.2 3.7 %collective-permute-done.10.b_ref = f32[4,5,8,128]{3,2,1,0:T(8,128)S(1)} collective-permute-done((f32[4,5,8,128]{3,2,1,0:T(8,128)S(1)}, f32[4,5,8,128]{3,2,1,0:T(8,128)S(1)}, u32[]{:S(2)}, u32[]{:S(2)}) %collective-permute-start.10) | collective-permute-done | bytes 81952 | tf_op jit(solution)/shard_map/ppermute | solution.py:396
  40.0 1.7 %collective-permute-start.11 = (f32[5,8,128]{2,1,0:T(8,128)S(1)}, f32[5,8,128]{2,1,0:T(8,128)S(1)}, u32[]{:S(2)}, u32[]{:S(2)}) collective-permute-start(f32[5,8,128]{2,1,0:T(8,128)S(1)} %get-tuple-element.30), channel_id=1, source_target_pairs={{0,8},{8,16},{16,24},{24,0},{1,9},{9,17},{17,25},{25,1},{2,10},{10... | collective-permute-start | bytes 61448 | tf_op jit(solution)/shard_map/ppermute | solution.py:388
  41.7 0.5 %collective-permute-start.12 = (f32[5,8,128]{2,1,0:T(8,128)S(1)}, f32[5,8,128]{2,1,0:T(8,128)S(1)}, u32[]{:S(2)}, u32[]{:S(2)}) collective-permute-start(f32[5,8,128]{2,1,0:T(8,128)S(1)} %get-tuple-element.31), channel_id=1, source_target_pairs={{0,16},{8,24},{16,0},{24,8},{1,17},{9,25},{17,1},{25,9},{2,18},{10... | collective-permute-start | bytes 61448 | tf_op jit(solution)/shard_map/ppermute | solution.py:388
  42.2 0.9 %collective-permute-start.13 = (f32[5,8,128]{2,1,0:T(8,128)S(1)}, f32[5,8,128]{2,1,0:T(8,128)S(1)}, u32[]{:S(2)}, u32[]{:S(2)}) collective-permute-start(f32[5,8,128]{2,1,0:T(8,128)S(1)} %get-tuple-element.32), channel_id=1, source_target_pairs={{0,24},{8,0},{16,8},{24,16},{1,25},{9,1},{17,9},{25,17},{2,26},{10... | collective-permute-start | bytes 61448 | tf_op jit(solution)/shard_map/ppermute | solution.py:388
  43.3 2.2 %collective-permute-done.12.refs_2_ = f32[5,8,128]{2,1,0:T(8,128)S(1)} collective-permute-done((f32[5,8,128]{2,1,0:T(8,128)S(1)}, f32[5,8,128]{2,1,0:T(8,128)S(1)}, u32[]{:S(2)}, u32[]{:S(2)}) %collective-permute-start.12) | collective-permute-done | bytes 20512 | tf_op jit(solution)/shard_map/ppermute | solution.py:388
  45.5 0.9 %final.1 = f32[160,128]{1,0:T(8,128)} custom-call(f32[160,128]{1,0:T(8,128)S(1)} %bitcast.30, f32[256,128]{1,0:T(8,128)S(1)} %copy-done.2, f32[5,8,128]{2,1,0:T(8,128)S(1)} %get-tuple-element.29.refs_0_, f32[5,8,128]{2,1,0:T(8,128)S(1)} %collective-permute-done.11.refs_1_, f32[5,8,128]{2,1,0:T(8,128)S(1)} %collective-permute-done.12.refs_2_, ...), custom_call_target="tpu_custom_call" | custom-call | tf_op jit(solution)/shard_map/final/pallas_call | solution.py:359
  (51 shorter events, 0.7 us)
Async XLA Ops:
  0.0 0.9 %copy-start.1 = (f32[256,128]{1,0:T(8,128)S(1)}, f32[256,128]{1,0:T(8,128)}, u32[]{:S(2)}) copy-start(f32[256,128]{1,0:T(8,128)} %constant.43.clone.pool_ref) | copy-start | bytes 393220
  0.9 0.9 %copy-start.3 = (f32[5,1,32,128]{3,2,1,0:T(8,128)S(1)}, f32[5,1,32,128]{3,2,1,0:T(8,128)}, u32[]{:S(2)}) copy-start(f32[5,1,32,128]{3,2,1,0:T(8,128)} %param.17) | copy-start | bytes 245764
  2.0 10.6 %collective-permute-start.2 = (f32[5,8,128]{2,1,0:T(8,128)S(1)}, f32[5,8,128]{2,1,0:T(8,128)S(1)}, u32[]{:S(2)}, u32[]{:S(2)}) collective-permute-start(f32[5,8,128]{2,1,0:T(8,128)S(1)} %bitcast.26), channel_id=1, source_target_pairs={{0,8},{8,16},{16,24},{24,0},{1,9},{9,17},{17,25},{25,1},{2,10},{10... | collective-permute-start | bytes 61448 | tf_op jit(solution)/shard_map/ppermute | solution.py:388
  2.5 10.0 %collective-permute-start.1 = (f32[5,8,128]{2,1,0:T(8,128)S(1)}, f32[5,8,128]{2,1,0:T(8,128)S(1)}, u32[]{:S(2)}, u32[]{:S(2)}) collective-permute-start(f32[5,8,128]{2,1,0:T(8,128)S(1)} %bitcast.27), channel_id=1, source_target_pairs={{0,16},{8,24},{16,0},{24,8},{1,17},{9,25},{17,1},{25,9},{2,18},{10... | collective-permute-start | bytes 61448 | tf_op jit(solution)/shard_map/ppermute | solution.py:388
  5.1 7.5 %collective-permute-start = (f32[5,8,128]{2,1,0:T(8,128)S(1)}, f32[5,8,128]{2,1,0:T(8,128)S(1)}, u32[]{:S(2)}, u32[]{:S(2)}) collective-permute-start(f32[5,8,128]{2,1,0:T(8,128)S(1)} %bitcast.28), channel_id=1, source_target_pairs={{0,24},{8,0},{16,8},{24,16},{1,25},{9,1},{17,9},{25,17},{2,26},{10... | collective-permute-start | bytes 61448 | tf_op jit(solution)/shard_map/ppermute | solution.py:388
  8.3 0.9 %copy-start.18 = (f32[32,5]{0,1:T(8,128)S(1)}, f32[32,5]{0,1:T(8,128)}, u32[]{:S(2)}) copy-start(f32[32,5]{0,1:T(8,128)} %param.22) | copy-start | bytes 1924
  8.3 1.0 %copy-start.7 = (f32[2,32,32]{2,1,0:T(8,128)S(1)}, f32[2,32,32]{2,1,0:T(8,128)}, u32[]{:S(2)}) copy-start(f32[2,32,32]{2,1,0:T(8,128)} %pointwise_ref.1) | copy-start | bytes 24580
  8.3 1.0 %copy-start.9 = (f32[128,128]{1,0:T(8,128)S(1)}, f32[128,128]{1,0:T(8,128)}, u32[]{:S(2)}) copy-start(f32[128,128]{1,0:T(8,128)} %constant.51.clone.b2t_ref) | copy-start | bytes 196612
  8.3 1.0 %copy-start.10 = (f32[128,128]{1,0:T(8,128)S(1)}, f32[128,128]{1,0:T(8,128)}, u32[]{:S(2)}) copy-start(f32[128,128]{1,0:T(8,128)} %constant.50.clone.b1t_ref) | copy-start | bytes 196612
  8.4 1.0 %copy-start.11 = (f32[128,32]{1,0:T(8,128)S(1)}, f32[128,32]{1,0:T(8,128)}, u32[]{:S(2)}) copy-start(f32[128,32]{1,0:T(8,128)} %constant.49.clone.yt_ref) | copy-start | bytes 49156
  8.4 1.0 %copy-start.12 = (f32[128,32]{1,0:T(8,128)S(1)}, f32[128,32]{1,0:T(8,128)}, u32[]{:S(2)}) copy-start(f32[128,32]{1,0:T(8,128)} %constant.48.clone.xt_ref) | copy-start | bytes 49156
  8.4 1.0 %copy-start.13 = (f32[128,128]{1,0:T(8,128)S(1)}, f32[128,128]{1,0:T(8,128)}, u32[]{:S(2)}) copy-start(f32[128,128]{1,0:T(8,128)} %constant.47.clone.b2_ref) | copy-start | bytes 196612
  8.4 1.0 %copy-start.14 = (f32[128,128]{1,0:T(8,128)S(1)}, f32[128,128]{1,0:T(8,128)}, u32[]{:S(2)}) copy-start(f32[128,128]{1,0:T(8,128)} %constant.46.clone.b1_ref) | copy-start | bytes 196612
  8.4 1.0 %copy-start.15 = (f32[32,128]{1,0:T(8,128)S(1)}, f32[32,128]{1,0:T(8,128)}, u32[]{:S(2)}) copy-start(f32[32,128]{1,0:T(8,128)} %constant.45.clone.y_ref) | copy-start | bytes 49156
  8.4 1.0 %copy-start.16 = (f32[32,128]{1,0:T(8,128)S(1)}, f32[32,128]{1,0:T(8,128)}, u32[]{:S(2)}) copy-start(f32[32,128]{1,0:T(8,128)} %constant.44.clone.x_ref) | copy-start | bytes 49156
  8.6 12.2 %copy-start.4 = (f32[5,1,32,128]{3,2,1,0:T(8,128)S(1)}, f32[5,1,32,128]{3,2,1,0:T(8,128)}, u32[]{:S(2)}) copy-start(f32[5,1,32,128]{3,2,1,0:T(8,128)} %param.17) | copy-start | bytes 245764
  8.6 12.2 %copy-start.5 = (bf16[128,640]{1,0:T(8,128)(2,1)S(1)}, bf16[128,640]{1,0:T(8,128)(2,1)}, u32[]{:S(2)}) copy-start(bf16[128,640]{1,0:T(8,128)(2,1)} %constant.53.clone.quarter_t_ref) | copy-start | bytes 491524
  8.6 12.2 %copy-start.6 = (bf16[640,128]{1,0:T(8,128)(2,1)S(1)}, bf16[640,128]{1,0:T(8,128)(2,1)}, u32[]{:S(2)}) copy-start(bf16[640,128]{1,0:T(8,128)(2,1)} %constant.52.clone.quarter_ref) | copy-start | bytes 491524
  8.6 12.2 %copy-start.8 = (f32[5,1,32,128]{3,2,1,0:T(8,128)S(1)}, f32[5,1,32,128]{3,2,1,0:T(8,128)}, u32[]{:S(2)}) copy-start(f32[5,1,32,128]{3,2,1,0:T(8,128)} %param.18) | copy-start | bytes 245764
  11.2 1.4 %copy-start = (bf16[256,4096]{1,0:T(8,128)(2,1)}, bf16[256,4096]{1,0:T(8,128)(2,1)S(1)}, u32[]{:S(2)}) copy-start(bf16[256,4096]{1,0:T(8,128)(2,1)S(1)} %get-tuple-element.20.flipped_ref) | copy-start | bytes 6291460
  12.6 6.6 %collective-permute-start.4 = (f32[4,5,8,128]{3,2,1,0:T(8,128)S(1)}, f32[4,5,8,128]{3,2,1,0:T(8,128)S(1)}, u32[]{:S(2)}, u32[]{:S(2)}) collective-permute-start(f32[4,5,8,128]{3,2,1,0:T(8,128)S(1)} %pad_maximum_fusion.1.blocks_ref), channel_id=1, source_target_pairs={{0,2},{1,3},{2,4},{3,5},{4,6},{5,7},{6,0},{7,1},{8,9},{9,10},{10,1... | collective-permute-start | bytes 245768 | tf_op jit(solution)/shard_map/ppermute | solution.py:396
  14.2 5.3 %collective-permute-start.3 = (f32[4,5,8,128]{3,2,1,0:T(8,128)S(1)}, f32[4,5,8,128]{3,2,1,0:T(8,128)S(1)}, u32[]{:S(2)}, u32[]{:S(2)}) collective-permute-start(f32[4,5,8,128]{3,2,1,0:T(8,128)S(1)} %pad_maximum_fusion.1.blocks_ref), channel_id=1, source_target_pairs={{0,6},{1,7},{2,0},{3,1},{4,2},{5,3},{6,4},{7,5},{8,15},{9,8},{10,9... | collective-permute-start | bytes 245768 | tf_op jit(solution)/shard_map/ppermute | solution.py:396
  19.2 1.3 %collective-permute-start.6 = (f32[4,5,8,128]{3,2,1,0:T(8,128)S(1)}, f32[4,5,8,128]{3,2,1,0:T(8,128)S(1)}, u32[]{:S(2)}, u32[]{:S(2)}) collective-permute-start(f32[4,5,8,128]{3,2,1,0:T(8,128)S(1)} %collective-permute-done.4.near_b), channel_id=1, source_target_pairs={{0,8},{8,0},{16,24},{24,16},{1,9},{9,1},{17,25},{25,17},{2,10},{10... | collective-permute-start | bytes 245768 | tf_op jit(solution)/shard_map/ppermute | solution.py:399
  19.5 1.3 %collective-permute-start.5 = (f32[4,5,8,128]{3,2,1,0:T(8,128)S(1)}, f32[4,5,8,128]{3,2,1,0:T(8,128)S(1)}, u32[]{:S(2)}, u32[]{:S(2)}) collective-permute-start(f32[4,5,8,128]{3,2,1,0:T(8,128)S(1)} %collective-permute-done.3.near_a), channel_id=1, source_target_pairs={{0,8},{8,0},{16,24},{24,16},{1,9},{9,1},{17,25},{25,17},{2,10},{10... | collective-permute-start | bytes 245768 | tf_op jit(solution)/shard_map/ppermute | solution.py:399
  20.8 24.6 %copy-start.2 = (f32[256,128]{1,0:T(8,128)S(1)}, f32[256,128]{1,0:T(8,128)}, u32[]{:S(2)}) copy-start(f32[256,128]{1,0:T(8,128)} %constant.43.clone.pool_ref) | copy-start | bytes 393220
  29.0 1.3 %collective-permute-start.7 = (f32[4,5,8,128]{3,2,1,0:T(8,128)S(1)}, f32[4,5,8,128]{3,2,1,0:T(8,128)S(1)}, u32[]{:S(2)}, u32[]{:S(2)}) collective-permute-start(f32[4,5,8,128]{3,2,1,0:T(8,128)S(1)} %get-tuple-element.25), channel_id=1, source_target_pairs={{0,8},{8,0},{16,24},{24,16},{1,9},{9,1},{17,25},{25,17},{2,10},{10... | collective-permute-start | bytes 245768 | tf_op jit(solution)/shard_map/ppermute | solution.py:399
  29.2 1.3 %collective-permute-start.8 = (f32[4,5,8,128]{3,2,1,0:T(8,128)S(1)}, f32[4,5,8,128]{3,2,1,0:T(8,128)S(1)}, u32[]{:S(2)}, u32[]{:S(2)}) collective-permute-start(f32[4,5,8,128]{3,2,1,0:T(8,128)S(1)} %get-tuple-element.26), channel_id=1, source_target_pairs={{0,8},{8,0},{16,24},{24,16},{1,9},{9,1},{17,25},{25,17},{2,10},{10... | collective-permute-start | bytes 245768 | tf_op jit(solution)/shard_map/ppermute | solution.py:399
  30.5 5.7 %collective-permute-start.9 = (f32[4,5,8,128]{3,2,1,0:T(8,128)S(1)}, f32[4,5,8,128]{3,2,1,0:T(8,128)S(1)}, u32[]{:S(2)}, u32[]{:S(2)}) collective-permute-start(f32[4,5,8,128]{3,2,1,0:T(8,128)S(1)} %get-tuple-element.27), channel_id=1, source_target_pairs={{0,6},{1,7},{2,0},{3,1},{4,2},{5,3},{6,4},{7,5},{8,15},{9,8},{10,9... | collective-permute-start | bytes 245768 | tf_op jit(solution)/shard_map/ppermute | solution.py:396
  33.7 6.2 %collective-permute-start.10 = (f32[4,5,8,128]{3,2,1,0:T(8,128)S(1)}, f32[4,5,8,128]{3,2,1,0:T(8,128)S(1)}, u32[]{:S(2)}, u32[]{:S(2)}) collective-permute-start(f32[4,5,8,128]{3,2,1,0:T(8,128)S(1)} %get-tuple-element.28), channel_id=1, source_target_pairs={{0,2},{1,3},{2,4},{3,5},{4,6},{5,7},{6,0},{7,1},{8,9},{9,10},{10,1... | collective-permute-start | bytes 245768 | tf_op jit(solution)/shard_map/ppermute | solution.py:396
  40.0 3.3 %collective-permute-start.11 = (f32[5,8,128]{2,1,0:T(8,128)S(1)}, f32[5,8,128]{2,1,0:T(8,128)S(1)}, u32[]{:S(2)}, u32[]{:S(2)}) collective-permute-start(f32[5,8,128]{2,1,0:T(8,128)S(1)} %get-tuple-element.30), channel_id=1, source_target_pairs={{0,8},{8,16},{16,24},{24,0},{1,9},{9,17},{17,25},{25,1},{2,10},{10... | collective-permute-start | bytes 61448 | tf_op jit(solution)/shard_map/ppermute | solution.py:388
  41.7 3.8 %collective-permute-start.12 = (f32[5,8,128]{2,1,0:T(8,128)S(1)}, f32[5,8,128]{2,1,0:T(8,128)S(1)}, u32[]{:S(2)}, u32[]{:S(2)}) collective-permute-start(f32[5,8,128]{2,1,0:T(8,128)S(1)} %get-tuple-element.31), channel_id=1, source_target_pairs={{0,16},{8,24},{16,0},{24,8},{1,17},{9,25},{17,1},{25,9},{2,18},{10... | collective-permute-start | bytes 61448 | tf_op jit(solution)/shard_map/ppermute | solution.py:388
  42.2 3.3 %collective-permute-start.13 = (f32[5,8,128]{2,1,0:T(8,128)S(1)}, f32[5,8,128]{2,1,0:T(8,128)S(1)}, u32[]{:S(2)}, u32[]{:S(2)}) collective-permute-start(f32[5,8,128]{2,1,0:T(8,128)S(1)} %get-tuple-element.32), channel_id=1, source_target_pairs={{0,24},{8,0},{16,8},{24,16},{1,25},{9,1},{17,9},{25,17},{2,26},{10... | collective-permute-start | bytes 61448 | tf_op jit(solution)/shard_map/ppermute | solution.py:388
  (1 other events, 0.7 us)
where the time goes:
time: 46.6 us; the launch traced here: 46.3 us
  starting transfers between devices  15.4 us (33%)
  waiting for transfers between devices  13.4 us (29%)
  Pallas kernels  11 us (24%)
  local copies, waits for them, and re-layouts  5.89 us (13%)
    pallas_call x6, Pallas kernels, call(): pl.pallas_call(kernel, out_shape=outs, in_specs=[SCALAR] * scalars + in_v...  11 us
    ppermute x4, waiting for transfers between devices, along_y(): return lax.ppermute(value, ('gx', 'gy'), pairs)  8.96 us
    ppermute x6, starting transfers between devices, along_x(): return lax.ppermute(value, 'gx', [(s, (s + steps) % gx) for s in range(gx)])  7.62 us
    ppermute x4, starting transfers between devices, along_y(): return lax.ppermute(value, ('gx', 'gy'), pairs)  7.09 us
    unnamed x43, local copies, waits for them, and re-layouts  5.7 us
    ppermute x6, waiting for transfers between devices, along_x(): return lax.ppermute(value, 'gx', [(s, (s + steps) % gx) for s in range(gx)])  2.36 us
    ppermute x4, waiting for transfers between devices, swap(): return lax.ppermute(value, 'gx', [(s, s ^ 1) for s in range(gx)])  2.04 us
  transfers between devices with their start and end apart: 14, of which 10 were waited for; matrix products, arithmetic and copies ran while one was open for 6% of the time, Pallas kernels for 4%

commit v1 on v0

--- a/solution.py
+++ b/solution.py
@@ -55,15 +55,6 @@
 def halves(value):
     rows = value.shape[0] // 2
     return value[:rows] + value[rows:]
-
-
-def row_pool_matrix(cols):
-    half = cols // 2
-    out = np.zeros((2 * cols, cols), np.float32)
-    for j in range(cols):
-        out[j, j // 2] = 0.25
-        out[cols + j, half + j // 2] = 0.25
-    return out
 
 
 def quarter_matrix(cols):
@@ -77,41 +68,202 @@
     return out
 
 
-def angle_tables(rows, cols):
+def wave_matrix(rows, cols):
     m = np.arange(MODES * MODES)
     wave_x, wave_y = m // MODES - MODES // 2, m % MODES
-    a = 2.0 * np.pi * ((np.arange(rows)[:, None] * wave_x[None]) % rows) / rows
     b = 2.0 * np.pi * ((np.arange(cols)[:, None] * wave_y[None]) % cols) / cols
     scale = 1.0 / np.sqrt(rows * cols)
-    x = np.concatenate([np.cos(a), -np.sin(a)], 1)
-    y = np.concatenate([-np.sin(a), -np.cos(a)], 1)
-    b1 = np.concatenate([np.cos(b), np.cos(b)], 1) * scale
-    b2 = np.concatenate([np.sin(b), np.sin(b)], 1) * scale
-    return [v.astype(np.float32) for v in (x, y, b1, b2)]
-
-
-def table_kernel(x_ref, y_ref, b1_ref, b2_ref, xt_ref, yt_ref, b1t_ref, b2t_ref, table_ref, flipped_ref):
-    rows = x_ref.shape[0]
-    cols, modes = b1_ref.shape
-    for i in range(rows):
-        piece = x_ref[i : i + 1, :] * b1_ref[...] + y_ref[i : i + 1, :] * b2_ref[...]
-        high, low = split(piece)
-        table_ref[i * cols : (i + 1) * cols, :modes] = high
-        table_ref[i * cols : (i + 1) * cols, modes:] = low
-        piece = xt_ref[:, i : i + 1] * b1t_ref[...] + yt_ref[:, i : i + 1] * b2t_ref[...]
-        high, low = split(piece)
-        flipped_ref[:modes, i * cols : (i + 1) * cols] = high
-        flipped_ref[modes:, i * cols : (i + 1) * cols] = low
-
-
-def pool_kernel(field_ref, pool_ref, out_ref):
+    cos, sin = np.cos(b) * scale, np.sin(b) * scale
+    parts = []
+    for k in range(MODES // 2 + 1):
+        held = (np.abs(wave_x) == k)[None]
+        parts.append(np.concatenate([cos * held, -sin * held], 1))
+    for k in range(1, MODES // 2 + 1):
+        held = (np.sign(wave_x) * (np.abs(wave_x) == k))[None]
+        parts.append(np.concatenate([-sin * held, -cos * held], 1))
+    return np.concatenate(parts, 0).astype(np.float32)
+
+
+def wave_pair(matrix, axis):
+    high = matrix.astype(BF16)
+    low = (matrix - high.astype(np.float32)).astype(BF16)
+    return jnp.asarray(np.concatenate([high, low], axis))
+
+
+def weighted(terms):
+    groups = {}
+    for factor, value in terms:
+        size = round(abs(factor), 12)
+        if size == 0:
+            continue
+        groups.setdefault(size, []).append((factor > 0, value, abs(factor)))
+    total = None
+    for size, members in groups.items():
+        members.sort(key=lambda member: not member[0])
+        part = members[0][1] if members[0][0] else -members[0][1]
+        for positive, value, _ in members[1:]:
+            part = part + value if positive else part - value
+        if size != 1:
+            part = part * members[0][2]
+        total = part if total is None else total + part
+    return total
+
+
+def wave_forward(values):
+    n = len(values)
+    top = MODES // 2
+    angle = lambda k, i: 2.0 * np.pi * ((k * i) % n) / n
+    plus = [values[0]] + [values[i] + values[n - i] for i in range(1, n // 2)] + [values[n // 2]]
+    minus = [None] + [values[i] - values[n - i] for i in range(1, n // 2)]
+    even = [plus[i] + plus[n // 2 - i] for i in range(n // 4)] + [plus[n // 4]]
+    odd = [plus[i] - plus[n // 2 - i] for i in range(n // 4)]
+    minus_odd = [None] + [minus[i] + minus[n // 2 - i] for i in range(1, n // 4)] + [minus[n // 4]]
+    minus_even = [None] + [minus[i] - minus[n // 2 - i] for i in range(1, n // 4)]
+    deep = {
+        1: [even[i] + even[n // 4 - i] for i in range(n // 8)],
+        -1: [even[i] - even[n // 4 - i] for i in range(n // 8)],
+    }
+    deep_minus = {
+        1: [None] + [minus_even[i] - minus_even[n // 4 - i] for i in range(1, n // 8)],
+        -1: [None] + [minus_even[i] + minus_even[n // 4 - i] for i in range(1, n // 8)],
+    }
+    out = []
+    for k in range(top + 1):
+        if k % 2:
+            out.append(weighted([(np.cos(angle(k, i)), odd[i]) for i in range(n // 4)]))
+        else:
+            sign = 1 if k % 4 == 0 else -1
+            terms = [(np.cos(angle(k, i)), deep[sign][i]) for i in range(n // 8)]
+            out.append(weighted(terms + [(np.cos(angle(k, n // 8)), even[n // 8])]))
+    for k in range(1, top + 1):
+        if k % 2:
+            out.append(weighted([(np.sin(angle(k, i)), minus_odd[i]) for i in range(1, n // 4 + 1)]))
+        else:
+            sign = 1 if k % 4 == 0 else -1
+            terms = [(np.sin(angle(k, i)), deep_minus[sign][i]) for i in range(1, n // 8)]
+            out.append(weighted(terms + [(np.sin(angle(k, n // 8)), minus_even[n // 8])]))
+    return out
+
+
+def added(a, b):
+    return b if a is None else a if b is None else a + b
+
+
+def taken(a, b):
+    return a if b is None else -b if a is None else a - b
+
+
+def wave_backward(parts, n):
+    top = MODES // 2
+    angle = lambda k, i: 2.0 * np.pi * ((k * i) % n) / n
+    cosine = lambda i, ks: weighted([(np.cos(angle(k, i)), parts[k]) for k in ks])
+    sine = lambda i, ks: weighted([(np.sin(angle(k, i)), parts[top + k]) for k in ks])
+    fours = [k for k in range(top + 1) if k % 4 == 0]
+    twos = [k for k in range(top + 1) if k % 4 == 2]
+    odds = [k for k in range(top + 1) if k % 2]
+    even = [None] * (n // 4 + 1)
+    for i in range(n // 8):
+        a, b = cosine(i, fours), cosine(i, twos)
+        even[i], even[n // 4 - i] = added(a, b), taken(a, b)
+    even[n // 8] = cosine(n // 8, sorted(fours + twos))
+    plus = [None] * (n // 2 + 1)
+    for i in range(n // 4):
+        b = cosine(i, odds)
+        plus[i], plus[n // 2 - i] = added(even[i], b), taken(even[i], b)
+    plus[n // 4] = even[n // 4]
+    minus_even = [None] * (n // 4)
+    for i in range(1, n // 8):
+        a, b = sine(i, [k for k in fours if k]), sine(i, twos)
+        minus_even[i], minus_even[n // 4 - i] = added(b, a), taken(b, a)
+    minus_even[n // 8] = sine(n // 8, sorted(k for k in fours + twos if k))
+    minus = [None] * (n // 2)
+    for i in range(1, n // 4):
+        a = sine(i, odds)
+        minus[i], minus[n // 2 - i] = added(a, minus_even[i]), taken(a, minus_even[i])
+    minus[n // 4] = sine(n // 4, odds)
+    out = [None] * n
+    out[0], out[n // 2] = plus[0], plus[n // 2]
+    for i in range(1, n // 2):
+        out[i], out[n - i] = added(plus[i], minus[i]), taken(plus[i], minus[i])
+    return out
+
+
+def prepare_kernel(
+    cotangent_hbm, lift_hbm, spectral_hbm, pointwise_hbm, project_hbm, *refs
+):
+    constants_hbm, refs = refs[:3], refs[3:]
+    constants, refs = refs[:3], refs[3:]
+    by_input, by_output_hbm, lift_ref, lift_t_ref, local_one, local_two, back_two, back_one, target_grad = refs[:9]
+    spectral_ref, by_output, target_ref, lift_in, pointwise_ref, project_ref, sems = refs[9:]
+    layers, _, width, _, modes = spectral_ref.shape
+    small, cols = project_ref.shape[0], target_ref.shape[1]
+    rows = target_ref.shape[0] // small
+    channels, features = project_hbm.shape[0], lift_hbm.shape[0]
+    pairs = [
+        (cotangent_hbm, target_ref.at[: channels * rows]),
+        (project_hbm, project_ref.at[:channels]),
+        (lift_hbm, lift_in.at[:features]),
+        (pointwise_hbm, pointwise_ref),
+    ]
+    pairs += [(spectral_hbm.at[layer], spectral_ref.at[layer]) for layer in range(layers)]
+    pairs += list(zip(constants_hbm, constants))
+    copies = [pltpu.make_async_copy(source, target, sems.at[k]) for k, (source, target) in enumerate(pairs)]
+    for copy in copies:
+        copy.start()
+    target_ref[channels * rows :, :] = jnp.zeros(((small - channels) * rows, cols), F32)
+    project_ref[channels:, :] = jnp.zeros((small - channels, width), F32)
+    lift_in[features:, :] = jnp.zeros((lift_in.shape[0] - features, width), F32)
+    for copy in copies[:4]:
+        copy.wait()
+
+    lift = lift_in[...]
+    lift_t = jnp.transpose(lift)
+    lift_ref[...] = lift
+    lift_t_ref[...] = lift_t
+    back_one[...] = tripled(exact_dot(lift, pointwise_ref[0]))
+    local_one[...] = tripled(exact_dot(jnp.transpose(pointwise_ref[0]), lift_t))
+    local_two[...] = tripled(jnp.transpose(pointwise_ref[1]))
+    back_two[...] = tripled(pointwise_ref[1])
+    out = tripled(jnp.transpose(project_ref[...]))
+    group = 4
+    for first in range(0, rows, group):
+        pieces = []
+        for i in range(first, first + group):
+            value = target_ref[pl.ds(i, small, stride=rows), :]
+            high = value.astype(BF16).astype(F32)
+            pieces.append(jnp.concatenate([high, value - high, high], axis=0).astype(BF16))
+        target_grad[:, first * cols : (first + group) * cols] = dot(out, jnp.concatenate(pieces, axis=1))
+
+    for layer in range(layers):
+        copies[4 + layer].wait()
+        for w in range(width):
+            both = [spectral_ref[layer, part, w] for part in range(2)]
+            by_input[layer, w] = jnp.concatenate(both, axis=1)
+        for o in range(width):
+            for first in range(0, width, 8):
+                both = [spectral_ref[layer, part, first : first + 8, o, :] for part in range(2)]
+                by_output[layer, o, first : first + 8, :] = jnp.concatenate(both, axis=1)
+        copies.append(pltpu.make_async_copy(by_output.at[layer], by_output_hbm.at[layer], sems.at[len(copies)]))
+        copies[-1].start()
+    for copy in copies[4 + layers :]:
+        copy.wait()
+
+
+def pool_matrix(cols):
+    half = cols // 2
+    row = lax.broadcasted_iota(jnp.int32, (2 * cols, cols), 0)
+    col = lax.broadcasted_iota(jnp.int32, (2 * cols, cols), 1)
+    return jnp.where(row // 2 == col, 0.25, 0.0).astype(F32)
+
+
+def pool_kernel(field_ref, out_ref):
     count = field_ref.shape[0] // 4
     rows = [field_ref[pl.ds(k, count, stride=4), :] for k in range(4)]
     pairs = jnp.concatenate([rows[0] + rows[1], rows[2] + rows[3]], axis=1)
-    out_ref[...] = exact_dot(pairs, pool_ref[...])
-
-
-def mix(weights, layer, coefficients, swap_ref):
+    out_ref[...] = exact_dot(pairs, pool_matrix(field_ref.shape[1]))
+
+
+def mix(weights, layer, coefficients):
     width, lanes = coefficients.shape
     half = lanes // 2
     lane = lax.broadcasted_iota(jnp.int32, (width, lanes), 1)
@@ -128,43 +280,70 @@
     return jnp.where(lane < half, total_real, total_imag)
 
 
-def unmix(weights, layer, grads, swap_ref):
+def unmix(weights, layer, grads):
     width, lanes = grads.shape
     half = lanes // 2
     lane = lax.broadcasted_iota(jnp.int32, (width, lanes), 1)
     turned = pltpu.roll(grads, half, 1)
     turned = jnp.where(lane < half, turned, -turned)
-    for w in range(width):
-        block = weights[layer, w]
-        swap_ref[0, w : w + 1, :] = jnp.sum(block * grads, axis=0, keepdims=True)
-        swap_ref[1, w : w + 1, :] = jnp.sum(block * turned, axis=0, keepdims=True)
-    real, imag = swap_ref[0], swap_ref[1]
-    real += pltpu.roll(real, half, 1)
-    imag += pltpu.roll(imag, half, 1)
-    return jnp.where(lane < half, real, imag)
-
-
-def contract(pair_ref, table_ref):
-    both = dot(pair_ref[...], table_ref[...])
+    total_real = jnp.zeros((width, lanes), F32)
+    total_imag = jnp.zeros((width, lanes), F32)
+    for o in range(width):
+        block = weights[layer, o]
+        total_real += block * grads[o : o + 1]
+        total_imag += block * turned[o : o + 1]
+    total_real += pltpu.roll(total_real, half, 1)
+    total_imag += pltpu.roll(total_imag, half, 1)
+    return jnp.where(lane < half, total_real, total_imag)
+
+
+def contract(parts, wave):
+    high, low = split(parts)
+    both = dot(jnp.concatenate([high, low], axis=0), wave)
     rows, modes = both.shape[0] // 2, both.shape[1] // 2
     return both[:rows, :modes] + both[:rows, modes:] + both[rows:, :modes]
 
 
+def tripled(value):
+    high, low = split(value)
+    return jnp.concatenate([high, high, low], axis=1)
+
+
+def local_product(out_ref, left, pair_ref, steps):
+    rows = pair_ref.shape[0] // 2
+    for at in steps:
+        right = jnp.concatenate([pair_ref[:, at], pair_ref[:rows, at]], axis=0)
+        out_ref[:, at] = dot(left, right)
+
+
+def store_pair(pair_ref, first, rows_total, at, value):
+    high, low = split(value)
+    count = value.shape[0]
+    pair_ref[first : first + count, at] = high
+    pair_ref[rows_total + first : rows_total + first + count, at] = low
+
+
 def network_kernel(
     ring, chunk,
-    core_ref, field_ref, blocks_ref, near_a, near_b, swap_a, swap_b, cotangent_ref, lift_ref, lift_t_ref, weights,
-    pointwise_ref, pointwise_t_ref, project_ref, quarter_ref, quarter_t_ref, table_ref, flipped_ref,
+    core_ref, field_ref, blocks_ref, near_a, near_b, swap_a, swap_b, quarter_t_hbm, by_output_hbm,
+    quarter_ref, wave_ref, wave_t_ref, by_input, lift_ref, lift_t_ref, local_one, local_two, back_two, back_one, target_grad,
     own_ref, center_ref, keep_a, keep_b, give_a, give_b,
-    x_ref, window_ref, feature_pair, hidden_pair, grad_pair, target_pair, slope_one, swap_ref, target_ref, grad_x_ref,
+    x_ref, window_ref, feature_pair, hidden_pair, slope_one, local_ref, grad_x_ref, parts_ref,
+    quarter_t_ref, by_output, sems,
 ):
     channels, rows, cols = field_ref.shape
     tall = rows // 4
     half, quarter = cols // 2, cols // 4
     cells = rows * cols
-    width = pointwise_ref.shape[1]
+    width = slope_one.shape[0]
     padded = x_ref.shape[0] // rows
     odd = core_ref[0] == 1
     lane = lax.broadcasted_iota(jnp.int32, (1, 1, cols), 2)
+
+    late = [(by_output_hbm, by_output), (quarter_t_hbm, quarter_t_ref)]
+    late = [pltpu.make_async_copy(source, target, sems.at[k]) for k, (source, target) in enumerate(late)]
+    for copy in late:
+        copy.start()
 
     for d in range(-2, 3):
         for e in range(-2, 3):
@@ -209,59 +388,76 @@
     for c in range(3 * channels, padded):
         x_ref[c * rows : (c + 1) * rows, :] = jnp.zeros((rows, cols), F32)
 
-    target_ref[channels * rows :, :] = jnp.zeros((target_ref.shape[0] - channels * rows, cols), F32)
-    for c in range(channels):
-        target_ref[c * rows : (c + 1) * rows, :] = cotangent_ref[c]
-    small = target_ref.shape[0] // rows
     for i in range(rows):
         at = slice(i * cols, (i + 1) * cols)
         high, low = split(x_ref[pl.ds(i, padded, stride=rows), :])
         feature_pair[:padded, at] = high
         feature_pair[padded:, at] = low
-        value = target_ref[pl.ds(i, small, stride=rows), :]
-        high = value.astype(BF16).astype(F32)
-        target_pair[:, at] = jnp.concatenate([high, value - high], axis=0).astype(BF16)
 
     lift = lift_ref[...]
     lift_t = lift_t_ref[...]
     steps = [slice(k, k + chunk) for k in range(0, cells, chunk)]
-
-    mixed = mix(weights, 0, exact_dot(lift_t, contract(feature_pair, table_ref)), swap_ref)
-    wave = stacked(mixed)
-    local = stacked(exact_dot(pointwise_t_ref[0], lift_t))
-    for at in steps:
-        u = halves(dot(wave, flipped_ref[:, at]) + dot(local, feature_pair[:, at]))
-        cdf = 0.5 + 0.5 * lax.erf(u * SQRT_HALF)
-        slope_one[:, at] = cdf + u * (INV_SQRT_2PI * jnp.exp(-0.5 * u * u))
-        high, low = split(u * cdf)
-        hidden_pair[:width, at] = high
-        hidden_pair[width:, at] = low
-
-    mixed = mix(weights, 1, contract(hidden_pair, table_ref), swap_ref)
-    wave = stacked(mixed)
-    local = stacked(pointwise_t_ref[1])
-    out = stacked(project_ref[...])
-    for at in steps:
-        u = halves(dot(wave, flipped_ref[:, at]) + dot(local, hidden_pair[:, at]))
-        cdf = 0.5 + 0.5 * lax.erf(u * SQRT_HALF)
-        slope = cdf + u * (INV_SQRT_2PI * jnp.exp(-0.5 * u * u))
-        high, low = split(slope * halves(dot(out, target_pair[:, at])))
-        grad_pair[:width, at] = high
-        grad_pair[width:, at] = low
-    wave = stacked(unmix(weights, 1, contract(grad_pair, table_ref), swap_ref))
-    local = stacked(pointwise_ref[1])
-    for at in steps:
-        g = halves(dot(wave, flipped_ref[:, at]) + dot(local, grad_pair[:, at]))
-        high, low = split(g * slope_one[:, at])
-        hidden_pair[:width, at] = high
-        hidden_pair[width:, at] = low
-
-    wave = stacked(exact_dot(lift, unmix(weights, 0, contract(hidden_pair, table_ref), swap_ref)))
-    local = stacked(exact_dot(lift, pointwise_ref[0]))
-    for k, at in enumerate(steps):
-        g = halves(dot(wave, flipped_ref[:, at]) + dot(local, hidden_pair[:, at]))
-        for n in range(chunk // cols):
-            grad_x_ref[pl.ds(k * (chunk // cols) + n, padded, stride=rows), :] = g[:, n * cols : (n + 1) * cols]
+    columns = [slice(i * cols, (i + 1) * cols) for i in range(rows)]
+    part_count = parts_ref.shape[1] // cols
+    part_columns = [slice(i * cols, (i + 1) * cols) for i in range(part_count)]
+
+    def store_parts(band, values):
+        for at, value in zip(part_columns, wave_forward(values)):
+            parts_ref[band, at] = value
+
+    def expanded(modes, band_rows):
+        parts_ref[:band_rows, :] = halves(dot(stacked(modes), wave_t_ref[...]))
+
+    def unfolded(band):
+        return wave_backward([parts_ref[band, at] for at in part_columns], rows)
+
+    bands = [slice(k, k + 8) for k in range(0, width, 8)]
+
+    for k in range(0, padded, 8):
+        store_parts(slice(k, k + 8), [x_ref[pl.ds(k * rows + i, 8, stride=rows), :] for i in range(rows)])
+    local_product(local_ref, local_one[...], feature_pair, steps)
+    modes = contract(parts_ref[:padded, :], wave_ref[...])
+    expanded(mix(by_input, 0, exact_dot(lift_t, modes)), width)
+    for band in bands:
+        hidden = []
+        for at, value in zip(columns, unfolded(band)):
+            u = value + local_ref[band, at]
+            cdf = 0.5 + 0.5 * lax.erf(u * SQRT_HALF)
+            slope_one[band, at] = cdf + u * (INV_SQRT_2PI * jnp.exp(-0.5 * u * u))
+            hidden.append(u * cdf)
+            store_pair(hidden_pair, band.start, width, at, hidden[-1])
+        store_parts(band, hidden)
+
+    local_product(local_ref, local_two[...], hidden_pair, steps)
+    modes = contract(parts_ref[...], wave_ref[...])
+    expanded(mix(by_input, 1, modes), width)
+    for band in bands:
+        grads = []
+        for at, value in zip(columns, unfolded(band)):
+            u = value + local_ref[band, at]
+            cdf = 0.5 + 0.5 * lax.erf(u * SQRT_HALF)
+            slope = cdf + u * (INV_SQRT_2PI * jnp.exp(-0.5 * u * u))
+            grads.append(slope * target_grad[band, at])
+            store_pair(hidden_pair, band.start, width, at, grads[-1])
+        store_parts(band, grads)
+    local_product(local_ref, back_two[...], hidden_pair, steps)
+    modes = contract(parts_ref[...], wave_ref[...])
+    late[0].wait()
+    expanded(unmix(by_output, 1, modes), width)
+    for band in bands:
+        grads = []
+        for at, value in zip(columns, unfolded(band)):
+            grads.append((value + local_ref[band, at]) * slope_one[band, at])
+            store_pair(hidden_pair, band.start, width, at, grads[-1])
+        store_parts(band, grads)
+
+    local_product(local_ref.at[:padded], back_one[...], hidden_pair, steps)
+    modes = contract(parts_ref[...], wave_ref[...])
+    expanded(exact_dot(lift, unmix(by_output, 0, modes)), padded)
+    for k in range(0, padded, 8):
+        band = slice(k, k + 8)
+        for i, (at, value) in enumerate(zip(columns, unfolded(band))):
+            grad_x_ref[pl.ds(k * rows + i, 8, stride=rows), :] = value + local_ref[band, at]
 
     for c in range(channels):
         own_ref[c] = grad_x_ref[c * rows : (c + 1) * rows, :]
@@ -285,6 +481,7 @@
         0: four(even_down, even_down, odd_up, odd_up),
         1: four(even_up, zero, odd_down, zero),
     }
+    late[1].wait()
     high, low = split(grad_x_ref[2 * channels * rows : 3 * channels * rows, :])
     spread = halves(dot(jnp.concatenate([high, low], axis=0), quarter_t_ref[...]))
     for d in range(5):
@@ -332,13 +529,13 @@
         out[...] = center_ref[place] + a_ref[place] + b_ref[place]
 
 
-def final_kernel(channels, own_ref, pool_ref, *refs):
+def final_kernel(own_ref, *refs):
     out_ref = refs[-1]
     total = refs[0][...]
     for ref in refs[1:-1]:
         total = total + ref[...]
     cols = total.shape[2]
-    spread = dot_t(total.reshape(-1, cols), pool_ref[...])
+    spread = dot_t(total.reshape(-1, cols), pool_matrix(cols))
     count = spread.shape[0]
     for k in range(4):
         part = spread[:, :cols] if k < 2 else spread[:, cols:]
@@ -346,23 +543,34 @@
         out_ref[at, :] = own_ref[at, :] + part
 
 
-def in_vmem(count):
-    return [pl.BlockSpec(memory_space=pltpu.VMEM)] * count
+def in_memory(count, space=pltpu.VMEM):
+    return [pl.BlockSpec(memory_space=space)] * count
 
 
 SCALAR = pl.BlockSpec(memory_space=pltpu.SMEM)
 
 
-def call(kernel, shapes, *operands, scalars=0, scratch=(), name=None):
+def call(kernel, shapes, *operands, scalars=0, scratch=(), name=None, limit=8 << 20, in_place=False, far=(), out_far=()):
     single = not isinstance(shapes, (list, tuple))
+    if in_place:
+        operands = [pltpu.with_memory_space_constraint(operand, pltpu.HBM) for operand in operands]
     outs = [shapes] if single else list(shapes)
+    if in_place:
+        far = range(scalars, len(operands))
+    places = [SCALAR] * scalars + in_memory(len(operands) - scalars)
+    for k in far:
+        places[k] = pl.BlockSpec(memory_space=pltpu.HBM)
+    out_places = in_memory(len(outs))
+    for k in out_far:
+        out_places[k] = pl.BlockSpec(memory_space=pltpu.HBM)
+        outs[k] = pltpu.HBM(outs[k].shape, outs[k].dtype)
     result = pl.pallas_call(
         kernel,
         out_shape=outs,
-        in_specs=[SCALAR] * scalars + in_vmem(len(operands) - scalars),
-        out_specs=in_vmem(len(outs)),
+        in_specs=places,
+        out_specs=out_places,
         scratch_shapes=list(scratch),
-        compiler_params=pltpu.CompilerParams(vmem_limit_bytes=48 << 20),
+        compiler_params=pltpu.CompilerParams(vmem_limit_bytes=limit),
         name=name,
     )(*operands)
     return result[0] if single else result
@@ -399,52 +607,69 @@
         return lax.ppermute(value, "gx", [(s, s ^ 1) for s in range(gx)])
 
     flat_field = field.reshape(channels * rows, cols)
-    pool = jnp.asarray(row_pool_matrix(cols))
+    packed = call(pool_kernel, shape(channels * tall, cols), flat_field, name="pool")
+    packed = packed.reshape(channels, tall, cols)
+
+    held = [packed] + [along_x(packed, -offset) for offset in ring.offsets[1:]]
+    wave = wave_matrix(rows, cols)
+    padded = -(-features // 16) * 16
+    small = -(-channels // 8) * 8
     quarter = quarter_matrix(cols)
-    packed = call(pool_kernel, shape(channels * tall, cols), flat_field, pool, name="pool")
-    packed = packed.reshape(channels, tall, cols)
-
-    held = [packed] + [along_x(packed, -offset) for offset in ring.offsets[1:]]
-    x, y, b1, b2 = angle_tables(rows, cols)
-    table, flipped = call(
-        table_kernel,
-        (shape(cells, 4 * modes, dtype=BF16), shape(4 * modes, cells, dtype=BF16)),
-        *(jnp.asarray(v) for v in (x, y, b1, b2, x.T.copy(), y.T.copy(), b1.T.copy(), b2.T.copy())),
-        name="table",
-    )
-    by_mode = jnp.transpose(spectral, (0, 1, 3, 4, 2))
-    weights = jnp.concatenate([by_mode[:, 0], by_mode[:, 1]], axis=-1)
+    constants = [jnp.asarray(quarter, BF16), wave_pair(wave, 1), wave_pair(wave.T, 0)]
+    packed_weights = shape(layers, width, width, 2 * modes)
+    prepared = list(call(
+        prepare_kernel,
+        [shape(*c.shape, dtype=BF16) for c in constants]
+        + [
+            packed_weights, packed_weights, shape(padded, width), shape(width, padded), shape(width, 3 * padded, dtype=BF16),
+            shape(width, 3 * width, dtype=BF16), shape(width, 3 * width, dtype=BF16), shape(padded, 3 * width, dtype=BF16),
+            shape(width, cells),
+        ],
+        cotangent.reshape(channels * rows, cols), lift, jnp.transpose(spectral, (0, 1, 3, 4, 2)), pointwise, project.T,
+        *constants,
+        in_place=True, out_far=(4,),
+        scratch=(
+            pltpu.VMEM((layers, 2, width, width, modes), F32),
+            pltpu.VMEM(packed_weights.shape, F32),
+            pltpu.VMEM((small * rows, cols), F32),
+            pltpu.VMEM((padded, width), F32),
+            pltpu.VMEM((layers, width, width), F32),
+            pltpu.VMEM((small, width), F32),
+            pltpu.SemaphoreType.DMA((7 + 2 * layers,)),
+        ),
+        limit=16 << 20,
+        name="prepare",
+    ))
+    by_output = prepared.pop(4)
+    quarter_t = jnp.asarray(quarter.T.copy(), BF16)
     held = jnp.stack(held)
     from_a = along_y(held, -2, -1)
     from_b = along_y(held, 2, 1)
+    from_a, from_b, prepared[4] = lax.optimization_barrier((from_a, from_b, prepared[4]))
     swap_a, swap_b = swap(from_a), swap(from_b)
 
-    padded = -(-features // 16) * 16
-    lift_rows = jnp.pad(lift, ((0, padded - features), (0, 0)))
-    small = -(-channels // 8) * 8
-    project_cols = jnp.pad(project, ((0, 0), (0, small - channels)))
     group = shape(blocks, channels, tall, cols)
     chunk = 4 * cols
     own, center, keep_a, keep_b, give_a, give_b = call(
         functools.partial(network_kernel, ring, chunk),
         (shape(channels, rows, cols), group, group, group, group, group),
         core, field.reshape(channels, rows, cols), held, from_a, from_b, swap_a, swap_b,
-        cotangent.reshape(channels, rows, cols), lift_rows, lift_rows.T, weights,
-        pointwise, jnp.transpose(pointwise, (0, 2, 1)), project_cols,
-        jnp.asarray(quarter, BF16), jnp.asarray(quarter.T.copy(), BF16), table, flipped,
-        scalars=1,
+        *(pltpu.with_memory_space_constraint(value, pltpu.HBM) for value in (quarter_t, by_output)), *prepared,
+        scalars=1, far=(7, 8),
         scratch=(
             pltpu.VMEM((padded * rows, cols), F32),
             pltpu.VMEM((5, channels, rows, cols), F32),
             pltpu.VMEM((2 * padded, cells), BF16),
             pltpu.VMEM((2 * width, cells), BF16),
-            pltpu.VMEM((2 * width, cells), BF16),
-            pltpu.VMEM((2 * small, cells), BF16),
             pltpu.VMEM((width, cells), F32),
-            pltpu.VMEM((2, width, 2 * modes), F32),
-            pltpu.VMEM((small * rows, cols), F32),
+            pltpu.VMEM((width, cells), F32),
             pltpu.VMEM((padded * rows, cols), F32),
+            pltpu.VMEM((width, wave.shape[0]), F32),
+            pltpu.VMEM(quarter_t.shape, BF16),
+            pltpu.VMEM(packed_weights.shape, F32),
+            pltpu.SemaphoreType.DMA((2,)),
         ),
+        limit=16 << 20,
         name="network",
     )
 
@@ -457,9 +682,9 @@
     parts = call(gather_kernel, [piece] * blocks, center, sum_a, sum_b, name="gather")
     parts = [parts[0]] + [along_x(part, offset) for part, offset in zip(parts[1:], ring.offsets[1:])]
     out = call(
-        functools.partial(final_kernel, channels),
+        final_kernel,
         shape(channels * rows, cols),
-        own.reshape(channels * rows, cols), pool, *parts,
+        own.reshape(channels * rows, cols), *parts,
         name="final",
     )
     return out.reshape(field.shape)

time: 46.6 us -> 38.8 us (0.83)
  local copies, waits for them, and re-layouts: 5.89 us -> 0.89 us
  waiting for transfers between devices: 13.4 us -> 12.3 us
  Pallas kernels: 11 us -> 10.1 us
    unnamed x43 -> x4, local copies, waits for them, and re-layouts: 5.7 us -> 0.89 us
    ppermute x4, waiting for transfers between devices: 8.96 us -> 6.29 us  [along_y(): return lax.ppermute(value, ('gx', 'gy'), pairs)]
    ppermute x6, waiting for transfers between devices: 2.36 us -> 3.84 us  [along_x(): return lax.ppermute(value, 'gx', [(s, (s + steps) % gx) for s in range(gx)])]
    ppermute x4, starting transfers between devices: 0.74 us -> 1.87 us  [swap(): return lax.ppermute(value, 'gx', [(s, s ^ 1) for s in range(gx)])]
    ppermute x4, starting transfers between devices: 7.09 us -> 5.99 us  [along_y(): return lax.ppermute(value, ('gx', 'gy'), pairs)]
    pallas_call x6, Pallas kernels: 11 us -> 10.1 us  [call(): pl.pallas_call(kernel, out_shape=outs, in_specs=places, out_specs=out_pla...]
  transfers between devices with their start and end apart: 14 -> 14, of which waited for: 10 -> 11; matrix products, arithmetic and copies ran while one was open for 6% -> 0% of each run, Pallas kernels for 4% -> 9%
where the time goes in v1:
time: 38.8 us; the launch traced here: 38.7 us
  starting transfers between devices  15.4 us (40%)
  waiting for transfers between devices  12.3 us (32%)
  Pallas kernels  10.1 us (26%)
  local copies, waits for them, and re-layouts  0.89 us (2%)
    pallas_call x6, Pallas kernels, call(): pl.pallas_call(kernel, out_shape=outs, in_specs=places, out_specs=out_pla...  10.1 us
    ppermute x6, starting transfers between devices, along_x(): return lax.ppermute(value, 'gx', [(s, (s + steps) % gx) for s in range(gx)])  7.53 us
    ppermute x4, waiting for transfers between devices, along_y(): return lax.ppermute(value, ('gx', 'gy'), pairs)  6.29 us
    ppermute x4, starting transfers between devices, along_y(): return lax.ppermute(value, ('gx', 'gy'), pairs)  5.99 us
    ppermute x6, waiting for transfers between devices, along_x(): return lax.ppermute(value, 'gx', [(s, (s + steps) % gx) for s in range(gx)])  3.84 us
    ppermute x4, waiting for transfers between devices, swap(): return lax.ppermute(value, 'gx', [(s, s ^ 1) for s in range(gx)])  2.12 us
    ppermute x4, starting transfers between devices, swap(): return lax.ppermute(value, 'gx', [(s, s ^ 1) for s in range(gx)])  1.87 us
    unnamed x4, local copies, waits for them, and re-layouts  0.89 us
  transfers between devices with their start and end apart: 14, of which 11 were waited for; matrix products, arithmetic and copies ran while one was open for 0% of the time, Pallas kernels for 9%

profile of v1, /device:TPU:0, one launch (start us, length us, event | category | flops | bytes accessed | tf_op | source)
XLA Modules:
  0.0 38.7 jit_solution(38079988616996070)
XLA Ops:
  0.0 0.9 %copy-done = f32[5,1,32,128]{3,2,1,0:T(8,128)S(1)} copy-done((f32[5,1,32,128]{3,2,1,0:T(8,128)S(1)}, f32[5,1,32,128]{3,2,1,0:T(8,128)}, u32[]{:S(2)}) %copy-start) | copy-done | bytes 81944
  0.9 0.2 pool.1
  1.1 0.5 %collective-permute-start.2 = (f32[5,8,128]{2,1,0:T(8,128)S(1)}, f32[5,8,128]{2,1,0:T(8,128)S(1)}, u32[]{:S(2)}, u32[]{:S(2)}) collective-permute-start(f32[5,8,128]{2,1,0:T(8,128)S(1)} %bitcast.17), channel_id=1, source_target_pairs={{0,8},{8,16},{16,24},{24,0},{1,9},{9,17},{17,25},{25,1},{2,10},{10... | collective-permute-start | bytes 61448 | tf_op jit(solution)/shard_map/ppermute | solution.py:596
  1.7 2.6 %collective-permute-start.1 = (f32[5,8,128]{2,1,0:T(8,128)S(1)}, f32[5,8,128]{2,1,0:T(8,128)S(1)}, u32[]{:S(2)}, u32[]{:S(2)}) collective-permute-start(f32[5,8,128]{2,1,0:T(8,128)S(1)} %bitcast.18), channel_id=1, source_target_pairs={{0,16},{8,24},{16,0},{24,8},{1,17},{9,25},{17,1},{25,9},{2,18},{10... | collective-permute-start | bytes 61448 | tf_op jit(solution)/shard_map/ppermute | solution.py:596
  4.2 1.4 %collective-permute-start = (f32[5,8,128]{2,1,0:T(8,128)S(1)}, f32[5,8,128]{2,1,0:T(8,128)S(1)}, u32[]{:S(2)}, u32[]{:S(2)}) collective-permute-start(f32[5,8,128]{2,1,0:T(8,128)S(1)} %bitcast.19), channel_id=1, source_target_pairs={{0,24},{8,0},{16,8},{24,16},{1,25},{9,1},{17,9},{25,17},{2,26},{10... | collective-permute-start | bytes 61448 | tf_op jit(solution)/shard_map/ppermute | solution.py:596
  5.6 0.0 collective-permute-done.2
  5.6 0.4 collective-permute-done.1
  6.0 1.1 %collective-permute-done = f32[5,8,128]{2,1,0:T(8,128)S(1)} collective-permute-done((f32[5,8,128]{2,1,0:T(8,128)S(1)}, f32[5,8,128]{2,1,0:T(8,128)S(1)}, u32[]{:S(2)}, u32[]{:S(2)}) %collective-permute-start) | collective-permute-done | bytes 20512 | tf_op jit(solution)/shard_map/ppermute | solution.py:596
  7.1 1.6 %collective-permute-start.4 = (f32[4,5,8,128]{3,2,1,0:T(8,128)S(1)}, f32[4,5,8,128]{3,2,1,0:T(8,128)S(1)}, u32[]{:S(2)}, u32[]{:S(2)}) collective-permute-start(f32[4,5,8,128]{3,2,1,0:T(8,128)S(1)} %pad_maximum_fusion.blocks_ref), channel_id=1, source_target_pairs={{0,2},{1,3},{2,4},{3,5},{4,6},{5,7},{6,0},{7,1},{8,9},{9,10},{10,1... | collective-permute-start | bytes 245768 | tf_op jit(solution)/shard_map/ppermute | solution.py:604
  8.7 2.2 %collective-permute-start.3 = (f32[4,5,8,128]{3,2,1,0:T(8,128)S(1)}, f32[4,5,8,128]{3,2,1,0:T(8,128)S(1)}, u32[]{:S(2)}, u32[]{:S(2)}) collective-permute-start(f32[4,5,8,128]{3,2,1,0:T(8,128)S(1)} %pad_maximum_fusion.blocks_ref), channel_id=1, source_target_pairs={{0,6},{1,7},{2,0},{3,1},{4,2},{5,3},{6,4},{7,5},{8,15},{9,8},{10,9... | collective-permute-start | bytes 245768 | tf_op jit(solution)/shard_map/ppermute | solution.py:604
  10.9 3.6 %prepare.1 = (bf16[640,128]{1,0:T(8,128)(2,1)S(1)}, bf16[1152,256]{1,0:T(8,128)(2,1)S(1)}, bf16[256,1152]{1,0:T(8,128)(2,1)S(1)}, f32[2,32,32,128]{3,2,1,0:T(8,1...) custom-call(f32[160,128]{1,0:T(8,128)} %bitcast.23, ...), custom_call_target="tpu_custom_call" | custom-call | tf_op jit(solution)/shard_map/prepare/pallas_call | solution.py:567
  14.5 0.0 collective-permute-done.4.near_b
  14.5 0.1 collective-permute-done.3.near_a
  14.5 1.2 %collective-permute-start.5 = (f32[4,5,8,128]{3,2,1,0:T(8,128)S(1)}, f32[4,5,8,128]{3,2,1,0:T(8,128)S(1)}, u32[]{:S(2)}, u32[]{:S(2)}) collective-permute-start(f32[4,5,8,128]{3,2,1,0:T(8,128)S(1)} %collective-permute-done.3.near_a), channel_id=1, source_target_pairs={{0,8},{8,0},{16,24},{24,16},{1,9},{9,1},{17,25},{25,17},{2,10},{10... | collective-permute-start | bytes 245768 | tf_op jit(solution)/shard_map/ppermute | solution.py:607
  15.8 0.1 collective-permute-start.6
  15.8 0.8 %collective-permute-done.5.swap_a = f32[4,5,8,128]{3,2,1,0:T(8,128)S(1)} collective-permute-done((f32[4,5,8,128]{3,2,1,0:T(8,128)S(1)}, f32[4,5,8,128]{3,2,1,0:T(8,128)S(1)}, u32[]{:S(2)}, u32[]{:S(2)}) %collective-permute-start.5) | collective-permute-done | bytes 81952 | tf_op jit(solution)/shard_map/ppermute | solution.py:607
  16.7 0.4 collective-permute-done.6.swap_b
  17.0 5.4 %network.1 = (f32[5,32,128]{2,1,0:T(8,128)S(1)}, f32[4,5,8,128]{3,2,1,0:T(8,128)S(1)}, f32[4,5,8,128]{3,2,1,0:T(8,128)S(1)}, f32[4,5,8,128]{3,2,1,0:T(8,128)S(1)...) custom-call(s32[1]{0:T(128)} %bitcast.core_ref, f32[5,32,128]{2,1,0:T(8,128)S(1)} %bitcast.16, ...), custom_call_target="tpu_custom_call" | custom-call | tf_op jit(solution)/shard_map/network/pallas_call | solution.py:567
  22.4 0.2 collective-permute-start.7
  22.6 0.4 collective-permute-start.8
  23.0 0.8 %collective-permute-done.7.got_a = f32[4,5,8,128]{3,2,1,0:T(8,128)S(1)} collective-permute-done((f32[4,5,8,128]{3,2,1,0:T(8,128)S(1)}, f32[4,5,8,128]{3,2,1,0:T(8,128)S(1)}, u32[]{:S(2)}, u32[]{:S(2)}) %collective-permute-start.7) | collective-permute-done | bytes 81952 | tf_op jit(solution)/shard_map/ppermute | solution.py:607
  23.8 0.2 collective-permute-done.8.got_b
  23.9 2.2 %collective-permute-start.9 = (f32[4,5,8,128]{3,2,1,0:T(8,128)S(1)}, f32[4,5,8,128]{3,2,1,0:T(8,128)S(1)}, u32[]{:S(2)}, u32[]{:S(2)}) collective-permute-start(f32[4,5,8,128]{3,2,1,0:T(8,128)S(1)} %get-tuple-element.53), channel_id=1, source_target_pairs={{0,6},{1,7},{2,0},{3,1},{4,2},{5,3},{6,4},{7,5},{8,15},{9,8},{10,9... | collective-permute-start | bytes 245768 | tf_op jit(solution)/shard_map/ppermute | solution.py:604
  26.1 0.0 collective-permute-start.10
  26.1 2.8 %collective-permute-done.9.a_ref = f32[4,5,8,128]{3,2,1,0:T(8,128)S(1)} collective-permute-done((f32[4,5,8,128]{3,2,1,0:T(8,128)S(1)}, f32[4,5,8,128]{3,2,1,0:T(8,128)S(1)}, u32[]{:S(2)}, u32[]{:S(2)}) %collective-permute-start.9) | collective-permute-done | bytes 81952 | tf_op jit(solution)/shard_map/ppermute | solution.py:604
  28.9 3.4 %collective-permute-done.10.b_ref = f32[4,5,8,128]{3,2,1,0:T(8,128)S(1)} collective-permute-done((f32[4,5,8,128]{3,2,1,0:T(8,128)S(1)}, f32[4,5,8,128]{3,2,1,0:T(8,128)S(1)}, u32[]{:S(2)}, u32[]{:S(2)}) %collective-permute-start.10) | collective-permute-done | bytes 81952 | tf_op jit(solution)/shard_map/ppermute | solution.py:604
  32.4 1.6 %collective-permute-start.11 = (f32[5,8,128]{2,1,0:T(8,128)S(1)}, f32[5,8,128]{2,1,0:T(8,128)S(1)}, u32[]{:S(2)}, u32[]{:S(2)}) collective-permute-start(f32[5,8,128]{2,1,0:T(8,128)S(1)} %get-tuple-element.56), channel_id=1, source_target_pairs={{0,8},{8,16},{16,24},{24,0},{1,9},{9,17},{17,25},{25,1},{2,10},{10... | collective-permute-start | bytes 61448 | tf_op jit(solution)/shard_map/ppermute | solution.py:596
  34.0 1.1 %collective-permute-start.12 = (f32[5,8,128]{2,1,0:T(8,128)S(1)}, f32[5,8,128]{2,1,0:T(8,128)S(1)}, u32[]{:S(2)}, u32[]{:S(2)}) collective-permute-start(f32[5,8,128]{2,1,0:T(8,128)S(1)} %get-tuple-element.57), channel_id=1, source_target_pairs={{0,16},{8,24},{16,0},{24,8},{1,17},{9,25},{17,1},{25,9},{2,18},{10... | collective-permute-start | bytes 61448 | tf_op jit(solution)/shard_map/ppermute | solution.py:596
  35.1 0.3 collective-permute-start.13
  35.4 0.8 %collective-permute-done.11.refs_1_ = f32[5,8,128]{2,1,0:T(8,128)S(1)} collective-permute-done((f32[5,8,128]{2,1,0:T(8,128)S(1)}, f32[5,8,128]{2,1,0:T(8,128)S(1)}, u32[]{:S(2)}, u32[]{:S(2)}) %collective-permute-start.11) | collective-permute-done | bytes 20512 | tf_op jit(solution)/shard_map/ppermute | solution.py:596
  36.2 1.6 %collective-permute-done.12.refs_2_ = f32[5,8,128]{2,1,0:T(8,128)S(1)} collective-permute-done((f32[5,8,128]{2,1,0:T(8,128)S(1)}, f32[5,8,128]{2,1,0:T(8,128)S(1)}, u32[]{:S(2)}, u32[]{:S(2)}) %collective-permute-start.12) | collective-permute-done | bytes 20512 | tf_op jit(solution)/shard_map/ppermute | solution.py:596
  37.8 0.9 %final.1 = f32[160,128]{1,0:T(8,128)} custom-call(f32[160,128]{1,0:T(8,128)S(1)} %bitcast.21, f32[5,8,128]{2,1,0:T(8,128)S(1)} %get-tuple-element.55.refs_0_, f32[5,8,128]{2,1,0:T(8,128)S(1)} %collective-permute-done.11.refs_1_, f32[5,8,128]{2,1,0:T(8,128)S(1)} %collective-permute-done.12.refs_2_, f32[5,8,128]{2,1,0:T(8,128)S(1)} %collective-permute-done.13.refs_3_), custom_call_target="tpu_custom_call" | custom-call | tf_op jit(solution)/shard_map/final/pallas_call | solution.py:567
  (7 shorter events, 0.1 us)
Async XLA Ops:
  0.0 0.9 %copy-start = (f32[5,1,32,128]{3,2,1,0:T(8,128)S(1)}, f32[5,1,32,128]{3,2,1,0:T(8,128)}, u32[]{:S(2)}) copy-start(f32[5,1,32,128]{3,2,1,0:T(8,128)} %param.10) | copy-start | bytes 245764
  0.9 16.1 %copy-start.1 = (f32[5,1,32,128]{3,2,1,0:T(8,128)S(1)}, f32[5,1,32,128]{3,2,1,0:T(8,128)}, u32[]{:S(2)}) copy-start(f32[5,1,32,128]{3,2,1,0:T(8,128)} %param.10) | copy-start | bytes 245764
  1.1 4.5 %collective-permute-start.2 = (f32[5,8,128]{2,1,0:T(8,128)S(1)}, f32[5,8,128]{2,1,0:T(8,128)S(1)}, u32[]{:S(2)}, u32[]{:S(2)}) collective-permute-start(f32[5,8,128]{2,1,0:T(8,128)S(1)} %bitcast.17), channel_id=1, source_target_pairs={{0,8},{8,16},{16,24},{24,0},{1,9},{9,17},{17,25},{25,1},{2,10},{10... | collective-permute-start | bytes 61448 | tf_op jit(solution)/shard_map/ppermute | solution.py:596
  1.7 4.3 %collective-permute-start.1 = (f32[5,8,128]{2,1,0:T(8,128)S(1)}, f32[5,8,128]{2,1,0:T(8,128)S(1)}, u32[]{:S(2)}, u32[]{:S(2)}) collective-permute-start(f32[5,8,128]{2,1,0:T(8,128)S(1)} %bitcast.18), channel_id=1, source_target_pairs={{0,16},{8,24},{16,0},{24,8},{1,17},{9,25},{17,1},{25,9},{2,18},{10... | collective-permute-start | bytes 61448 | tf_op jit(solution)/shard_map/ppermute | solution.py:596
  4.2 2.9 %collective-permute-start = (f32[5,8,128]{2,1,0:T(8,128)S(1)}, f32[5,8,128]{2,1,0:T(8,128)S(1)}, u32[]{:S(2)}, u32[]{:S(2)}) collective-permute-start(f32[5,8,128]{2,1,0:T(8,128)S(1)} %bitcast.19), channel_id=1, source_target_pairs={{0,24},{8,0},{16,8},{24,16},{1,25},{9,1},{17,9},{25,17},{2,26},{10... | collective-permute-start | bytes 61448 | tf_op jit(solution)/shard_map/ppermute | solution.py:596
  7.1 7.4 %collective-permute-start.4 = (f32[4,5,8,128]{3,2,1,0:T(8,128)S(1)}, f32[4,5,8,128]{3,2,1,0:T(8,128)S(1)}, u32[]{:S(2)}, u32[]{:S(2)}) collective-permute-start(f32[4,5,8,128]{3,2,1,0:T(8,128)S(1)} %pad_maximum_fusion.blocks_ref), channel_id=1, source_target_pairs={{0,2},{1,3},{2,4},{3,5},{4,6},{5,7},{6,0},{7,1},{8,9},{9,10},{10,1... | collective-permute-start | bytes 245768 | tf_op jit(solution)/shard_map/ppermute | solution.py:604
  8.7 5.9 %collective-permute-start.3 = (f32[4,5,8,128]{3,2,1,0:T(8,128)S(1)}, f32[4,5,8,128]{3,2,1,0:T(8,128)S(1)}, u32[]{:S(2)}, u32[]{:S(2)}) collective-permute-start(f32[4,5,8,128]{3,2,1,0:T(8,128)S(1)} %pad_maximum_fusion.blocks_ref), channel_id=1, source_target_pairs={{0,6},{1,7},{2,0},{3,1},{4,2},{5,3},{6,4},{7,5},{8,15},{9,8},{10,9... | collective-permute-start | bytes 245768 | tf_op jit(solution)/shard_map/ppermute | solution.py:604
  14.5 2.1 %collective-permute-start.5 = (f32[4,5,8,128]{3,2,1,0:T(8,128)S(1)}, f32[4,5,8,128]{3,2,1,0:T(8,128)S(1)}, u32[]{:S(2)}, u32[]{:S(2)}) collective-permute-start(f32[4,5,8,128]{3,2,1,0:T(8,128)S(1)} %collective-permute-done.3.near_a), channel_id=1, source_target_pairs={{0,8},{8,0},{16,24},{24,16},{1,9},{9,1},{17,25},{25,17},{2,10},{10... | collective-permute-start | bytes 245768 | tf_op jit(solution)/shard_map/ppermute | solution.py:607
  15.8 1.3 %collective-permute-start.6 = (f32[4,5,8,128]{3,2,1,0:T(8,128)S(1)}, f32[4,5,8,128]{3,2,1,0:T(8,128)S(1)}, u32[]{:S(2)}, u32[]{:S(2)}) collective-permute-start(f32[4,5,8,128]{3,2,1,0:T(8,128)S(1)} %collective-permute-done.4.near_b), channel_id=1, source_target_pairs={{0,8},{8,0},{16,24},{24,16},{1,9},{9,1},{17,25},{25,17},{2,10},{10... | collective-permute-start | bytes 245768 | tf_op jit(solution)/shard_map/ppermute | solution.py:607
  22.4 1.3 %collective-permute-start.7 = (f32[4,5,8,128]{3,2,1,0:T(8,128)S(1)}, f32[4,5,8,128]{3,2,1,0:T(8,128)S(1)}, u32[]{:S(2)}, u32[]{:S(2)}) collective-permute-start(f32[4,5,8,128]{3,2,1,0:T(8,128)S(1)} %get-tuple-element.51), channel_id=1, source_target_pairs={{0,8},{8,0},{16,24},{24,16},{1,9},{9,1},{17,25},{25,17},{2,10},{10... | collective-permute-start | bytes 245768 | tf_op jit(solution)/shard_map/ppermute | solution.py:607
  22.6 1.3 %collective-permute-start.8 = (f32[4,5,8,128]{3,2,1,0:T(8,128)S(1)}, f32[4,5,8,128]{3,2,1,0:T(8,128)S(1)}, u32[]{:S(2)}, u32[]{:S(2)}) collective-permute-start(f32[4,5,8,128]{3,2,1,0:T(8,128)S(1)} %get-tuple-element.52), channel_id=1, source_target_pairs={{0,8},{8,0},{16,24},{24,16},{1,9},{9,1},{17,25},{25,17},{2,10},{10... | collective-permute-start | bytes 245768 | tf_op jit(solution)/shard_map/ppermute | solution.py:607
  23.9 5.0 %collective-permute-start.9 = (f32[4,5,8,128]{3,2,1,0:T(8,128)S(1)}, f32[4,5,8,128]{3,2,1,0:T(8,128)S(1)}, u32[]{:S(2)}, u32[]{:S(2)}) collective-permute-start(f32[4,5,8,128]{3,2,1,0:T(8,128)S(1)} %get-tuple-element.53), channel_id=1, source_target_pairs={{0,6},{1,7},{2,0},{3,1},{4,2},{5,3},{6,4},{7,5},{8,15},{9,8},{10,9... | collective-permute-start | bytes 245768 | tf_op jit(solution)/shard_map/ppermute | solution.py:604
  26.1 6.2 %collective-permute-start.10 = (f32[4,5,8,128]{3,2,1,0:T(8,128)S(1)}, f32[4,5,8,128]{3,2,1,0:T(8,128)S(1)}, u32[]{:S(2)}, u32[]{:S(2)}) collective-permute-start(f32[4,5,8,128]{3,2,1,0:T(8,128)S(1)} %get-tuple-element.54), channel_id=1, source_target_pairs={{0,2},{1,3},{2,4},{3,5},{4,6},{5,7},{6,0},{7,1},{8,9},{9,10},{10,1... | collective-permute-start | bytes 245768 | tf_op jit(solution)/shard_map/ppermute | solution.py:604
  32.4 3.8 %collective-permute-start.11 = (f32[5,8,128]{2,1,0:T(8,128)S(1)}, f32[5,8,128]{2,1,0:T(8,128)S(1)}, u32[]{:S(2)}, u32[]{:S(2)}) collective-permute-start(f32[5,8,128]{2,1,0:T(8,128)S(1)} %get-tuple-element.56), channel_id=1, source_target_pairs={{0,8},{8,16},{16,24},{24,0},{1,9},{9,17},{17,25},{25,1},{2,10},{10... | collective-permute-start | bytes 61448 | tf_op jit(solution)/shard_map/ppermute | solution.py:596
  34.0 3.8 %collective-permute-start.12 = (f32[5,8,128]{2,1,0:T(8,128)S(1)}, f32[5,8,128]{2,1,0:T(8,128)S(1)}, u32[]{:S(2)}, u32[]{:S(2)}) collective-permute-start(f32[5,8,128]{2,1,0:T(8,128)S(1)} %get-tuple-element.57), channel_id=1, source_target_pairs={{0,16},{8,24},{16,0},{24,8},{1,17},{9,25},{17,1},{25,9},{2,18},{10... | collective-permute-start | bytes 61448 | tf_op jit(solution)/shard_map/ppermute | solution.py:596
  35.1 2.7 %collective-permute-start.13 = (f32[5,8,128]{2,1,0:T(8,128)S(1)}, f32[5,8,128]{2,1,0:T(8,128)S(1)}, u32[]{:S(2)}, u32[]{:S(2)}) collective-permute-start(f32[5,8,128]{2,1,0:T(8,128)S(1)} %get-tuple-element.58), channel_id=1, source_target_pairs={{0,24},{8,0},{16,8},{24,16},{1,25},{9,1},{17,9},{25,17},{2,26},{10... | collective-permute-start | bytes 61448 | tf_op jit(solution)/shard_map/ppermute | solution.py:596

commit v2 on v1

--- a/solution.py
+++ b/solution.py
@@ -16,16 +16,27 @@
 INV_SQRT_2PI = float(1.0 / np.sqrt(2.0 * np.pi))
 
 
-class Ring:
-    def __init__(self, count):
-        self.count = count
-        self.whole = count <= 7
-        self.offsets = list(range(count)) if self.whole else [0, 1, 2, 3, -3, -2, -1]
+class Chip:
+    def __init__(self, count, channels):
+        self.ring = count == 4
+        self.offsets = [0, -1, 1, 2] if self.ring else [0, -1, 1, 2, -2, 3, -3]
+        self.returned = [0, 1, 2, -1] if self.ring else [0, 1, 2, 3, -3, -2, -1]
+        self.shared = [0, 1, 2, -1] if self.ring else [-2, -1, 0, 1, 2, 3]
+        self.edge_tiles = channels + (channels + 1) // 2
+        self.tiles = self.edge_tiles + channels * -(-len(self.shared) // 4)
 
     def place(self, offset):
-        if self.whole:
-            return offset % self.count
-        return self.offsets.index(max(-3, min(3, offset)))
+        return self.offsets.index((offset + 1) % 4 - 1 if self.ring else offset)
+
+    def group(self, offset):
+        return offset % 4 if self.ring else self.shared.index(offset)
+
+    def within(self, offset):
+        return self.ring or offset in self.shared
+
+    def quarter_tile(self, channel, group):
+        channels = (self.tiles - self.edge_tiles) // -(-len(self.shared) // 4)
+        return self.edge_tiles + (group // 4) * channels + channel
 
 
 def split(value):
@@ -55,17 +66,6 @@
 def halves(value):
     rows = value.shape[0] // 2
     return value[:rows] + value[rows:]
-
-
-def quarter_matrix(cols):
-    half, quarter, eighth = cols // 2, cols // 4, cols // 8
-    out = np.zeros((5 * cols, cols), np.float32)
-    for lane in range(cols):
-        coarse = lane - eighth * 3
-        d, t = coarse // quarter, coarse % quarter
-        for m in (2 * t, 2 * t + 1, half + 2 * t, half + 2 * t + 1):
-            out[(d + 2) * cols + m, lane] = 0.25
-    return out
 
 
 def wave_matrix(rows, cols):
@@ -191,21 +191,21 @@
 def prepare_kernel(
     cotangent_hbm, lift_hbm, spectral_hbm, pointwise_hbm, project_hbm, *refs
 ):
-    constants_hbm, refs = refs[:3], refs[3:]
-    constants, refs = refs[:3], refs[3:]
-    by_input, by_output_hbm, lift_ref, lift_t_ref, local_one, local_two, back_two, back_one, target_grad = refs[:9]
-    spectral_ref, by_output, target_ref, lift_in, pointwise_ref, project_ref, sems = refs[9:]
+    constants_hbm, refs = refs[:2], refs[2:]
+    constants, refs = refs[:2], refs[2:]
+    by_input, lift_ref, lift_t_ref, local_one, local_two, back_two, back_one, target_grad = refs[:8]
+    spectral_ref, target_ref, lift_in, pointwise_ref, project_ref, sems = refs[8:]
     layers, _, width, _, modes = spectral_ref.shape
     small, cols = project_ref.shape[0], target_ref.shape[1]
     rows = target_ref.shape[0] // small
     channels, features = project_hbm.shape[0], lift_hbm.shape[0]
-    pairs = [
+    pairs = [(spectral_hbm.at[layer], spectral_ref.at[layer]) for layer in range(layers)]
+    pairs += [
         (cotangent_hbm, target_ref.at[: channels * rows]),
         (project_hbm, project_ref.at[:channels]),
         (lift_hbm, lift_in.at[:features]),
         (pointwise_hbm, pointwise_ref),
     ]
-    pairs += [(spectral_hbm.at[layer], spectral_ref.at[layer]) for layer in range(layers)]
     pairs += list(zip(constants_hbm, constants))
     copies = [pltpu.make_async_copy(source, target, sems.at[k]) for k, (source, target) in enumerate(pairs)]
     for copy in copies:
@@ -213,7 +213,12 @@
     target_ref[channels * rows :, :] = jnp.zeros(((small - channels) * rows, cols), F32)
     project_ref[channels:, :] = jnp.zeros((small - channels, width), F32)
     lift_in[features:, :] = jnp.zeros((lift_in.shape[0] - features, width), F32)
-    for copy in copies[:4]:
+    for layer in range(layers):
+        copies[layer].wait()
+        for w in range(width):
+            both = [spectral_ref[layer, part, w] for part in range(2)]
+            by_input[layer, w] = jnp.concatenate(both, axis=1)
+    for copy in copies[layers : layers + 4]:
         copy.wait()
 
     lift = lift_in[...]
@@ -234,33 +239,90 @@
             pieces.append(jnp.concatenate([high, value - high, high], axis=0).astype(BF16))
         target_grad[:, first * cols : (first + group) * cols] = dot(out, jnp.concatenate(pieces, axis=1))
 
-    for layer in range(layers):
-        copies[4 + layer].wait()
-        for w in range(width):
-            both = [spectral_ref[layer, part, w] for part in range(2)]
-            by_input[layer, w] = jnp.concatenate(both, axis=1)
-        for o in range(width):
-            for first in range(0, width, 8):
-                both = [spectral_ref[layer, part, first : first + 8, o, :] for part in range(2)]
-                by_output[layer, o, first : first + 8, :] = jnp.concatenate(both, axis=1)
-        copies.append(pltpu.make_async_copy(by_output.at[layer], by_output_hbm.at[layer], sems.at[len(copies)]))
-        copies[-1].start()
     for copy in copies[4 + layers :]:
         copy.wait()
 
 
-def pool_matrix(cols):
-    half = cols // 2
-    row = lax.broadcasted_iota(jnp.int32, (2 * cols, cols), 0)
-    col = lax.broadcasted_iota(jnp.int32, (2 * cols, cols), 1)
-    return jnp.where(row // 2 == col, 0.25, 0.0).astype(F32)
+def index_of(shape, axis):
+    return lax.broadcasted_iota(jnp.int32, shape, axis)
+
+
+def quarter_matrix(cols, flipped=False):
+    shape = (2 * cols, cols)
+    fine, coarse = (index_of(shape, 1), index_of(shape, 0)) if flipped else (index_of(shape, 0), index_of(shape, 1))
+    fine, coarse = fine % (cols // 2) // 2, coarse % (cols // 4)
+    return jnp.where(fine == coarse, 0.25, 0.0).astype(BF16)
+
+
+def spread_matrix(cols):
+    shape = (2 * cols, 2 * cols)
+    row, col = index_of(shape, 0) % cols, index_of(shape, 1)
+    return jnp.where(row == col // 2, 0.25, 0.0).astype(BF16)
+
+
+def pooling_matrix(cols):
+    shape = (2 * cols, cols)
+    return jnp.where(index_of(shape, 0) // 2 == index_of(shape, 1), 0.25, 0.0).astype(BF16)
+
+
+def beside(value):
+    return jnp.concatenate(split(value), axis=1)
+
+
+def above(value):
+    return jnp.concatenate(split(value), axis=0)
+
+
+def turned(value, steps):
+    lanes = value.shape[-1]
+    if steps % lanes == 0:
+        return value
+    flat = value.reshape(-1, lanes)
+    return pltpu.roll(flat, steps % lanes, 1).reshape(value.shape)
+
+
+def by_group(values, lanes):
+    lane = index_of((1,) * (values[0].ndim - 1) + (lanes,), values[0].ndim - 1)
+    q = lanes // 4
+    low = jnp.where(lane < q, values[0], values[1])
+    high = jnp.where(lane < 3 * q, values[2], values[3])
+    return jnp.where(lane < 2 * q, low, high)
 
 
 def pool_kernel(field_ref, out_ref):
     count = field_ref.shape[0] // 4
     rows = [field_ref[pl.ds(k, count, stride=4), :] for k in range(4)]
     pairs = jnp.concatenate([rows[0] + rows[1], rows[2] + rows[3]], axis=1)
-    out_ref[...] = exact_dot(pairs, pool_matrix(field_ref.shape[1]))
+    out_ref[...] = halves(dot(above(pairs), pooling_matrix(field_ref.shape[1])))
+
+
+def pack_kernel(chip, core_ref, *refs):
+    blocks, (to_previous, to_following) = refs[: len(chip.offsets)], refs[len(chip.offsets) :]
+    channels, tall, cols = blocks[0].shape
+    q = cols // 4
+    odd = core_ref[0] == 1
+    sub = index_of((1, tall, cols), 1)
+    shared = {}
+    for e in chip.shared:
+        even_at, odd_at = chip.place(e), (chip.place(e - 1))
+        shared[e] = jnp.where(odd, blocks[odd_at][...], blocks[even_at][...])
+    stacked_rows = jnp.concatenate([shared[e].reshape(channels * tall, cols) for e in chip.shared], axis=0)
+    coarse = dot(beside(stacked_rows), quarter_matrix(cols)).reshape(len(chip.shared), channels, tall, cols)
+    for first in range(0, len(chip.shared), 4):
+        groups = [min(first + k, len(chip.shared) - 1) for k in range(4)]
+        tile = by_group([coarse[k] for k in groups], cols)
+        at = chip.quarter_tile(0, first)
+        to_previous[at : at + channels] = tile
+        to_following[at : at + channels] = tile
+    outer = jnp.where(sub < tall // 2, shared[2], shared[-1])
+
+    def pair(one, two, shifts):
+        return by_group([turned(v, k * q) for v, k in zip((one, one, two, two), shifts)], cols)
+
+    for ref, shifts in ((to_previous, (0, -1, 2, 1)), (to_following, (-1, -2, 1, 0))):
+        ref[:channels] = pair(shared[0], shared[1], shifts)
+        for c in range(0, channels, 2):
+            ref[channels + c // 2] = pair(outer[c], outer[min(c + 1, channels - 1)], shifts)
 
 
 def mix(weights, layer, coefficients):
@@ -280,21 +342,38 @@
     return jnp.where(lane < half, total_real, total_imag)
 
 
+def rows_summed(values):
+    row = index_of(values[0].shape, 0)
+    step = 1
+    while len(values) > 1:
+        held = (row & step) != 0
+        values = [
+            jnp.where(held, x, y) + pltpu.roll(jnp.where(held, y, x), step, 0) for y, x in zip(values[::2], values[1::2])
+        ]
+        step *= 2
+    return values[0]
+
+
 def unmix(weights, layer, grads):
     width, lanes = grads.shape
     half = lanes // 2
-    lane = lax.broadcasted_iota(jnp.int32, (width, lanes), 1)
-    turned = pltpu.roll(grads, half, 1)
-    turned = jnp.where(lane < half, turned, -turned)
-    total_real = jnp.zeros((width, lanes), F32)
-    total_imag = jnp.zeros((width, lanes), F32)
-    for o in range(width):
-        block = weights[layer, o]
-        total_real += block * grads[o : o + 1]
-        total_imag += block * turned[o : o + 1]
-    total_real += pltpu.roll(total_real, half, 1)
-    total_imag += pltpu.roll(total_imag, half, 1)
-    return jnp.where(lane < half, total_real, total_imag)
+    lane = index_of((width, lanes), 1)
+    turned_grads = pltpu.roll(grads, half, 1)
+    turned_grads = jnp.where(lane < half, turned_grads, -turned_grads)
+
+    def folded(block, value):
+        product = block * value
+        return sum(product[k : k + 8] for k in range(8, width, 8)) + product[:8]
+
+    real, imag = [], []
+    for first in range(0, width, 8):
+        blocks = [weights[layer, w] for w in range(first, first + 8)]
+        real.append(rows_summed([folded(block, grads) for block in blocks]))
+        imag.append(rows_summed([folded(block, turned_grads) for block in blocks]))
+    real, imag = jnp.concatenate(real, axis=0), jnp.concatenate(imag, axis=0)
+    real += pltpu.roll(real, half, 1)
+    imag += pltpu.roll(imag, half, 1)
+    return jnp.where(lane < half, real, imag)
 
 
 def contract(parts, wave):
@@ -324,67 +403,72 @@
 
 
 def network_kernel(
-    ring, chunk,
-    core_ref, field_ref, blocks_ref, near_a, near_b, swap_a, swap_b, quarter_t_hbm, by_output_hbm,
-    quarter_ref, wave_ref, wave_t_ref, by_input, lift_ref, lift_t_ref, local_one, local_two, back_two, back_one, target_grad,
-    own_ref, center_ref, keep_a, keep_b, give_a, give_b,
-    x_ref, window_ref, feature_pair, hidden_pair, slope_one, local_ref, grad_x_ref, parts_ref,
-    quarter_t_ref, by_output, sems,
+    chip, chunk,
+    core_ref, field_ref, here_ref, after_ref, before_ref, mine_ref, got_after, got_before, other_after, other_before,
+    wave_ref, wave_t_ref, by_input, lift_ref, lift_t_ref, local_one, local_two, back_two, back_one, target_grad,
+    own_ref, center_edge, center_quarter, keep_a, keep_b, give_a, give_b,
+    x_ref, even_ref, odd_ref, mid_ref, far_ref, far_blocks, feature_pair, hidden_pair, slope_one, local_ref, grad_x_ref, parts_ref,
 ):
     channels, rows, cols = field_ref.shape
     tall = rows // 4
-    half, quarter = cols // 2, cols // 4
+    q = cols // 4
     cells = rows * cols
     width = slope_one.shape[0]
     padded = x_ref.shape[0] // rows
     odd = core_ref[0] == 1
-    lane = lax.broadcasted_iota(jnp.int32, (1, 1, cols), 2)
-
-    late = [(by_output_hbm, by_output), (quarter_t_hbm, quarter_t_ref)]
-    late = [pltpu.make_async_copy(source, target, sems.at[k]) for k, (source, target) in enumerate(late)]
-    for copy in late:
-        copy.start()
-
-    for d in range(-2, 3):
-        for e in range(-2, 3):
-            here = ring.place(e)
-            if d == 0:
-                block = blocks_ref[here]
-            else:
-                there = jnp.where(odd, ring.place(e + 1), ring.place(e - 1))
-                direct, swapped = (near_a, swap_a) if d > 0 else (near_b, swap_b)
-                block = jnp.where(odd == (abs(d) == 1), direct[here], swapped[there])
-            if e == -2:
-                window_ref[d + 2, :, : tall // 2, :] = block[:, tall // 2 :, :]
-            elif e == 2:
-                window_ref[d + 2, :, 4 * tall - tall // 2 :, :] = block[:, : tall // 2, :]
-            else:
-                first = tall // 2 + (e + 1) * tall
-                window_ref[d + 2, :, first : first + tall, :] = block
-
+    shift = core_ref[0] * tall
+    lane = index_of((1, 1, cols), 2)
     for c in range(channels):
         x_ref[c * rows : (c + 1) * rows, :] = field_ref[c]
-    previous, own, following = (window_ref[d, :, tall : 3 * tall, :] for d in (1, 2, 3))
-
-    def turn(value, steps):
-        flat = value.reshape(channels * 2 * tall, cols)
-        return pltpu.roll(flat, steps % cols, 1).reshape(value.shape)
-
-    def three(a, b, c):
-        return jnp.where(lane < quarter, a, jnp.where(lane < 3 * quarter, b, c))
-
-    even_rows = three(turn(previous, -quarter), turn(own, quarter), turn(following, -quarter))
-    odd_rows = three(turn(previous, quarter), turn(own, -quarter), turn(following, quarter))
+    mid_ref[:, : tall // 2, :] = before_ref[:, tall // 2 :, :]
+    mid_ref[:, tall // 2 : tall // 2 + tall, :] = here_ref[...]
+    mid_ref[:, tall // 2 + tall :, :] = after_ref[:, : tall // 2, :]
+    edges = slice(0, chip.edge_tiles)
+    previous = jnp.where(odd, got_before[edges], other_before[edges])
+    following = jnp.where(odd, got_after[edges], other_after[edges])
+    first = tall // 2
+    for ref, shifts in ((even_ref, ((0, 3), (2, 1))), (odd_ref, ((-1, 2), (1, 0)))):
+        one, two = (
+            jnp.where(lane < 2 * q, turned(previous, a * q), turned(following, b * q)) for a, b in shifts
+        )
+        ref[:, first : first + tall, :] = one[:channels]
+        ref[:, first + tall : first + 2 * tall, :] = two[:channels]
+        for c in range(channels):
+            outer = (two if c % 2 else one)[channels + c // 2]
+            ref[c, :first, :] = outer[first:]
+            ref[c, first + 2 * tall :, :] = outer[:first]
+    middle = (lane >= q) & (lane < 3 * q)
+    own = mid_ref[...]
+    even_rows = jnp.where(middle, turned(own, q), even_ref[:, pl.ds(shift, 2 * tall), :])
+    odd_rows = jnp.where(middle, turned(own, -q), odd_ref[:, pl.ds(shift, 2 * tall), :])
     for c in range(channels):
-        first = (channels + c) * rows
-        x_ref[pl.ds(first, 2 * tall, stride=2), :] = even_rows[c]
-        x_ref[pl.ds(first + 1, 2 * tall, stride=2), :] = odd_rows[c]
-    pieces = []
-    for d in range(5):
-        high, low = split(window_ref[d].reshape(channels * rows, cols))
-        pieces.append(jnp.concatenate([high, low], axis=0))
-    far = halves(dot(jnp.concatenate(pieces, axis=1), quarter_ref[...]))
-    x_ref[2 * channels * rows : 3 * channels * rows, :] = far
+        at = (channels + c) * rows
+        x_ref[pl.ds(at, 2 * tall, stride=2), :] = even_rows[c]
+        x_ref[pl.ds(at + 1, 2 * tall, stride=2), :] = odd_rows[c]
+    eighth = q // 2
+    starts = {-2: -eighth, -1: eighth, 0: 3 * eighth, 1: 5 * eighth, 2: 7 * eighth}
+    spans = {e: (e, first + (e + 1) * tall, slice(0, tall)) for e in (-1, 0, 1, 2)}
+    spans[-2] = (-2, 0, slice(first, tall))
+    spans[3] = (3, first + 4 * tall, slice(0, first))
+    for group in range(len(chip.shared)):
+        at = chip.quarter_tile(0, group)
+        at = slice(at, at + channels)
+        columns = {
+            -2: jnp.where(odd, other_before[at], got_before[at]),
+            -1: jnp.where(odd, got_before[at], other_before[at]),
+            0: mine_ref[at],
+            1: jnp.where(odd, got_after[at], other_after[at]),
+            2: jnp.where(odd, other_after[at], got_after[at]),
+        }
+        value = turned(columns[2], starts[2] - group % 4 * q)
+        for d in (1, 0, -1, -2):
+            value = jnp.where(lane < starts[d + 1], turned(columns[d], starts[d] - group % 4 * q), value)
+        for e, row, part in spans.values():
+            if chip.within(e) and chip.group(e) == group:
+                far_ref[:, row : row + part.stop - part.start, :] = value[:, part, :]
+    far = far_ref[:, pl.ds(shift, rows), :]
+    for c in range(channels):
+        x_ref[(2 * channels + c) * rows : (2 * channels + c + 1) * rows, :] = far[c]
     for c in range(3 * channels, padded):
         x_ref[c * rows : (c + 1) * rows, :] = jnp.zeros((rows, cols), F32)
 
@@ -442,8 +526,7 @@
         store_parts(band, grads)
     local_product(local_ref, back_two[...], hidden_pair, steps)
     modes = contract(parts_ref[...], wave_ref[...])
-    late[0].wait()
-    expanded(unmix(by_output, 1, modes), width)
+    expanded(unmix(by_input, 1, modes), width)
     for band in bands:
         grads = []
         for at, value in zip(columns, unfolded(band)):
@@ -453,7 +536,7 @@
 
     local_product(local_ref.at[:padded], back_one[...], hidden_pair, steps)
     modes = contract(parts_ref[...], wave_ref[...])
-    expanded(exact_dot(lift, unmix(by_output, 0, modes)), padded)
+    expanded(exact_dot(lift, unmix(by_input, 0, modes)), padded)
     for k in range(0, padded, 8):
         band = slice(k, k + 8)
         for i, (at, value) in enumerate(zip(columns, unfolded(band))):
@@ -464,69 +547,107 @@
 
     even_grads, odd_grads = [], []
     for c in range(channels):
-        first = (channels + c) * rows
-        even_grads.append(grad_x_ref[pl.ds(first, 2 * tall, stride=2), :][None])
-        odd_grads.append(grad_x_ref[pl.ds(first + 1, 2 * tall, stride=2), :][None])
+        at = (channels + c) * rows
+        even_grads.append(grad_x_ref[pl.ds(at, 2 * tall, stride=2), :][None])
+        odd_grads.append(grad_x_ref[pl.ds(at + 1, 2 * tall, stride=2), :][None])
     even_grads = jnp.concatenate(even_grads, axis=0)
     odd_grads = jnp.concatenate(odd_grads, axis=0)
-    even_up, even_down = turn(even_grads, quarter), turn(even_grads, -quarter)
-    odd_up, odd_down = turn(odd_grads, quarter), turn(odd_grads, -quarter)
-    zero = jnp.zeros_like(even_grads)
-
-    def four(a, b, c, d):
-        return jnp.where(lane < quarter, a, jnp.where(lane < half, b, jnp.where(lane < 3 * quarter, c, d)))
-
-    near = {
-        -1: four(zero, even_up, zero, odd_down),
-        0: four(even_down, even_down, odd_up, odd_up),
-        1: four(even_up, zero, odd_down, zero),
+    center_edge[...] = jnp.where(lane < 2 * q, turned(even_grads, -q), turned(odd_grads, q))
+    for ref, value in ((even_ref, even_grads), (odd_ref, odd_grads)):
+        ref[...] = jnp.zeros_like(ref)
+        ref[:, pl.ds(shift, 2 * tall), :] = value
+
+    def edge_tiles(shifts):
+        def pair(one, two):
+            return by_group([turned(v, k * q) for v, k in zip((*one, *two), shifts)], cols)
+
+        refs = (even_ref, odd_ref)
+        inner = pair(*([ref[:, first + k * tall : first + (k + 1) * tall, :] for ref in refs] for k in (0, 1)))
+        outer = [jnp.concatenate([ref[:, first + 2 * tall :, :], ref[:, :first, :]], axis=1) for ref in refs]
+        tiles = [inner]
+        for c in range(0, channels, 2):
+            other = min(c + 1, channels - 1)
+            tiles.append(pair([v[c] for v in outer], [v[other] for v in outer])[None])
+        return jnp.concatenate(tiles, axis=0)
+
+    near = {-1: edge_tiles((0, 1, 2, 3)), 1: edge_tiles((1, 2, 3, 0))}
+    for one, keep, give in ((-1, keep_a, give_a), (1, keep_b, give_b)):
+        zero = jnp.zeros_like(near[one])
+        keep[: chip.edge_tiles] = jnp.where(odd, near[one], zero)
+        give[: chip.edge_tiles] = jnp.where(odd, zero, near[one])
+    far_ref[...] = jnp.zeros_like(far_ref)
+    for c in range(channels):
+        at = (2 * channels + c) * rows
+        far_ref[c, pl.ds(shift, rows), :] = grad_x_ref[at : at + rows, :]
+    far_blocks[...] = jnp.zeros_like(far_blocks)
+    for e in (-1, 0, 1, 2, -2, 3):
+        if chip.within(e):
+            _, row, part = spans[e]
+            far_blocks[chip.group(e), :, part, :] += far_ref[:, row : row + part.stop - part.start, :]
+    for start in range(0, len(chip.shared), 4):
+        groups = [min(start + k, len(chip.shared) - 1) for k in range(4)]
+        at = chip.quarter_tile(0, start)
+        at = slice(at, at + channels)
+        tiles = {}
+        for d in range(-2, 3):
+            value = by_group([turned(far_blocks[g], k * q - starts[d]) for k, g in enumerate(groups)], cols)
+            if abs(d) == 2:
+                value = jnp.where((lane % q >= eighth) == (d < 0), value, 0.0)
+            tiles[d] = value
+        center_quarter[at.start - chip.edge_tiles : at.stop - chip.edge_tiles] = tiles[0]
+        for one, two, keep, give in ((-1, -2, keep_a, give_a), (1, 2, keep_b, give_b)):
+            keep[at] = jnp.where(odd, tiles[one], tiles[two])
+            give[at] = jnp.where(odd, tiles[two], tiles[one])
+
+
+def join_kernel(keep_b, keep_a, got_b, got_a, out_b, out_a):
+    out_b[...] = keep_b[...] + got_b[...]
+    out_a[...] = keep_a[...] + got_a[...]
+
+
+def gather_kernel(chip, core_ref, center_edge, center_quarter, from_before, from_after, *outs):
+    channels, _, cols = center_edge.shape
+    tall = from_after.shape[1]
+    q, first = cols // 4, tall // 2
+    odd = core_ref[0] == 1
+    sub = index_of((1, tall, cols), 1)
+    lane = index_of((1, 1, cols), 2)
+    edges = chip.edge_tiles
+    coarse = center_quarter[...] + from_after[edges:] + from_before[edges:]
+    rows = []
+    for group in range(len(chip.shared)):
+        at = chip.quarter_tile(0, group) - edges
+        value = jnp.where(lane // q == group % 4, coarse[at : at + channels], 0.0)
+        rows.append(value.reshape(channels * tall, cols))
+    shared = dot(beside(jnp.concatenate(rows, axis=0)), quarter_matrix(cols, flipped=True))
+    shared = shared.reshape(len(chip.shared), channels, tall, cols)
+    tail, head = from_after[:edges], from_before[:edges]
+
+    def unpaired(moves):
+        return by_group([turned(v, k * q) for v, k in zip((head, tail, head, tail), moves)], cols)
+
+    one, two = unpaired((0, 1, 1, 2)), unpaired((-2, -1, -1, 0))
+    outer = [(two if c % 2 else one)[channels + c // 2][None] for c in range(channels)]
+    outer = jnp.concatenate(outer, axis=0)
+    edge = {
+        0: one[:channels],
+        1: two[:channels],
+        2: jnp.where(sub < first, outer, 0.0),
+        -1: jnp.where(sub < first, 0.0, outer),
     }
-    late[1].wait()
-    high, low = split(grad_x_ref[2 * channels * rows : 3 * channels * rows, :])
-    spread = halves(dot(jnp.concatenate([high, low], axis=0), quarter_t_ref[...]))
-    for d in range(5):
-        window_ref[d] = spread[:, d * cols : (d + 1) * cols].reshape(channels, rows, cols)
-    for d in (-1, 0, 1):
-        window_ref[d + 2, :, tall : 3 * tall, :] += near[d]
-
-    def block_of(d, e):
-        if abs(e) < 2:
-            first = tall // 2 + (e + 1) * tall
-            return window_ref[d + 2, :, first : first + tall, :]
-        low_part = window_ref[d + 2, :, 4 * tall - tall // 2 :, :]
-        high_part = window_ref[d + 2, :, : tall // 2, :]
-        if not (ring.whole and ring.count == 4):
-            low_part, high_part = (low_part, jnp.zeros_like(low_part)) if e > 0 else (jnp.zeros_like(low_part), high_part)
-        return jnp.concatenate([low_part, high_part], axis=1)
-
-    reached = {}
-    for e in range(-2, 3):
-        reached[ring.place(e)] = e
-    for place in range(len(ring.offsets)):
-        if place not in reached:
-            for ref in (center_ref, keep_a, keep_b, give_a, give_b):
-                ref[place] = jnp.zeros((channels, tall, cols), F32)
-            continue
-        e = reached[place]
-        center_ref[place] = block_of(0, e)
-        for one, two, keep, give in ((-1, -2, keep_a, give_a), (1, 2, keep_b, give_b)):
-            near_block, far_block = block_of(one, e), block_of(two, e)
-            keep[place] = jnp.where(odd, near_block, far_block)
-            give[place] = jnp.where(odd, far_block, near_block)
-
-
-def join_kernel(ring, core_ref, keep_a, keep_b, got_a, got_b, out_a, out_b):
-    odd = core_ref[0] == 1
-    for offset in ring.offsets:
-        here = ring.place(offset)
-        there = jnp.where(odd, ring.place(offset + 1), ring.place(offset - 1))
-        out_a[here] = keep_a[here] + got_a[there]
-        out_b[here] = keep_b[here] + got_b[there]
-
-
-def gather_kernel(center_ref, a_ref, b_ref, *outs):
-    for place, out in enumerate(outs):
-        out[...] = center_ref[place] + a_ref[place] + b_ref[place]
+    shared = {e: shared[chip.group(e)] + edge[e] if e in edge else shared[chip.group(e)] for e in chip.shared}
+    if chip.ring:
+        shared[3] = shared[-1]
+    zero = jnp.zeros((channels, tall, cols), F32)
+    blank = zero[:, :first]
+    own = {
+        -1: jnp.concatenate([blank, center_edge[:, :first, :]], axis=1),
+        0: center_edge[:, first : first + tall, :],
+        1: jnp.concatenate([center_edge[:, first + tall :, :], blank], axis=1),
+    }
+    for out, e in zip(outs, chip.returned):
+        value = jnp.where(odd, shared.get(e + 1, zero), shared.get(e, zero))
+        out[...] = value + own[e] if e in own else value
 
 
 def final_kernel(own_ref, *refs):
@@ -535,7 +656,7 @@
     for ref in refs[1:-1]:
         total = total + ref[...]
     cols = total.shape[2]
-    spread = dot_t(total.reshape(-1, cols), pool_matrix(cols))
+    spread = dot(beside(total.reshape(-1, cols)), spread_matrix(cols))
     count = spread.shape[0]
     for k in range(4):
         part = spread[:, :cols] if k < 2 else spread[:, cols:]
@@ -585,8 +706,7 @@
     cells = rows * cols
     tall = rows // 4
     gx, gy = lax.axis_size("gx"), lax.axis_size("gy")
-    ring = Ring(gx)
-    blocks = len(ring.offsets)
+    chip = Chip(gx, channels)
     core = (lax.axis_index("gx") % 2).astype(jnp.int32).reshape(1)
 
     def shape(*dims, dtype=F32):
@@ -610,77 +730,80 @@
     packed = call(pool_kernel, shape(channels * tall, cols), flat_field, name="pool")
     packed = packed.reshape(channels, tall, cols)
 
-    held = [packed] + [along_x(packed, -offset) for offset in ring.offsets[1:]]
+    held = [packed] + [along_x(packed, -offset) for offset in chip.offsets[1:]]
     wave = wave_matrix(rows, cols)
     padded = -(-features // 16) * 16
     small = -(-channels // 8) * 8
-    quarter = quarter_matrix(cols)
-    constants = [jnp.asarray(quarter, BF16), wave_pair(wave, 1), wave_pair(wave.T, 0)]
+    constants = [wave_pair(wave, 1), wave_pair(wave.T, 0)]
     packed_weights = shape(layers, width, width, 2 * modes)
     prepared = list(call(
         prepare_kernel,
         [shape(*c.shape, dtype=BF16) for c in constants]
         + [
-            packed_weights, packed_weights, shape(padded, width), shape(width, padded), shape(width, 3 * padded, dtype=BF16),
+            packed_weights, shape(padded, width), shape(width, padded), shape(width, 3 * padded, dtype=BF16),
             shape(width, 3 * width, dtype=BF16), shape(width, 3 * width, dtype=BF16), shape(padded, 3 * width, dtype=BF16),
             shape(width, cells),
         ],
         cotangent.reshape(channels * rows, cols), lift, jnp.transpose(spectral, (0, 1, 3, 4, 2)), pointwise, project.T,
         *constants,
-        in_place=True, out_far=(4,),
+        in_place=True,
         scratch=(
             pltpu.VMEM((layers, 2, width, width, modes), F32),
-            pltpu.VMEM(packed_weights.shape, F32),
             pltpu.VMEM((small * rows, cols), F32),
             pltpu.VMEM((padded, width), F32),
             pltpu.VMEM((layers, width, width), F32),
             pltpu.VMEM((small, width), F32),
-            pltpu.SemaphoreType.DMA((7 + 2 * layers,)),
+            pltpu.SemaphoreType.DMA((6 + layers,)),
         ),
         limit=16 << 20,
         name="prepare",
     ))
-    by_output = prepared.pop(4)
-    quarter_t = jnp.asarray(quarter.T.copy(), BF16)
-    held = jnp.stack(held)
-    from_a = along_y(held, -2, -1)
-    from_b = along_y(held, 2, 1)
-    from_a, from_b, prepared[4] = lax.optimization_barrier((from_a, from_b, prepared[4]))
+    message = shape(chip.tiles, tall, cols)
+    to_previous, to_following = call(
+        functools.partial(pack_kernel, chip), (message, message), core, *held, scalars=1, name="pack"
+    )
+    from_a = along_y(to_previous, -2, -1)
+    from_b = along_y(to_following, 2, 1)
+    from_a, from_b, prepared[3] = lax.optimization_barrier((from_a, from_b, prepared[3]))
     swap_a, swap_b = swap(from_a), swap(from_b)
 
-    group = shape(blocks, channels, tall, cols)
     chunk = 4 * cols
-    own, center, keep_a, keep_b, give_a, give_b = call(
-        functools.partial(network_kernel, ring, chunk),
-        (shape(channels, rows, cols), group, group, group, group, group),
-        core, field.reshape(channels, rows, cols), held, from_a, from_b, swap_a, swap_b,
-        *(pltpu.with_memory_space_constraint(value, pltpu.HBM) for value in (quarter_t, by_output)), *prepared,
-        scalars=1, far=(7, 8),
+    quarter_part = shape(chip.tiles - chip.edge_tiles, tall, cols)
+    own, center_edge, center_quarter, keep_a, keep_b, give_a, give_b = call(
+        functools.partial(network_kernel, chip, chunk),
+        (shape(channels, rows, cols), shape(channels, 2 * tall, cols), quarter_part, message, message, message, message),
+        core, field.reshape(channels, rows, cols), held[0], held[chip.place(1)], held[chip.place(-1)],
+        to_previous, from_a, from_b, swap_a, swap_b, *prepared,
+        scalars=1,
         scratch=(
             pltpu.VMEM((padded * rows, cols), F32),
-            pltpu.VMEM((5, channels, rows, cols), F32),
+            pltpu.VMEM((channels, 3 * tall, cols), F32),
+            pltpu.VMEM((channels, 3 * tall, cols), F32),
+            pltpu.VMEM((channels, 2 * tall, cols), F32),
+            pltpu.VMEM((channels, rows + tall, cols), F32),
+            pltpu.VMEM((len(chip.shared), channels, tall, cols), F32),
             pltpu.VMEM((2 * padded, cells), BF16),
             pltpu.VMEM((2 * width, cells), BF16),
             pltpu.VMEM((width, cells), F32),
             pltpu.VMEM((width, cells), F32),
             pltpu.VMEM((padded * rows, cols), F32),
             pltpu.VMEM((width, wave.shape[0]), F32),
-            pltpu.VMEM(quarter_t.shape, BF16),
-            pltpu.VMEM(packed_weights.shape, F32),
-            pltpu.SemaphoreType.DMA((2,)),
         ),
         limit=16 << 20,
         name="network",
     )
 
     got_a, got_b = swap(give_a), swap(give_b)
-    sum_a, sum_b = call(
-        functools.partial(join_kernel, ring), (group, group), core, keep_a, keep_b, got_a, got_b, scalars=1, name="join"
+    sum_b, sum_a = call(join_kernel, (message, message), keep_b, keep_a, got_b, got_a, name="join")
+    sum_b = along_y(sum_b, 2, 1)
+    sum_a = along_y(sum_a, -2, -1)
+    parts = call(
+        functools.partial(gather_kernel, chip),
+        [shape(channels, tall, cols)] * len(chip.offsets),
+        core, center_edge, center_quarter, sum_b, sum_a, scalars=1,
+        name="gather",
     )
-    sum_a, sum_b = along_y(sum_a, -2, -1), along_y(sum_b, 2, 1)
-    piece = shape(channels, tall, cols)
-    parts = call(gather_kernel, [piece] * blocks, center, sum_a, sum_b, name="gather")
-    parts = [parts[0]] + [along_x(part, offset) for part, offset in zip(parts[1:], ring.offsets[1:])]
+    parts = [parts[0]] + [along_x(part, offset) for part, offset in zip(parts[1:], chip.returned[1:])]
     out = call(
         final_kernel,
         shape(channels * rows, cols),

time: 38.8 us -> 34.7 us (0.89)
  waiting for transfers between devices: 12.3 us -> 7.71 us
  starting transfers between devices: 15.4 us -> 17.3 us
  Pallas kernels: 10.1 us -> 8.65 us
    ppermute x4, waiting for transfers between devices: 6.29 us -> 2.71 us  [along_y(): return lax.ppermute(value, ('gx', 'gy'), pairs)]
    ppermute x4, starting transfers between devices: 5.99 us -> 7.75 us  [along_y(): return lax.ppermute(value, ('gx', 'gy'), pairs)]
    pallas_call x6 -> x7, Pallas kernels: 10.1 us -> 8.65 us  [call(): pl.pallas_call(kernel, out_shape=outs, in_specs=places, out_specs=out_pla...]
    ppermute x6, waiting for transfers between devices: 3.84 us -> 2.96 us  [along_x(): return lax.ppermute(value, 'gx', [(s, (s + steps) % gx) for s in range(gx)])]
    ppermute x6, starting transfers between devices: 7.53 us -> 8.13 us  [along_x(): return lax.ppermute(value, 'gx', [(s, (s + steps) % gx) for s in range(gx)])]
    ppermute x4, starting transfers between devices: 1.87 us -> 1.4 us  [swap(): return lax.ppermute(value, 'gx', [(s, s ^ 1) for s in range(gx)])]
  transfers between devices with their start and end apart: 14 -> 14, of which waited for: 11 -> 9; matrix products, arithmetic and copies ran while one was open for 0% -> 0% of each run, Pallas kernels for 9% -> 7%
where the time goes in v2:
time: 34.7 us; the launch traced here: 34.6 us
  starting transfers between devices  17.3 us (50%)
  Pallas kernels  8.65 us (25%)
  waiting for transfers between devices  7.71 us (22%)
  local copies, waits for them, and re-layouts  0.89 us (3%)
    pallas_call x7, Pallas kernels, call(): pl.pallas_call(kernel, out_shape=outs, in_specs=places, out_specs=out_pla...  8.65 us
    ppermute x6, starting transfers between devices, along_x(): return lax.ppermute(value, 'gx', [(s, (s + steps) % gx) for s in range(gx)])  8.13 us
    ppermute x4, starting transfers between devices, along_y(): return lax.ppermute(value, ('gx', 'gy'), pairs)  7.75 us
    ppermute x6, waiting for transfers between devices, along_x(): return lax.ppermute(value, 'gx', [(s, (s + steps) % gx) for s in range(gx)])  2.96 us
    ppermute x4, waiting for transfers between devices, along_y(): return lax.ppermute(value, ('gx', 'gy'), pairs)  2.71 us
    ppermute x4, waiting for transfers between devices, swap(): return lax.ppermute(value, 'gx', [(s, s ^ 1) for s in range(gx)])  2.04 us
    ppermute x4, starting transfers between devices, swap(): return lax.ppermute(value, 'gx', [(s, s ^ 1) for s in range(gx)])  1.4 us
    unnamed x4, local copies, waits for them, and re-layouts  0.89 us
  transfers between devices with their start and end apart: 14, of which 9 were waited for; matrix products, arithmetic and copies ran while one was open for 0% of the time, Pallas kernels for 7%

profile of v2, /device:TPU:0, one launch (start us, length us, event | category | flops | bytes accessed | tf_op | source)
XLA Modules:
  0.0 34.6 jit_solution(1839698777211362297)
XLA Ops:
  0.0 0.9 %copy-done = f32[5,1,32,128]{3,2,1,0:T(8,128)S(1)} copy-done((f32[5,1,32,128]{3,2,1,0:T(8,128)S(1)}, f32[5,1,32,128]{3,2,1,0:T(8,128)}, u32[]{:S(2)}) %copy-start) | copy-done | bytes 81944
  0.9 0.1 pool.1
  1.0 3.0 %collective-permute-start.2 = (f32[5,8,128]{2,1,0:T(8,128)S(1)}, f32[5,8,128]{2,1,0:T(8,128)S(1)}, u32[]{:S(2)}, u32[]{:S(2)}) collective-permute-start(f32[5,8,128]{2,1,0:T(8,128)S(1)} %bitcast.13), channel_id=1, source_target_pairs={{0,16},{8,24},{16,0},{24,8},{1,17},{9,25},{17,1},{25,9},{2,18},{10... | collective-permute-start | bytes 61448 | tf_op jit(solution)/shard_map/ppermute | solution.py:716
  4.1 1.7 %collective-permute-start = (f32[5,8,128]{2,1,0:T(8,128)S(1)}, f32[5,8,128]{2,1,0:T(8,128)S(1)}, u32[]{:S(2)}, u32[]{:S(2)}) collective-permute-start(f32[5,8,128]{2,1,0:T(8,128)S(1)} %bitcast.15), channel_id=1, source_target_pairs={{0,24},{8,0},{16,8},{24,16},{1,25},{9,1},{17,9},{25,17},{2,26},{10... | collective-permute-start | bytes 61448 | tf_op jit(solution)/shard_map/ppermute | solution.py:716
  5.8 0.0 collective-permute-done.2.refs_3_
  5.8 1.4 %collective-permute-done.1.refs_1_.before_ref = f32[5,8,128]{2,1,0:T(8,128)S(1)} collective-permute-done((f32[5,8,128]{2,1,0:T(8,128)S(1)}, f32[5,8,128]{2,1,0:T(8,128)S(1)}, u32[]{:S(2)}, u32[]{:S(2)}) %collective-permute-start.1) | collective-permute-done | bytes 20512 | tf_op jit(solution)/shard_map/ppermute | solution.py:716
  7.3 0.0 collective-permute-done.refs_2_.after_ref
  7.3 0.2 pack.1
  7.5 1.6 %collective-permute-start.4 = (f32[13,8,128]{2,1,0:T(8,128)S(1)}, f32[13,8,128]{2,1,0:T(8,128)S(1)}, u32[]{:S(2)}, u32[]{:S(2)}) collective-permute-start(f32[13,8,128]{2,1,0:T(8,128)S(1)} %get-tuple-element.34), channel_id=1, source_target_pairs={{0,2},{1,3},{2,4},{3,5},{4,6},{5,7},{6,0},{7,1},{8,9},{9,10},{10,1... | collective-permute-start | bytes 159752 | tf_op jit(solution)/shard_map/ppermute | solution.py:724
  9.1 2.2 %collective-permute-start.3 = (f32[13,8,128]{2,1,0:T(8,128)S(1)}, f32[13,8,128]{2,1,0:T(8,128)S(1)}, u32[]{:S(2)}, u32[]{:S(2)}) collective-permute-start(f32[13,8,128]{2,1,0:T(8,128)S(1)} %get-tuple-element.33.mine_ref), channel_id=1, source_target_pairs={{0,6},{1,7},{2,0},{3,1},{4,2},{5,3},{6,4},{7,5},{8,15},{9,8},{10,9... | collective-permute-start | bytes 159752 | tf_op jit(solution)/shard_map/ppermute | solution.py:724
  11.4 2.3 %prepare.1 = (bf16[1152,256]{1,0:T(8,128)(2,1)S(1)}, bf16[256,1152]{1,0:T(8,128)(2,1)S(1)}, f32[2,32,32,128]{3,2,1,0:T(8,128)S(1)}, f32[16,32]{1,0:T(8,128)S(1)}...) custom-call(f32[160,128]{1,0:T(8,128)} %bitcast.20, ...), custom_call_target="tpu_custom_call" | custom-call | tf_op jit(solution)/shard_map/prepare/pallas_call | solution.py:688
  13.6 0.5 %collective-permute-done.3.got_after = f32[13,8,128]{2,1,0:T(8,128)S(1)} collective-permute-done((f32[13,8,128]{2,1,0:T(8,128)S(1)}, f32[13,8,128]{2,1,0:T(8,128)S(1)}, u32[]{:S(2)}, u32[]{:S(2)}) %collective-permute-start.3) | collective-permute-done | bytes 53280 | tf_op jit(solution)/shard_map/ppermute | solution.py:724
  14.1 0.7 %collective-permute-start.5 = (f32[13,8,128]{2,1,0:T(8,128)S(1)}, f32[13,8,128]{2,1,0:T(8,128)S(1)}, u32[]{:S(2)}, u32[]{:S(2)}) collective-permute-start(f32[13,8,128]{2,1,0:T(8,128)S(1)} %collective-permute-done.3.got_after), channel_id=1, source_target_pairs={{0,8},{8,0},{16,24},{24,16},{1,9},{9,1},{17,25},{25,17},{2,10},{10... | collective-permute-start | bytes 159752 | tf_op jit(solution)/shard_map/ppermute | solution.py:727
  14.9 0.1 collective-permute-start.6
  14.9 0.8 %collective-permute-done.5.other_after = f32[13,8,128]{2,1,0:T(8,128)S(1)} collective-permute-done((f32[13,8,128]{2,1,0:T(8,128)S(1)}, f32[13,8,128]{2,1,0:T(8,128)S(1)}, u32[]{:S(2)}, u32[]{:S(2)}) %collective-permute-start.5) | collective-permute-done | bytes 53280 | tf_op jit(solution)/shard_map/ppermute | solution.py:727
  15.7 0.3 %collective-permute-done.6.other_before = f32[13,8,128]{2,1,0:T(8,128)S(1)} collective-permute-done((f32[13,8,128]{2,1,0:T(8,128)S(1)}, f32[13,8,128]{2,1,0:T(8,128)S(1)}, u32[]{:S(2)}, u32[]{:S(2)}) %collective-permute-start.6) | collective-permute-done | bytes 53280 | tf_op jit(solution)/shard_map/ppermute | solution.py:727
  16.1 5.1 %network.1 = (f32[5,32,128]{2,1,0:T(8,128)S(1)}, f32[5,16,128]{2,1,0:T(8,128)S(1)}, f32[5,8,128]{2,1,0:T(8,128)S(1)}, f32[13,8,128]{2,1,0:T(8,128)S(1)}, f32[13,...) custom-call(s32[1]{0:T(128)} %bitcast.core_ref, f32[5,32,128]{2,1,0:T(8,128)S(1)} %bitcast.12, ...), custom_call_target="tpu_custom_call" | custom-call | tf_op jit(solution)/shard_map/network/pallas_call | solution.py:688
  21.2 0.2 collective-permute-start.7
  21.4 0.4 %collective-permute-start.8 = (f32[13,8,128]{2,1,0:T(8,128)S(1)}, f32[13,8,128]{2,1,0:T(8,128)S(1)}, u32[]{:S(2)}, u32[]{:S(2)}) collective-permute-start(f32[13,8,128]{2,1,0:T(8,128)S(1)} %get-tuple-element.54), channel_id=1, source_target_pairs={{0,8},{8,0},{16,24},{24,16},{1,9},{9,1},{17,25},{25,17},{2,10},{10... | collective-permute-start | bytes 159752 | tf_op jit(solution)/shard_map/ppermute | solution.py:727
  21.8 0.7 %collective-permute-done.7.got_b = f32[13,8,128]{2,1,0:T(8,128)S(1)} collective-permute-done((f32[13,8,128]{2,1,0:T(8,128)S(1)}, f32[13,8,128]{2,1,0:T(8,128)S(1)}, u32[]{:S(2)}, u32[]{:S(2)}) %collective-permute-start.7) | collective-permute-done | bytes 53280 | tf_op jit(solution)/shard_map/ppermute | solution.py:727
  22.5 0.2 collective-permute-done.8.got_a
  22.7 0.6 %collective-permute-start.9 = (f32[13,8,128]{2,1,0:T(8,128)S(1)}, f32[13,8,128]{2,1,0:T(8,128)S(1)}, u32[]{:S(2)}, u32[]{:S(2)}) collective-permute-start(f32[13,8,128]{2,1,0:T(8,128)S(1)} %get-tuple-element.55), channel_id=1, source_target_pairs={{0,2},{1,3},{2,4},{3,5},{4,6},{5,7},{6,0},{7,1},{8,9},{9,10},{10,1... | collective-permute-start | bytes 159752 | tf_op jit(solution)/shard_map/ppermute | solution.py:724
  23.3 3.2 %collective-permute-start.10 = (f32[13,8,128]{2,1,0:T(8,128)S(1)}, f32[13,8,128]{2,1,0:T(8,128)S(1)}, u32[]{:S(2)}, u32[]{:S(2)}) collective-permute-start(f32[13,8,128]{2,1,0:T(8,128)S(1)} %get-tuple-element.56), channel_id=1, source_target_pairs={{0,6},{1,7},{2,0},{3,1},{4,2},{5,3},{6,4},{7,5},{8,15},{9,8},{10,9... | collective-permute-start | bytes 159752 | tf_op jit(solution)/shard_map/ppermute | solution.py:724
  26.6 2.2 %collective-permute-done.9.from_before = f32[13,8,128]{2,1,0:T(8,128)S(1)} collective-permute-done((f32[13,8,128]{2,1,0:T(8,128)S(1)}, f32[13,8,128]{2,1,0:T(8,128)S(1)}, u32[]{:S(2)}, u32[]{:S(2)}) %collective-permute-start.9) | collective-permute-done | bytes 53280 | tf_op jit(solution)/shard_map/ppermute | solution.py:724
  28.8 0.0 collective-permute-done.10.from_after
  28.8 0.2 gather.1
  29.0 0.2 collective-permute-start.11
  29.1 1.8 %collective-permute-start.12 = (f32[5,8,128]{2,1,0:T(8,128)S(1)}, f32[5,8,128]{2,1,0:T(8,128)S(1)}, u32[]{:S(2)}, u32[]{:S(2)}) collective-permute-start(f32[5,8,128]{2,1,0:T(8,128)S(1)} %get-tuple-element.59), channel_id=1, source_target_pairs={{0,16},{8,24},{16,0},{24,8},{1,17},{9,25},{17,1},{25,9},{2,18},{10... | collective-permute-start | bytes 61448 | tf_op jit(solution)/shard_map/ppermute | solution.py:716
  31.0 1.4 %collective-permute-start.13 = (f32[5,8,128]{2,1,0:T(8,128)S(1)}, f32[5,8,128]{2,1,0:T(8,128)S(1)}, u32[]{:S(2)}, u32[]{:S(2)}) collective-permute-start(f32[5,8,128]{2,1,0:T(8,128)S(1)} %get-tuple-element.60), channel_id=1, source_target_pairs={{0,24},{8,0},{16,8},{24,16},{1,25},{9,1},{17,9},{25,17},{2,26},{10... | collective-permute-start | bytes 61448 | tf_op jit(solution)/shard_map/ppermute | solution.py:716
  32.3 0.6 %collective-permute-done.12.refs_2_ = f32[5,8,128]{2,1,0:T(8,128)S(1)} collective-permute-done((f32[5,8,128]{2,1,0:T(8,128)S(1)}, f32[5,8,128]{2,1,0:T(8,128)S(1)}, u32[]{:S(2)}, u32[]{:S(2)}) %collective-permute-start.12) | collective-permute-done | bytes 20512 | tf_op jit(solution)/shard_map/ppermute | solution.py:716
  32.9 0.9 %collective-permute-done.13.refs_3_ = f32[5,8,128]{2,1,0:T(8,128)S(1)} collective-permute-done((f32[5,8,128]{2,1,0:T(8,128)S(1)}, f32[5,8,128]{2,1,0:T(8,128)S(1)}, u32[]{:S(2)}, u32[]{:S(2)}) %collective-permute-start.13) | collective-permute-done | bytes 20512 | tf_op jit(solution)/shard_map/ppermute | solution.py:716
  33.8 0.8 %final.1 = f32[160,128]{1,0:T(8,128)} custom-call(f32[160,128]{1,0:T(8,128)S(1)} %bitcast.18, f32[5,8,128]{2,1,0:T(8,128)S(1)} %get-tuple-element.57.refs_0_, f32[5,8,128]{2,1,0:T(8,128)S(1)} %collective-permute-done.11.refs_1_, f32[5,8,128]{2,1,0:T(8,128)S(1)} %collective-permute-done.12.refs_2_, f32[5,8,128]{2,1,0:T(8,128)S(1)} %collective-permute-done.13.refs_3_), custom_call_target="tpu_custom_call" | custom-call | tf_op jit(solution)/shard_map/final/pallas_call | solution.py:688
  (7 shorter events, 0.0 us)
Async XLA Ops:
  0.0 0.9 %copy-start = (f32[5,1,32,128]{3,2,1,0:T(8,128)S(1)}, f32[5,1,32,128]{3,2,1,0:T(8,128)}, u32[]{:S(2)}) copy-start(f32[5,1,32,128]{3,2,1,0:T(8,128)} %param.8) | copy-start | bytes 245764
  0.9 15.2 %copy-start.1 = (f32[5,1,32,128]{3,2,1,0:T(8,128)S(1)}, f32[5,1,32,128]{3,2,1,0:T(8,128)}, u32[]{:S(2)}) copy-start(f32[5,1,32,128]{3,2,1,0:T(8,128)} %param.8) | copy-start | bytes 245764
  1.0 4.8 %collective-permute-start.2 = (f32[5,8,128]{2,1,0:T(8,128)S(1)}, f32[5,8,128]{2,1,0:T(8,128)S(1)}, u32[]{:S(2)}, u32[]{:S(2)}) collective-permute-start(f32[5,8,128]{2,1,0:T(8,128)S(1)} %bitcast.13), channel_id=1, source_target_pairs={{0,16},{8,24},{16,0},{24,8},{1,17},{9,25},{17,1},{25,9},{2,18},{10... | collective-permute-start | bytes 61448 | tf_op jit(solution)/shard_map/ppermute | solution.py:716
  4.1 3.2 %collective-permute-start.1 = (f32[5,8,128]{2,1,0:T(8,128)S(1)}, f32[5,8,128]{2,1,0:T(8,128)S(1)}, u32[]{:S(2)}, u32[]{:S(2)}) collective-permute-start(f32[5,8,128]{2,1,0:T(8,128)S(1)} %bitcast.14), channel_id=1, source_target_pairs={{0,8},{8,16},{16,24},{24,0},{1,9},{9,17},{17,25},{25,1},{2,10},{10... | collective-permute-start | bytes 61448 | tf_op jit(solution)/shard_map/ppermute | solution.py:716
  4.1 3.2 %collective-permute-start = (f32[5,8,128]{2,1,0:T(8,128)S(1)}, f32[5,8,128]{2,1,0:T(8,128)S(1)}, u32[]{:S(2)}, u32[]{:S(2)}) collective-permute-start(f32[5,8,128]{2,1,0:T(8,128)S(1)} %bitcast.15), channel_id=1, source_target_pairs={{0,24},{8,0},{16,8},{24,16},{1,25},{9,1},{17,9},{25,17},{2,26},{10... | collective-permute-start | bytes 61448 | tf_op jit(solution)/shard_map/ppermute | solution.py:716
  7.5 6.1 %collective-permute-start.4 = (f32[13,8,128]{2,1,0:T(8,128)S(1)}, f32[13,8,128]{2,1,0:T(8,128)S(1)}, u32[]{:S(2)}, u32[]{:S(2)}) collective-permute-start(f32[13,8,128]{2,1,0:T(8,128)S(1)} %get-tuple-element.34), channel_id=1, source_target_pairs={{0,2},{1,3},{2,4},{3,5},{4,6},{5,7},{6,0},{7,1},{8,9},{9,10},{10,1... | collective-permute-start | bytes 159752 | tf_op jit(solution)/shard_map/ppermute | solution.py:724
  9.1 5.0 %collective-permute-start.3 = (f32[13,8,128]{2,1,0:T(8,128)S(1)}, f32[13,8,128]{2,1,0:T(8,128)S(1)}, u32[]{:S(2)}, u32[]{:S(2)}) collective-permute-start(f32[13,8,128]{2,1,0:T(8,128)S(1)} %get-tuple-element.33.mine_ref), channel_id=1, source_target_pairs={{0,6},{1,7},{2,0},{3,1},{4,2},{5,3},{6,4},{7,5},{8,15},{9,8},{10,9... | collective-permute-start | bytes 159752 | tf_op jit(solution)/shard_map/ppermute | solution.py:724
  14.1 1.6 %collective-permute-start.5 = (f32[13,8,128]{2,1,0:T(8,128)S(1)}, f32[13,8,128]{2,1,0:T(8,128)S(1)}, u32[]{:S(2)}, u32[]{:S(2)}) collective-permute-start(f32[13,8,128]{2,1,0:T(8,128)S(1)} %collective-permute-done.3.got_after), channel_id=1, source_target_pairs={{0,8},{8,0},{16,24},{24,16},{1,9},{9,1},{17,25},{25,17},{2,10},{10... | collective-permute-start | bytes 159752 | tf_op jit(solution)/shard_map/ppermute | solution.py:727
  14.9 1.2 %collective-permute-start.6 = (f32[13,8,128]{2,1,0:T(8,128)S(1)}, f32[13,8,128]{2,1,0:T(8,128)S(1)}, u32[]{:S(2)}, u32[]{:S(2)}) collective-permute-start(f32[13,8,128]{2,1,0:T(8,128)S(1)} %collective-permute-done.4.got_before), channel_id=1, source_target_pairs={{0,8},{8,0},{16,24},{24,16},{1,9},{9,1},{17,25},{25,17},{2,10},{10... | collective-permute-start | bytes 159752 | tf_op jit(solution)/shard_map/ppermute | solution.py:727
  21.2 1.3 %collective-permute-start.7 = (f32[13,8,128]{2,1,0:T(8,128)S(1)}, f32[13,8,128]{2,1,0:T(8,128)S(1)}, u32[]{:S(2)}, u32[]{:S(2)}) collective-permute-start(f32[13,8,128]{2,1,0:T(8,128)S(1)} %get-tuple-element.53), channel_id=1, source_target_pairs={{0,8},{8,0},{16,24},{24,16},{1,9},{9,1},{17,25},{25,17},{2,10},{10... | collective-permute-start | bytes 159752 | tf_op jit(solution)/shard_map/ppermute | solution.py:727
  21.4 1.2 %collective-permute-start.8 = (f32[13,8,128]{2,1,0:T(8,128)S(1)}, f32[13,8,128]{2,1,0:T(8,128)S(1)}, u32[]{:S(2)}, u32[]{:S(2)}) collective-permute-start(f32[13,8,128]{2,1,0:T(8,128)S(1)} %get-tuple-element.54), channel_id=1, source_target_pairs={{0,8},{8,0},{16,24},{24,16},{1,9},{9,1},{17,25},{25,17},{2,10},{10... | collective-permute-start | bytes 159752 | tf_op jit(solution)/shard_map/ppermute | solution.py:727
  22.7 6.1 %collective-permute-start.9 = (f32[13,8,128]{2,1,0:T(8,128)S(1)}, f32[13,8,128]{2,1,0:T(8,128)S(1)}, u32[]{:S(2)}, u32[]{:S(2)}) collective-permute-start(f32[13,8,128]{2,1,0:T(8,128)S(1)} %get-tuple-element.55), channel_id=1, source_target_pairs={{0,2},{1,3},{2,4},{3,5},{4,6},{5,7},{6,0},{7,1},{8,9},{9,10},{10,1... | collective-permute-start | bytes 159752 | tf_op jit(solution)/shard_map/ppermute | solution.py:724
  23.3 5.5 %collective-permute-start.10 = (f32[13,8,128]{2,1,0:T(8,128)S(1)}, f32[13,8,128]{2,1,0:T(8,128)S(1)}, u32[]{:S(2)}, u32[]{:S(2)}) collective-permute-start(f32[13,8,128]{2,1,0:T(8,128)S(1)} %get-tuple-element.56), channel_id=1, source_target_pairs={{0,6},{1,7},{2,0},{3,1},{4,2},{5,3},{6,4},{7,5},{8,15},{9,8},{10,9... | collective-permute-start | bytes 159752 | tf_op jit(solution)/shard_map/ppermute | solution.py:724
  29.0 3.4 %collective-permute-start.11 = (f32[5,8,128]{2,1,0:T(8,128)S(1)}, f32[5,8,128]{2,1,0:T(8,128)S(1)}, u32[]{:S(2)}, u32[]{:S(2)}) collective-permute-start(f32[5,8,128]{2,1,0:T(8,128)S(1)} %get-tuple-element.58), channel_id=1, source_target_pairs={{0,8},{8,16},{16,24},{24,0},{1,9},{9,17},{17,25},{25,1},{2,10},{10... | collective-permute-start | bytes 61448 | tf_op jit(solution)/shard_map/ppermute | solution.py:716
  29.1 3.8 %collective-permute-start.12 = (f32[5,8,128]{2,1,0:T(8,128)S(1)}, f32[5,8,128]{2,1,0:T(8,128)S(1)}, u32[]{:S(2)}, u32[]{:S(2)}) collective-permute-start(f32[5,8,128]{2,1,0:T(8,128)S(1)} %get-tuple-element.59), channel_id=1, source_target_pairs={{0,16},{8,24},{16,0},{24,8},{1,17},{9,25},{17,1},{25,9},{2,18},{10... | collective-permute-start | bytes 61448 | tf_op jit(solution)/shard_map/ppermute | solution.py:716
  31.0 2.8 %collective-permute-start.13 = (f32[5,8,128]{2,1,0:T(8,128)S(1)}, f32[5,8,128]{2,1,0:T(8,128)S(1)}, u32[]{:S(2)}, u32[]{:S(2)}) collective-permute-start(f32[5,8,128]{2,1,0:T(8,128)S(1)} %get-tuple-element.60), channel_id=1, source_target_pairs={{0,24},{8,0},{16,8},{24,16},{1,25},{9,1},{17,9},{25,17},{2,26},{10... | collective-permute-start | bytes 61448 | tf_op jit(solution)/shard_map/ppermute | solution.py:716

commit v3 on v2

--- a/solution.py
+++ b/solution.py
@@ -18,15 +18,26 @@
 
 class Chip:
     def __init__(self, count, channels):
+        self.count = count
         self.ring = count == 4
-        self.offsets = [0, -1, 1, 2] if self.ring else [0, -1, 1, 2, -2, 3, -3]
-        self.returned = [0, 1, 2, -1] if self.ring else [0, 1, 2, 3, -3, -2, -1]
+        if self.ring:
+            self.slots = [(0, 0), (1, -1), (2, 2), (-1, 1)]
+        else:
+            self.slots = [(k, k) for k in (0, 1, 2, -1, -2, 3, -3)]
         self.shared = [0, 1, 2, -1] if self.ring else [-2, -1, 0, 1, 2, 3]
         self.edge_tiles = channels + (channels + 1) // 2
         self.tiles = self.edge_tiles + channels * -(-len(self.shared) // 4)
 
-    def place(self, offset):
-        return self.offsets.index((offset + 1) % 4 - 1 if self.ring else offset)
+    def place(self, offset, odd):
+        offset = (offset + 1) % 4 - 1 if self.ring else offset
+        return [slot[odd] for slot in self.slots].index(offset)
+
+    def pairs(self, slot, back=False):
+        count = self.count
+        if self.ring:
+            return [(s, s ^ slot) for s in range(count)]
+        steps = self.slots[slot][0] if back else -self.slots[slot][0]
+        return [(s, (s + steps) % count) for s in range(count)]
 
     def group(self, offset):
         return offset % 4 if self.ring else self.shared.index(offset)
@@ -199,13 +210,13 @@
     small, cols = project_ref.shape[0], target_ref.shape[1]
     rows = target_ref.shape[0] // small
     channels, features = project_hbm.shape[0], lift_hbm.shape[0]
-    pairs = [(spectral_hbm.at[layer], spectral_ref.at[layer]) for layer in range(layers)]
-    pairs += [
+    pairs = [
         (cotangent_hbm, target_ref.at[: channels * rows]),
         (project_hbm, project_ref.at[:channels]),
         (lift_hbm, lift_in.at[:features]),
         (pointwise_hbm, pointwise_ref),
     ]
+    pairs += [(spectral_hbm.at[layer], spectral_ref.at[layer]) for layer in range(layers)]
     pairs += list(zip(constants_hbm, constants))
     copies = [pltpu.make_async_copy(source, target, sems.at[k]) for k, (source, target) in enumerate(pairs)]
     for copy in copies:
@@ -213,12 +224,7 @@
     target_ref[channels * rows :, :] = jnp.zeros(((small - channels) * rows, cols), F32)
     project_ref[channels:, :] = jnp.zeros((small - channels, width), F32)
     lift_in[features:, :] = jnp.zeros((lift_in.shape[0] - features, width), F32)
-    for layer in range(layers):
-        copies[layer].wait()
-        for w in range(width):
-            both = [spectral_ref[layer, part, w] for part in range(2)]
-            by_input[layer, w] = jnp.concatenate(both, axis=1)
-    for copy in copies[layers : layers + 4]:
+    for copy in copies[:4]:
         copy.wait()
 
     lift = lift_in[...]
@@ -239,6 +245,11 @@
             pieces.append(jnp.concatenate([high, value - high, high], axis=0).astype(BF16))
         target_grad[:, first * cols : (first + group) * cols] = dot(out, jnp.concatenate(pieces, axis=1))
 
+    for layer in range(layers):
+        copies[4 + layer].wait()
+        for w in range(width):
+            both = [spectral_ref[layer, part, w] for part in range(2)]
+            by_input[layer, w] = jnp.concatenate(both, axis=1)
     for copy in copies[4 + layers :]:
         copy.wait()
 
@@ -297,14 +308,14 @@
 
 
 def pack_kernel(chip, core_ref, *refs):
-    blocks, (to_previous, to_following) = refs[: len(chip.offsets)], refs[len(chip.offsets) :]
+    blocks, (to_previous, to_following) = refs[: len(chip.slots)], refs[len(chip.slots) :]
     channels, tall, cols = blocks[0].shape
     q = cols // 4
     odd = core_ref[0] == 1
     sub = index_of((1, tall, cols), 1)
     shared = {}
     for e in chip.shared:
-        even_at, odd_at = chip.place(e), (chip.place(e - 1))
+        even_at, odd_at = chip.place(e, 0), chip.place(e - 1, 1)
         shared[e] = jnp.where(odd, blocks[odd_at][...], blocks[even_at][...])
     stacked_rows = jnp.concatenate([shared[e].reshape(channels * tall, cols) for e in chip.shared], axis=0)
     coarse = dot(beside(stacked_rows), quarter_matrix(cols)).reshape(len(chip.shared), channels, tall, cols)
@@ -331,12 +342,12 @@
     lane = lax.broadcasted_iota(jnp.int32, (width, lanes), 1)
     swapped = pltpu.roll(coefficients, half, 1)
     signed = jnp.where(lane < half, coefficients, -coefficients)
-    total_real = jnp.zeros((width, lanes), F32)
-    total_imag = jnp.zeros((width, lanes), F32)
+    total_real, total_imag = [None] * 2, [None] * 2
     for w in range(width):
         block = weights[layer, w]
-        total_real += block * signed[w : w + 1]
-        total_imag += block * swapped[w : w + 1]
+        total_real[w % 2] = added(total_real[w % 2], block * signed[w : w + 1])
+        total_imag[w % 2] = added(total_imag[w % 2], block * swapped[w : w + 1])
+    total_real, total_imag = sum(total_real), sum(total_imag)
     total_real += pltpu.roll(total_real, half, 1)
     total_imag += pltpu.roll(total_imag, half, 1)
     return jnp.where(lane < half, total_real, total_imag)
@@ -404,7 +415,7 @@
 
 def network_kernel(
     chip, chunk,
-    core_ref, field_ref, here_ref, after_ref, before_ref, mine_ref, got_after, got_before, other_after, other_before,
+    core_ref, field_ref, here_ref, next_ref, last_ref, mine_ref, got_after, got_before, other_after, other_before,
     wave_ref, wave_t_ref, by_input, lift_ref, lift_t_ref, local_one, local_two, back_two, back_one, target_grad,
     own_ref, center_edge, center_quarter, keep_a, keep_b, give_a, give_b,
     x_ref, even_ref, odd_ref, mid_ref, far_ref, far_blocks, feature_pair, hidden_pair, slope_one, local_ref, grad_x_ref, parts_ref,
@@ -420,9 +431,12 @@
     lane = index_of((1, 1, cols), 2)
     for c in range(channels):
         x_ref[c * rows : (c + 1) * rows, :] = field_ref[c]
-    mid_ref[:, : tall // 2, :] = before_ref[:, tall // 2 :, :]
+    before, after = last_ref[...], next_ref[...]
+    if chip.ring:
+        before, after = jnp.where(odd, after, before), jnp.where(odd, before, after)
+    mid_ref[:, : tall // 2, :] = before[:, tall // 2 :, :]
     mid_ref[:, tall // 2 : tall // 2 + tall, :] = here_ref[...]
-    mid_ref[:, tall // 2 + tall :, :] = after_ref[:, : tall // 2, :]
+    mid_ref[:, tall // 2 + tall :, :] = after[:, : tall // 2, :]
     edges = slice(0, chip.edge_tiles)
     previous = jnp.where(odd, got_before[edges], other_before[edges])
     following = jnp.where(odd, got_after[edges], other_after[edges])
@@ -474,7 +488,9 @@
 
     for i in range(rows):
         at = slice(i * cols, (i + 1) * cols)
-        high, low = split(x_ref[pl.ds(i, padded, stride=rows), :])
+        value = x_ref[pl.ds(i, padded, stride=rows), :]
+        local_ref[:padded, at] = value
+        high, low = split(value)
         feature_pair[:padded, at] = high
         feature_pair[padded:, at] = low
 
@@ -498,7 +514,7 @@
     bands = [slice(k, k + 8) for k in range(0, width, 8)]
 
     for k in range(0, padded, 8):
-        store_parts(slice(k, k + 8), [x_ref[pl.ds(k * rows + i, 8, stride=rows), :] for i in range(rows)])
+        store_parts(slice(k, k + 8), [local_ref[k : k + 8, at] for at in columns])
     local_product(local_ref, local_one[...], feature_pair, steps)
     modes = contract(parts_ref[:padded, :], wave_ref[...])
     expanded(mix(by_input, 0, exact_dot(lift_t, modes)), width)
@@ -645,9 +661,12 @@
         0: center_edge[:, first : first + tall, :],
         1: jnp.concatenate([center_edge[:, first + tall :, :], blank], axis=1),
     }
-    for out, e in zip(outs, chip.returned):
-        value = jnp.where(odd, shared.get(e + 1, zero), shared.get(e, zero))
-        out[...] = value + own[e] if e in own else value
+    def block_of(offset, is_odd):
+        value = shared.get(offset + is_odd, zero)
+        return value + own[offset] if offset in own else value
+
+    for out, (even_offset, odd_offset) in zip(outs, chip.slots):
+        out[...] = jnp.where(odd, block_of(odd_offset, 1), block_of(even_offset, 0))
 
 
 def final_kernel(own_ref, *refs):
@@ -712,9 +731,6 @@
     def shape(*dims, dtype=F32):
         return jax.ShapeDtypeStruct(dims, dtype)
 
-    def along_x(value, steps):
-        return lax.ppermute(value, "gx", [(s, (s + steps) % gx) for s in range(gx)])
-
     def along_y(value, even_steps, odd_steps):
         pairs = []
         for a in range(gx):
@@ -730,7 +746,8 @@
     packed = call(pool_kernel, shape(channels * tall, cols), flat_field, name="pool")
     packed = packed.reshape(channels, tall, cols)
 
-    held = [packed] + [along_x(packed, -offset) for offset in chip.offsets[1:]]
+    others = range(1, len(chip.slots))
+    held = [packed] + [lax.ppermute(packed, "gx", chip.pairs(slot)) for slot in others]
     wave = wave_matrix(rows, cols)
     padded = -(-features // 16) * 16
     small = -(-channels // 8) * 8
@@ -772,7 +789,7 @@
     own, center_edge, center_quarter, keep_a, keep_b, give_a, give_b = call(
         functools.partial(network_kernel, chip, chunk),
         (shape(channels, rows, cols), shape(channels, 2 * tall, cols), quarter_part, message, message, message, message),
-        core, field.reshape(channels, rows, cols), held[0], held[chip.place(1)], held[chip.place(-1)],
+        core, field.reshape(channels, rows, cols), held[0], held[chip.place(1, 0)], held[chip.place(-1, 0)],
         to_previous, from_a, from_b, swap_a, swap_b, *prepared,
         scalars=1,
         scratch=(
@@ -799,11 +816,11 @@
     sum_a = along_y(sum_a, -2, -1)
     parts = call(
         functools.partial(gather_kernel, chip),
-        [shape(channels, tall, cols)] * len(chip.offsets),
+        [shape(channels, tall, cols)] * len(chip.slots),
         core, center_edge, center_quarter, sum_b, sum_a, scalars=1,
         name="gather",
     )
-    parts = [parts[0]] + [along_x(part, offset) for part, offset in zip(parts[1:], chip.returned[1:])]
+    parts = [parts[0]] + [lax.ppermute(parts[slot], "gx", chip.pairs(slot, back=True)) for slot in others]
     out = call(
         final_kernel,
         shape(channels * rows, cols),

time: 34.7 us -> 33.6 us (0.968)
  starting transfers between devices: 17.3 us -> 14 us
  waiting for transfers between devices: 7.71 us -> 10.2 us
    ppermute x6, starting transfers between devices: 8.13 us -> 5.14 us  [the longest x3 3.23 us: body(): lax.ppermute(packed, 'gx', chip.pairs(slot))]
    ppermute x6, waiting for transfers between devices: 2.96 us -> 5.23 us  [the longest x3 3.02 us: body(): lax.ppermute(packed, 'gx', chip.pairs(slot))]
  transfers between devices with their start and end apart: 14 -> 14, of which waited for: 9 -> 12; matrix products, arithmetic and copies ran while one was open for 0% -> 0% of each run, Pallas kernels for 7% -> 6%
where the time goes in v3:
time: 33.6 us; the launch traced here: 33.5 us
  starting transfers between devices  14 us (42%)
  waiting for transfers between devices  10.2 us (30%)
  Pallas kernels  8.33 us (25%)
  local copies, waits for them, and re-layouts  0.89 us (3%)
    pallas_call x7, Pallas kernels, call(): pl.pallas_call(kernel, out_shape=outs, in_specs=places, out_specs=out_pla...  8.33 us
    ppermute x4, starting transfers between devices, along_y(): return lax.ppermute(value, ('gx', 'gy'), pairs)  7.75 us
    ppermute x3, starting transfers between devices, body(): lax.ppermute(packed, 'gx', chip.pairs(slot))  3.23 us
    ppermute x4, waiting for transfers between devices, along_y(): return lax.ppermute(value, ('gx', 'gy'), pairs)  3.02 us
    ppermute x3, waiting for transfers between devices, body(): lax.ppermute(packed, 'gx', chip.pairs(slot))  3.02 us
    ppermute x3, waiting for transfers between devices, body(): lax.ppermute(parts[slot], 'gx', chip.pairs(slot, back=True))  2.22 us
    ppermute x4, waiting for transfers between devices, swap(): return lax.ppermute(value, 'gx', [(s, s ^ 1) for s in range(gx)])  1.96 us
    ppermute x3, starting transfers between devices, body(): lax.ppermute(parts[slot], 'gx', chip.pairs(slot, back=True))  1.92 us
  transfers between devices with their start and end apart: 14, of which 12 were waited for; matrix products, arithmetic and copies ran while one was open for 0% of the time, Pallas kernels for 6%

profile of v3, /device:TPU:0, one launch (start us, length us, event | category | flops | bytes accessed | tf_op | source)
XLA Modules:
  0.0 33.5 jit_solution(13075749941785228651)
XLA Ops:
  0.0 0.9 %copy-done = f32[5,1,32,128]{3,2,1,0:T(8,128)S(1)} copy-done((f32[5,1,32,128]{3,2,1,0:T(8,128)S(1)}, f32[5,1,32,128]{3,2,1,0:T(8,128)}, u32[]{:S(2)}) %copy-start) | copy-done | bytes 81944
  0.9 0.1 pool.1
  1.0 3.0 %collective-permute-start.2 = (f32[5,8,128]{2,1,0:T(8,128)S(1)}, f32[5,8,128]{2,1,0:T(8,128)S(1)}, u32[]{:S(2)}, u32[]{:S(2)}) collective-permute-start(f32[5,8,128]{2,1,0:T(8,128)S(1)} %bitcast.13), channel_id=1, source_target_pairs={{0,16},{8,24},{16,0},{24,8},{1,17},{9,25},{17,1},{25,9},{2,18},{10... | collective-permute-start | bytes 61448 | tf_op jit(solution)/shard_map/ppermute | solution.py:750
  4.1 0.0 collective-permute-start.1
  4.1 0.2 collective-permute-start
  4.3 1.6 %collective-permute-done.2.refs_2_ = f32[5,8,128]{2,1,0:T(8,128)S(1)} collective-permute-done((f32[5,8,128]{2,1,0:T(8,128)S(1)}, f32[5,8,128]{2,1,0:T(8,128)S(1)}, u32[]{:S(2)}, u32[]{:S(2)}) %collective-permute-start.2) | collective-permute-done | bytes 20512 | tf_op jit(solution)/shard_map/ppermute | solution.py:750
  5.8 1.4 %collective-permute-done.1.refs_3_.last_ref = f32[5,8,128]{2,1,0:T(8,128)S(1)} collective-permute-done((f32[5,8,128]{2,1,0:T(8,128)S(1)}, f32[5,8,128]{2,1,0:T(8,128)S(1)}, u32[]{:S(2)}, u32[]{:S(2)}) %collective-permute-start.1) | collective-permute-done | bytes 20512 | tf_op jit(solution)/shard_map/ppermute | solution.py:750
  7.3 0.2 pack.1
  7.5 1.6 %collective-permute-start.4 = (f32[13,8,128]{2,1,0:T(8,128)S(1)}, f32[13,8,128]{2,1,0:T(8,128)S(1)}, u32[]{:S(2)}, u32[]{:S(2)}) collective-permute-start(f32[13,8,128]{2,1,0:T(8,128)S(1)} %get-tuple-element.34), channel_id=1, source_target_pairs={{0,2},{1,3},{2,4},{3,5},{4,6},{5,7},{6,0},{7,1},{8,9},{9,10},{10,1... | collective-permute-start | bytes 159752 | tf_op jit(solution)/shard_map/ppermute | solution.py:740
  9.1 2.2 %collective-permute-start.3 = (f32[13,8,128]{2,1,0:T(8,128)S(1)}, f32[13,8,128]{2,1,0:T(8,128)S(1)}, u32[]{:S(2)}, u32[]{:S(2)}) collective-permute-start(f32[13,8,128]{2,1,0:T(8,128)S(1)} %get-tuple-element.33.mine_ref), channel_id=1, source_target_pairs={{0,6},{1,7},{2,0},{3,1},{4,2},{5,3},{6,4},{7,5},{8,15},{9,8},{10,9... | collective-permute-start | bytes 159752 | tf_op jit(solution)/shard_map/ppermute | solution.py:740
  11.3 2.0 %prepare.1 = (bf16[1152,256]{1,0:T(8,128)(2,1)S(1)}, bf16[256,1152]{1,0:T(8,128)(2,1)S(1)}, f32[2,32,32,128]{3,2,1,0:T(8,128)S(1)}, f32[16,32]{1,0:T(8,128)S(1)}...) custom-call(f32[160,128]{1,0:T(8,128)} %bitcast.20, ...), custom_call_target="tpu_custom_call" | custom-call | tf_op jit(solution)/shard_map/prepare/pallas_call | solution.py:707
  13.4 0.2 collective-permute-done.4.got_before
  13.5 0.2 collective-permute-done.3.got_after
  13.8 0.5 %collective-permute-start.6 = (f32[13,8,128]{2,1,0:T(8,128)S(1)}, f32[13,8,128]{2,1,0:T(8,128)S(1)}, u32[]{:S(2)}, u32[]{:S(2)}) collective-permute-start(f32[13,8,128]{2,1,0:T(8,128)S(1)} %collective-permute-done.4.got_before), channel_id=1, source_target_pairs={{0,8},{8,0},{16,24},{24,16},{1,9},{9,1},{17,25},{25,17},{2,10},{10... | collective-permute-start | bytes 159752 | tf_op jit(solution)/shard_map/ppermute | solution.py:743
  14.3 0.7 %collective-permute-done.5.other_after = f32[13,8,128]{2,1,0:T(8,128)S(1)} collective-permute-done((f32[13,8,128]{2,1,0:T(8,128)S(1)}, f32[13,8,128]{2,1,0:T(8,128)S(1)}, u32[]{:S(2)}, u32[]{:S(2)}) %collective-permute-start.5) | collective-permute-done | bytes 53280 | tf_op jit(solution)/shard_map/ppermute | solution.py:743
  15.0 0.2 collective-permute-done.6.other_before
  15.2 5.0 %network.1 = (f32[5,32,128]{2,1,0:T(8,128)S(1)}, f32[5,16,128]{2,1,0:T(8,128)S(1)}, f32[5,8,128]{2,1,0:T(8,128)S(1)}, f32[13,8,128]{2,1,0:T(8,128)S(1)}, f32[13,...) custom-call(s32[1]{0:T(128)} %bitcast.core_ref, f32[5,32,128]{2,1,0:T(8,128)S(1)} %bitcast.12, ...), custom_call_target="tpu_custom_call" | custom-call | tf_op jit(solution)/shard_map/network/pallas_call | solution.py:707
  20.2 0.4 %collective-permute-start.7 = (f32[13,8,128]{2,1,0:T(8,128)S(1)}, f32[13,8,128]{2,1,0:T(8,128)S(1)}, u32[]{:S(2)}, u32[]{:S(2)}) collective-permute-start(f32[13,8,128]{2,1,0:T(8,128)S(1)} %get-tuple-element.53), channel_id=1, source_target_pairs={{0,8},{8,0},{16,24},{24,16},{1,9},{9,1},{17,25},{25,17},{2,10},{10... | collective-permute-start | bytes 159752 | tf_op jit(solution)/shard_map/ppermute | solution.py:743
  20.6 0.2 collective-permute-start.8
  20.8 0.7 %collective-permute-done.7.got_b = f32[13,8,128]{2,1,0:T(8,128)S(1)} collective-permute-done((f32[13,8,128]{2,1,0:T(8,128)S(1)}, f32[13,8,128]{2,1,0:T(8,128)S(1)}, u32[]{:S(2)}, u32[]{:S(2)}) %collective-permute-start.7) | collective-permute-done | bytes 53280 | tf_op jit(solution)/shard_map/ppermute | solution.py:743
  21.5 0.3 %collective-permute-done.8.got_a = f32[13,8,128]{2,1,0:T(8,128)S(1)} collective-permute-done((f32[13,8,128]{2,1,0:T(8,128)S(1)}, f32[13,8,128]{2,1,0:T(8,128)S(1)}, u32[]{:S(2)}, u32[]{:S(2)}) %collective-permute-start.8) | collective-permute-done | bytes 53280 | tf_op jit(solution)/shard_map/ppermute | solution.py:743
  21.9 1.4 %collective-permute-start.9 = (f32[13,8,128]{2,1,0:T(8,128)S(1)}, f32[13,8,128]{2,1,0:T(8,128)S(1)}, u32[]{:S(2)}, u32[]{:S(2)}) collective-permute-start(f32[13,8,128]{2,1,0:T(8,128)S(1)} %get-tuple-element.55), channel_id=1, source_target_pairs={{0,2},{1,3},{2,4},{3,5},{4,6},{5,7},{6,0},{7,1},{8,9},{9,10},{10,1... | collective-permute-start | bytes 159752 | tf_op jit(solution)/shard_map/ppermute | solution.py:740
  23.3 2.5 %collective-permute-start.10 = (f32[13,8,128]{2,1,0:T(8,128)S(1)}, f32[13,8,128]{2,1,0:T(8,128)S(1)}, u32[]{:S(2)}, u32[]{:S(2)}) collective-permute-start(f32[13,8,128]{2,1,0:T(8,128)S(1)} %get-tuple-element.56), channel_id=1, source_target_pairs={{0,6},{1,7},{2,0},{3,1},{4,2},{5,3},{6,4},{7,5},{8,15},{9,8},{10,9... | collective-permute-start | bytes 159752 | tf_op jit(solution)/shard_map/ppermute | solution.py:740
  25.7 2.2 %collective-permute-done.9.from_before = f32[13,8,128]{2,1,0:T(8,128)S(1)} collective-permute-done((f32[13,8,128]{2,1,0:T(8,128)S(1)}, f32[13,8,128]{2,1,0:T(8,128)S(1)}, u32[]{:S(2)}, u32[]{:S(2)}) %collective-permute-start.9) | collective-permute-done | bytes 53280 | tf_op jit(solution)/shard_map/ppermute | solution.py:740
  27.9 0.4 %collective-permute-done.10.from_after = f32[13,8,128]{2,1,0:T(8,128)S(1)} collective-permute-done((f32[13,8,128]{2,1,0:T(8,128)S(1)}, f32[13,8,128]{2,1,0:T(8,128)S(1)}, u32[]{:S(2)}, u32[]{:S(2)}) %collective-permute-start.10) | collective-permute-done | bytes 53280 | tf_op jit(solution)/shard_map/ppermute | solution.py:740
  28.3 0.2 gather.1
  28.5 0.1 collective-permute-start.11
  28.6 0.8 %collective-permute-start.12 = (f32[5,8,128]{2,1,0:T(8,128)S(1)}, f32[5,8,128]{2,1,0:T(8,128)S(1)}, u32[]{:S(2)}, u32[]{:S(2)}) collective-permute-start(f32[5,8,128]{2,1,0:T(8,128)S(1)} %get-tuple-element.59), channel_id=1, source_target_pairs={{0,16},{8,24},{16,0},{24,8},{1,17},{9,25},{17,1},{25,9},{2,18},{10... | collective-permute-start | bytes 61448 | tf_op jit(solution)/shard_map/ppermute | solution.py:823
  29.4 1.0 %collective-permute-start.13 = (f32[5,8,128]{2,1,0:T(8,128)S(1)}, f32[5,8,128]{2,1,0:T(8,128)S(1)}, u32[]{:S(2)}, u32[]{:S(2)}) collective-permute-start(f32[5,8,128]{2,1,0:T(8,128)S(1)} %get-tuple-element.60), channel_id=1, source_target_pairs={{0,24},{8,16},{16,8},{24,0},{1,25},{9,17},{17,9},{25,1},{2,26},{10... | collective-permute-start | bytes 61448 | tf_op jit(solution)/shard_map/ppermute | solution.py:823
  30.5 2.0 %collective-permute-done.12.refs_2_ = f32[5,8,128]{2,1,0:T(8,128)S(1)} collective-permute-done((f32[5,8,128]{2,1,0:T(8,128)S(1)}, f32[5,8,128]{2,1,0:T(8,128)S(1)}, u32[]{:S(2)}, u32[]{:S(2)}) %collective-permute-start.12) | collective-permute-done | bytes 20512 | tf_op jit(solution)/shard_map/ppermute | solution.py:823
  32.5 0.2 collective-permute-done.13.refs_3_
  32.7 0.8 %final.1 = f32[160,128]{1,0:T(8,128)} custom-call(f32[160,128]{1,0:T(8,128)S(1)} %bitcast.18, f32[5,8,128]{2,1,0:T(8,128)S(1)} %get-tuple-element.57.refs_0_, f32[5,8,128]{2,1,0:T(8,128)S(1)} %collective-permute-done.11.refs_1_, f32[5,8,128]{2,1,0:T(8,128)S(1)} %collective-permute-done.12.refs_2_, f32[5,8,128]{2,1,0:T(8,128)S(1)} %collective-permute-done.13.refs_3_), custom_call_target="tpu_custom_call" | custom-call | tf_op jit(solution)/shard_map/final/pallas_call | solution.py:707
  (7 shorter events, 0.0 us)
Async XLA Ops:
  0.0 0.9 %copy-start = (f32[5,1,32,128]{3,2,1,0:T(8,128)S(1)}, f32[5,1,32,128]{3,2,1,0:T(8,128)}, u32[]{:S(2)}) copy-start(f32[5,1,32,128]{3,2,1,0:T(8,128)} %param.8) | copy-start | bytes 245764
  0.9 14.3 %copy-start.1 = (f32[5,1,32,128]{3,2,1,0:T(8,128)S(1)}, f32[5,1,32,128]{3,2,1,0:T(8,128)}, u32[]{:S(2)}) copy-start(f32[5,1,32,128]{3,2,1,0:T(8,128)} %param.8) | copy-start | bytes 245764
  1.0 4.8 %collective-permute-start.2 = (f32[5,8,128]{2,1,0:T(8,128)S(1)}, f32[5,8,128]{2,1,0:T(8,128)S(1)}, u32[]{:S(2)}, u32[]{:S(2)}) collective-permute-start(f32[5,8,128]{2,1,0:T(8,128)S(1)} %bitcast.13), channel_id=1, source_target_pairs={{0,16},{8,24},{16,0},{24,8},{1,17},{9,25},{17,1},{25,9},{2,18},{10... | collective-permute-start | bytes 61448 | tf_op jit(solution)/shard_map/ppermute | solution.py:750
  4.1 3.2 %collective-permute-start.1 = (f32[5,8,128]{2,1,0:T(8,128)S(1)}, f32[5,8,128]{2,1,0:T(8,128)S(1)}, u32[]{:S(2)}, u32[]{:S(2)}) collective-permute-start(f32[5,8,128]{2,1,0:T(8,128)S(1)} %bitcast.14), channel_id=1, source_target_pairs={{0,24},{8,16},{16,8},{24,0},{1,25},{9,17},{17,9},{25,1},{2,26},{10... | collective-permute-start | bytes 61448 | tf_op jit(solution)/shard_map/ppermute | solution.py:750
  4.1 3.2 %collective-permute-start = (f32[5,8,128]{2,1,0:T(8,128)S(1)}, f32[5,8,128]{2,1,0:T(8,128)S(1)}, u32[]{:S(2)}, u32[]{:S(2)}) collective-permute-start(f32[5,8,128]{2,1,0:T(8,128)S(1)} %bitcast.15), channel_id=1, source_target_pairs={{0,8},{8,0},{16,24},{24,16},{1,9},{9,1},{17,25},{25,17},{2,10},{10... | collective-permute-start | bytes 61448 | tf_op jit(solution)/shard_map/ppermute | solution.py:750
  7.5 6.1 %collective-permute-start.4 = (f32[13,8,128]{2,1,0:T(8,128)S(1)}, f32[13,8,128]{2,1,0:T(8,128)S(1)}, u32[]{:S(2)}, u32[]{:S(2)}) collective-permute-start(f32[13,8,128]{2,1,0:T(8,128)S(1)} %get-tuple-element.34), channel_id=1, source_target_pairs={{0,2},{1,3},{2,4},{3,5},{4,6},{5,7},{6,0},{7,1},{8,9},{9,10},{10,1... | collective-permute-start | bytes 159752 | tf_op jit(solution)/shard_map/ppermute | solution.py:740
  9.1 4.7 %collective-permute-start.3 = (f32[13,8,128]{2,1,0:T(8,128)S(1)}, f32[13,8,128]{2,1,0:T(8,128)S(1)}, u32[]{:S(2)}, u32[]{:S(2)}) collective-permute-start(f32[13,8,128]{2,1,0:T(8,128)S(1)} %get-tuple-element.33.mine_ref), channel_id=1, source_target_pairs={{0,6},{1,7},{2,0},{3,1},{4,2},{5,3},{6,4},{7,5},{8,15},{9,8},{10,9... | collective-permute-start | bytes 159752 | tf_op jit(solution)/shard_map/ppermute | solution.py:740
  13.8 1.2 %collective-permute-start.5 = (f32[13,8,128]{2,1,0:T(8,128)S(1)}, f32[13,8,128]{2,1,0:T(8,128)S(1)}, u32[]{:S(2)}, u32[]{:S(2)}) collective-permute-start(f32[13,8,128]{2,1,0:T(8,128)S(1)} %collective-permute-done.3.got_after), channel_id=1, source_target_pairs={{0,8},{8,0},{16,24},{24,16},{1,9},{9,1},{17,25},{25,17},{2,10},{10... | collective-permute-start | bytes 159752 | tf_op jit(solution)/shard_map/ppermute | solution.py:743
  13.8 1.4 %collective-permute-start.6 = (f32[13,8,128]{2,1,0:T(8,128)S(1)}, f32[13,8,128]{2,1,0:T(8,128)S(1)}, u32[]{:S(2)}, u32[]{:S(2)}) collective-permute-start(f32[13,8,128]{2,1,0:T(8,128)S(1)} %collective-permute-done.4.got_before), channel_id=1, source_target_pairs={{0,8},{8,0},{16,24},{24,16},{1,9},{9,1},{17,25},{25,17},{2,10},{10... | collective-permute-start | bytes 159752 | tf_op jit(solution)/shard_map/ppermute | solution.py:743
  20.2 1.3 %collective-permute-start.7 = (f32[13,8,128]{2,1,0:T(8,128)S(1)}, f32[13,8,128]{2,1,0:T(8,128)S(1)}, u32[]{:S(2)}, u32[]{:S(2)}) collective-permute-start(f32[13,8,128]{2,1,0:T(8,128)S(1)} %get-tuple-element.53), channel_id=1, source_target_pairs={{0,8},{8,0},{16,24},{24,16},{1,9},{9,1},{17,25},{25,17},{2,10},{10... | collective-permute-start | bytes 159752 | tf_op jit(solution)/shard_map/ppermute | solution.py:743
  20.6 1.2 %collective-permute-start.8 = (f32[13,8,128]{2,1,0:T(8,128)S(1)}, f32[13,8,128]{2,1,0:T(8,128)S(1)}, u32[]{:S(2)}, u32[]{:S(2)}) collective-permute-start(f32[13,8,128]{2,1,0:T(8,128)S(1)} %get-tuple-element.54), channel_id=1, source_target_pairs={{0,8},{8,0},{16,24},{24,16},{1,9},{9,1},{17,25},{25,17},{2,10},{10... | collective-permute-start | bytes 159752 | tf_op jit(solution)/shard_map/ppermute | solution.py:743
  21.9 6.1 %collective-permute-start.9 = (f32[13,8,128]{2,1,0:T(8,128)S(1)}, f32[13,8,128]{2,1,0:T(8,128)S(1)}, u32[]{:S(2)}, u32[]{:S(2)}) collective-permute-start(f32[13,8,128]{2,1,0:T(8,128)S(1)} %get-tuple-element.55), channel_id=1, source_target_pairs={{0,2},{1,3},{2,4},{3,5},{4,6},{5,7},{6,0},{7,1},{8,9},{9,10},{10,1... | collective-permute-start | bytes 159752 | tf_op jit(solution)/shard_map/ppermute | solution.py:740
  23.3 5.1 %collective-permute-start.10 = (f32[13,8,128]{2,1,0:T(8,128)S(1)}, f32[13,8,128]{2,1,0:T(8,128)S(1)}, u32[]{:S(2)}, u32[]{:S(2)}) collective-permute-start(f32[13,8,128]{2,1,0:T(8,128)S(1)} %get-tuple-element.56), channel_id=1, source_target_pairs={{0,6},{1,7},{2,0},{3,1},{4,2},{5,3},{6,4},{7,5},{8,15},{9,8},{10,9... | collective-permute-start | bytes 159752 | tf_op jit(solution)/shard_map/ppermute | solution.py:740
  28.5 1.9 %collective-permute-start.11 = (f32[5,8,128]{2,1,0:T(8,128)S(1)}, f32[5,8,128]{2,1,0:T(8,128)S(1)}, u32[]{:S(2)}, u32[]{:S(2)}) collective-permute-start(f32[5,8,128]{2,1,0:T(8,128)S(1)} %get-tuple-element.58), channel_id=1, source_target_pairs={{0,8},{8,0},{16,24},{24,16},{1,9},{9,1},{17,25},{25,17},{2,10},{10... | collective-permute-start | bytes 61448 | tf_op jit(solution)/shard_map/ppermute | solution.py:823
  28.6 3.9 %collective-permute-start.12 = (f32[5,8,128]{2,1,0:T(8,128)S(1)}, f32[5,8,128]{2,1,0:T(8,128)S(1)}, u32[]{:S(2)}, u32[]{:S(2)}) collective-permute-start(f32[5,8,128]{2,1,0:T(8,128)S(1)} %get-tuple-element.59), channel_id=1, source_target_pairs={{0,16},{8,24},{16,0},{24,8},{1,17},{9,25},{17,1},{25,9},{2,18},{10... | collective-permute-start | bytes 61448 | tf_op jit(solution)/shard_map/ppermute | solution.py:823
  29.4 3.3 %collective-permute-start.13 = (f32[5,8,128]{2,1,0:T(8,128)S(1)}, f32[5,8,128]{2,1,0:T(8,128)S(1)}, u32[]{:S(2)}, u32[]{:S(2)}) collective-permute-start(f32[5,8,128]{2,1,0:T(8,128)S(1)} %get-tuple-element.60), channel_id=1, source_target_pairs={{0,24},{8,16},{16,8},{24,0},{1,25},{9,17},{17,9},{25,1},{2,26},{10... | collective-permute-start | bytes 61448 | tf_op jit(solution)/shard_map/ppermute | solution.py:823

commit v4 on v3

--- a/solution.py
+++ b/solution.py
@@ -363,6 +363,19 @@
         ]
         step *= 2
     return values[0]
+
+
+def exchanged(values):
+    row = index_of(values[0].shape, 0)
+    for step in (1, 2, 4):
+        held = (row & step) != 0
+        values = list(values)
+        for k in range(8):
+            if not k & step:
+                a, b = values[k], values[k + step]
+                values[k] = jnp.where(held, pltpu.roll(b, step, 0), a)
+                values[k + step] = jnp.where(held, b, pltpu.roll(a, 8 - step, 0))
+    return values
 
 
 def unmix(weights, layer, grads):
@@ -486,13 +499,18 @@
     for c in range(3 * channels, padded):
         x_ref[c * rows : (c + 1) * rows, :] = jnp.zeros((rows, cols), F32)
 
-    for i in range(rows):
-        at = slice(i * cols, (i + 1) * cols)
-        value = x_ref[pl.ds(i, padded, stride=rows), :]
-        local_ref[:padded, at] = value
-        high, low = split(value)
-        feature_pair[:padded, at] = high
-        feature_pair[padded:, at] = low
+    for block in range(0, rows, 8):
+        bands = [
+            exchanged([x_ref[c * rows + block : c * rows + block + 8, :] for c in range(k, k + 8)])
+            for k in range(0, padded, 8)
+        ]
+        for i in range(8):
+            at = slice((block + i) * cols, (block + i + 1) * cols)
+            value = jnp.concatenate([band[i] for band in bands], axis=0)
+            local_ref[:padded, at] = value
+            high, low = split(value)
+            feature_pair[:padded, at] = high
+            feature_pair[padded:, at] = low
 
     lift = lift_ref[...]
     lift_t = lift_t_ref[...]
@@ -555,8 +573,11 @@
     expanded(exact_dot(lift, unmix(by_input, 0, modes)), padded)
     for k in range(0, padded, 8):
         band = slice(k, k + 8)
-        for i, (at, value) in enumerate(zip(columns, unfolded(band))):
-            grad_x_ref[pl.ds(k * rows + i, 8, stride=rows), :] = value + local_ref[band, at]
+        values = [value + local_ref[band, at] for at, value in zip(columns, unfolded(band))]
+        for block in range(0, rows, 8):
+            for c, value in enumerate(exchanged(values[block : block + 8])):
+                at = (k + c) * rows + block
+                grad_x_ref[at : at + 8, :] = value
 
     for c in range(channels):
         own_ref[c] = grad_x_ref[c * rows : (c + 1) * rows, :]

time: 33.6 us -> 33.4 us (level)
  no operation moved by 1% of the time
where the time goes in v4:
time: 33.4 us; the launch traced here: 33.3 us
  starting transfers between devices  14 us (42%)
  waiting for transfers between devices  10.2 us (31%)
  Pallas kernels  8.15 us (24%)
  local copies, waits for them, and re-layouts  0.89 us (3%)
    pallas_call x7, Pallas kernels, call(): pl.pallas_call(kernel, out_shape=outs, in_specs=places, out_specs=out_pla...  8.15 us
    ppermute x4, starting transfers between devices, along_y(): return lax.ppermute(value, ('gx', 'gy'), pairs)  7.75 us
    ppermute x3, starting transfers between devices, body(): lax.ppermute(packed, 'gx', chip.pairs(slot))  3.23 us
    ppermute x3, waiting for transfers between devices, body(): lax.ppermute(packed, 'gx', chip.pairs(slot))  3.02 us
    ppermute x4, waiting for transfers between devices, along_y(): return lax.ppermute(value, ('gx', 'gy'), pairs)  3.01 us
    ppermute x3, waiting for transfers between devices, body(): lax.ppermute(parts[slot], 'gx', chip.pairs(slot, back=True))  2.22 us
    ppermute x4, waiting for transfers between devices, swap(): return lax.ppermute(value, 'gx', [(s, s ^ 1) for s in range(gx)])  1.96 us
    ppermute x3, starting transfers between devices, body(): lax.ppermute(parts[slot], 'gx', chip.pairs(slot, back=True))  1.92 us
  transfers between devices with their start and end apart: 14, of which 12 were waited for; matrix products, arithmetic and copies ran while one was open for 0% of the time, Pallas kernels for 6%

profile of v4, /device:TPU:0, one launch (start us, length us, event | category | flops | bytes accessed | tf_op | source)
XLA Modules:
  0.0 33.3 jit_solution(8514082234712546256)
XLA Ops:
  0.0 0.9 %copy-done = f32[5,1,32,128]{3,2,1,0:T(8,128)S(1)} copy-done((f32[5,1,32,128]{3,2,1,0:T(8,128)S(1)}, f32[5,1,32,128]{3,2,1,0:T(8,128)}, u32[]{:S(2)}) %copy-start) | copy-done | bytes 81944
  0.9 0.1 pool.1
  1.0 3.0 %collective-permute-start.2 = (f32[5,8,128]{2,1,0:T(8,128)S(1)}, f32[5,8,128]{2,1,0:T(8,128)S(1)}, u32[]{:S(2)}, u32[]{:S(2)}) collective-permute-start(f32[5,8,128]{2,1,0:T(8,128)S(1)} %bitcast.13), channel_id=1, source_target_pairs={{0,16},{8,24},{16,0},{24,8},{1,17},{9,25},{17,1},{25,9},{2,18},{10... | collective-permute-start | bytes 61448 | tf_op jit(solution)/shard_map/ppermute | solution.py:771
  4.1 0.0 collective-permute-start.1
  4.1 0.2 collective-permute-start
  4.3 1.6 %collective-permute-done.2.refs_2_ = f32[5,8,128]{2,1,0:T(8,128)S(1)} collective-permute-done((f32[5,8,128]{2,1,0:T(8,128)S(1)}, f32[5,8,128]{2,1,0:T(8,128)S(1)}, u32[]{:S(2)}, u32[]{:S(2)}) %collective-permute-start.2) | collective-permute-done | bytes 20512 | tf_op jit(solution)/shard_map/ppermute | solution.py:771
  5.8 1.4 %collective-permute-done.1.refs_3_.last_ref = f32[5,8,128]{2,1,0:T(8,128)S(1)} collective-permute-done((f32[5,8,128]{2,1,0:T(8,128)S(1)}, f32[5,8,128]{2,1,0:T(8,128)S(1)}, u32[]{:S(2)}, u32[]{:S(2)}) %collective-permute-start.1) | collective-permute-done | bytes 20512 | tf_op jit(solution)/shard_map/ppermute | solution.py:771
  7.3 0.2 pack.1
  7.5 1.6 %collective-permute-start.4 = (f32[13,8,128]{2,1,0:T(8,128)S(1)}, f32[13,8,128]{2,1,0:T(8,128)S(1)}, u32[]{:S(2)}, u32[]{:S(2)}) collective-permute-start(f32[13,8,128]{2,1,0:T(8,128)S(1)} %get-tuple-element.34), channel_id=1, source_target_pairs={{0,2},{1,3},{2,4},{3,5},{4,6},{5,7},{6,0},{7,1},{8,9},{9,10},{10,1... | collective-permute-start | bytes 159752 | tf_op jit(solution)/shard_map/ppermute | solution.py:761
  9.1 2.2 %collective-permute-start.3 = (f32[13,8,128]{2,1,0:T(8,128)S(1)}, f32[13,8,128]{2,1,0:T(8,128)S(1)}, u32[]{:S(2)}, u32[]{:S(2)}) collective-permute-start(f32[13,8,128]{2,1,0:T(8,128)S(1)} %get-tuple-element.33.mine_ref), channel_id=1, source_target_pairs={{0,6},{1,7},{2,0},{3,1},{4,2},{5,3},{6,4},{7,5},{8,15},{9,8},{10,9... | collective-permute-start | bytes 159752 | tf_op jit(solution)/shard_map/ppermute | solution.py:761
  11.3 2.0 %prepare.1 = (bf16[1152,256]{1,0:T(8,128)(2,1)S(1)}, bf16[256,1152]{1,0:T(8,128)(2,1)S(1)}, f32[2,32,32,128]{3,2,1,0:T(8,128)S(1)}, f32[16,32]{1,0:T(8,128)S(1)}...) custom-call(f32[160,128]{1,0:T(8,128)} %bitcast.20, ...), custom_call_target="tpu_custom_call" | custom-call | tf_op jit(solution)/shard_map/prepare/pallas_call | solution.py:728
  13.4 0.2 collective-permute-done.4.got_before
  13.5 0.2 collective-permute-done.3.got_after
  13.8 0.5 %collective-permute-start.6 = (f32[13,8,128]{2,1,0:T(8,128)S(1)}, f32[13,8,128]{2,1,0:T(8,128)S(1)}, u32[]{:S(2)}, u32[]{:S(2)}) collective-permute-start(f32[13,8,128]{2,1,0:T(8,128)S(1)} %collective-permute-done.4.got_before), channel_id=1, source_target_pairs={{0,8},{8,0},{16,24},{24,16},{1,9},{9,1},{17,25},{25,17},{2,10},{10... | collective-permute-start | bytes 159752 | tf_op jit(solution)/shard_map/ppermute | solution.py:764
  14.3 0.7 %collective-permute-done.5.other_after = f32[13,8,128]{2,1,0:T(8,128)S(1)} collective-permute-done((f32[13,8,128]{2,1,0:T(8,128)S(1)}, f32[13,8,128]{2,1,0:T(8,128)S(1)}, u32[]{:S(2)}, u32[]{:S(2)}) %collective-permute-start.5) | collective-permute-done | bytes 53280 | tf_op jit(solution)/shard_map/ppermute | solution.py:764
  15.0 0.2 collective-permute-done.6.other_before
  15.2 4.8 %network.1 = (f32[5,32,128]{2,1,0:T(8,128)S(1)}, f32[5,16,128]{2,1,0:T(8,128)S(1)}, f32[5,8,128]{2,1,0:T(8,128)S(1)}, f32[13,8,128]{2,1,0:T(8,128)S(1)}, f32[13,...) custom-call(s32[1]{0:T(128)} %bitcast.core_ref, f32[5,32,128]{2,1,0:T(8,128)S(1)} %bitcast.12, ...), custom_call_target="tpu_custom_call" | custom-call | tf_op jit(solution)/shard_map/network/pallas_call | solution.py:728
  20.0 0.4 %collective-permute-start.7 = (f32[13,8,128]{2,1,0:T(8,128)S(1)}, f32[13,8,128]{2,1,0:T(8,128)S(1)}, u32[]{:S(2)}, u32[]{:S(2)}) collective-permute-start(f32[13,8,128]{2,1,0:T(8,128)S(1)} %get-tuple-element.53), channel_id=1, source_target_pairs={{0,8},{8,0},{16,24},{24,16},{1,9},{9,1},{17,25},{25,17},{2,10},{10... | collective-permute-start | bytes 159752 | tf_op jit(solution)/shard_map/ppermute | solution.py:764
  20.4 0.2 collective-permute-start.8
  20.6 0.7 %collective-permute-done.7.got_b = f32[13,8,128]{2,1,0:T(8,128)S(1)} collective-permute-done((f32[13,8,128]{2,1,0:T(8,128)S(1)}, f32[13,8,128]{2,1,0:T(8,128)S(1)}, u32[]{:S(2)}, u32[]{:S(2)}) %collective-permute-start.7) | collective-permute-done | bytes 53280 | tf_op jit(solution)/shard_map/ppermute | solution.py:764
  21.3 0.3 %collective-permute-done.8.got_a = f32[13,8,128]{2,1,0:T(8,128)S(1)} collective-permute-done((f32[13,8,128]{2,1,0:T(8,128)S(1)}, f32[13,8,128]{2,1,0:T(8,128)S(1)}, u32[]{:S(2)}, u32[]{:S(2)}) %collective-permute-start.8) | collective-permute-done | bytes 53280 | tf_op jit(solution)/shard_map/ppermute | solution.py:764
  21.7 1.4 %collective-permute-start.9 = (f32[13,8,128]{2,1,0:T(8,128)S(1)}, f32[13,8,128]{2,1,0:T(8,128)S(1)}, u32[]{:S(2)}, u32[]{:S(2)}) collective-permute-start(f32[13,8,128]{2,1,0:T(8,128)S(1)} %get-tuple-element.55), channel_id=1, source_target_pairs={{0,2},{1,3},{2,4},{3,5},{4,6},{5,7},{6,0},{7,1},{8,9},{9,10},{10,1... | collective-permute-start | bytes 159752 | tf_op jit(solution)/shard_map/ppermute | solution.py:761
  23.1 2.5 %collective-permute-start.10 = (f32[13,8,128]{2,1,0:T(8,128)S(1)}, f32[13,8,128]{2,1,0:T(8,128)S(1)}, u32[]{:S(2)}, u32[]{:S(2)}) collective-permute-start(f32[13,8,128]{2,1,0:T(8,128)S(1)} %get-tuple-element.56), channel_id=1, source_target_pairs={{0,6},{1,7},{2,0},{3,1},{4,2},{5,3},{6,4},{7,5},{8,15},{9,8},{10,9... | collective-permute-start | bytes 159752 | tf_op jit(solution)/shard_map/ppermute | solution.py:761
  25.6 2.2 %collective-permute-done.9.from_before = f32[13,8,128]{2,1,0:T(8,128)S(1)} collective-permute-done((f32[13,8,128]{2,1,0:T(8,128)S(1)}, f32[13,8,128]{2,1,0:T(8,128)S(1)}, u32[]{:S(2)}, u32[]{:S(2)}) %collective-permute-start.9) | collective-permute-done | bytes 53280 | tf_op jit(solution)/shard_map/ppermute | solution.py:761
  27.8 0.4 %collective-permute-done.10.from_after = f32[13,8,128]{2,1,0:T(8,128)S(1)} collective-permute-done((f32[13,8,128]{2,1,0:T(8,128)S(1)}, f32[13,8,128]{2,1,0:T(8,128)S(1)}, u32[]{:S(2)}, u32[]{:S(2)}) %collective-permute-start.10) | collective-permute-done | bytes 53280 | tf_op jit(solution)/shard_map/ppermute | solution.py:761
  28.2 0.2 gather.1
  28.3 0.1 collective-permute-start.11
  28.4 0.8 %collective-permute-start.12 = (f32[5,8,128]{2,1,0:T(8,128)S(1)}, f32[5,8,128]{2,1,0:T(8,128)S(1)}, u32[]{:S(2)}, u32[]{:S(2)}) collective-permute-start(f32[5,8,128]{2,1,0:T(8,128)S(1)} %get-tuple-element.59), channel_id=1, source_target_pairs={{0,16},{8,24},{16,0},{24,8},{1,17},{9,25},{17,1},{25,9},{2,18},{10... | collective-permute-start | bytes 61448 | tf_op jit(solution)/shard_map/ppermute | solution.py:844
  29.2 1.0 %collective-permute-start.13 = (f32[5,8,128]{2,1,0:T(8,128)S(1)}, f32[5,8,128]{2,1,0:T(8,128)S(1)}, u32[]{:S(2)}, u32[]{:S(2)}) collective-permute-start(f32[5,8,128]{2,1,0:T(8,128)S(1)} %get-tuple-element.60), channel_id=1, source_target_pairs={{0,24},{8,16},{16,8},{24,0},{1,25},{9,17},{17,9},{25,1},{2,26},{10... | collective-permute-start | bytes 61448 | tf_op jit(solution)/shard_map/ppermute | solution.py:844
  30.3 2.0 %collective-permute-done.12.refs_2_ = f32[5,8,128]{2,1,0:T(8,128)S(1)} collective-permute-done((f32[5,8,128]{2,1,0:T(8,128)S(1)}, f32[5,8,128]{2,1,0:T(8,128)S(1)}, u32[]{:S(2)}, u32[]{:S(2)}) %collective-permute-start.12) | collective-permute-done | bytes 20512 | tf_op jit(solution)/shard_map/ppermute | solution.py:844
  32.3 0.2 collective-permute-done.13.refs_3_
  32.5 0.8 %final.1 = f32[160,128]{1,0:T(8,128)} custom-call(f32[160,128]{1,0:T(8,128)S(1)} %bitcast.18, f32[5,8,128]{2,1,0:T(8,128)S(1)} %get-tuple-element.57.refs_0_, f32[5,8,128]{2,1,0:T(8,128)S(1)} %collective-permute-done.11.refs_1_, f32[5,8,128]{2,1,0:T(8,128)S(1)} %collective-permute-done.12.refs_2_, f32[5,8,128]{2,1,0:T(8,128)S(1)} %collective-permute-done.13.refs_3_), custom_call_target="tpu_custom_call" | custom-call | tf_op jit(solution)/shard_map/final/pallas_call | solution.py:728
  (7 shorter events, 0.0 us)
Async XLA Ops:
  0.0 0.9 %copy-start = (f32[5,1,32,128]{3,2,1,0:T(8,128)S(1)}, f32[5,1,32,128]{3,2,1,0:T(8,128)}, u32[]{:S(2)}) copy-start(f32[5,1,32,128]{3,2,1,0:T(8,128)} %param.8) | copy-start | bytes 245764
  0.9 14.3 %copy-start.1 = (f32[5,1,32,128]{3,2,1,0:T(8,128)S(1)}, f32[5,1,32,128]{3,2,1,0:T(8,128)}, u32[]{:S(2)}) copy-start(f32[5,1,32,128]{3,2,1,0:T(8,128)} %param.8) | copy-start | bytes 245764
  1.0 4.8 %collective-permute-start.2 = (f32[5,8,128]{2,1,0:T(8,128)S(1)}, f32[5,8,128]{2,1,0:T(8,128)S(1)}, u32[]{:S(2)}, u32[]{:S(2)}) collective-permute-start(f32[5,8,128]{2,1,0:T(8,128)S(1)} %bitcast.13), channel_id=1, source_target_pairs={{0,16},{8,24},{16,0},{24,8},{1,17},{9,25},{17,1},{25,9},{2,18},{10... | collective-permute-start | bytes 61448 | tf_op jit(solution)/shard_map/ppermute | solution.py:771
  4.1 3.2 %collective-permute-start.1 = (f32[5,8,128]{2,1,0:T(8,128)S(1)}, f32[5,8,128]{2,1,0:T(8,128)S(1)}, u32[]{:S(2)}, u32[]{:S(2)}) collective-permute-start(f32[5,8,128]{2,1,0:T(8,128)S(1)} %bitcast.14), channel_id=1, source_target_pairs={{0,24},{8,16},{16,8},{24,0},{1,25},{9,17},{17,9},{25,1},{2,26},{10... | collective-permute-start | bytes 61448 | tf_op jit(solution)/shard_map/ppermute | solution.py:771
  4.1 3.2 %collective-permute-start = (f32[5,8,128]{2,1,0:T(8,128)S(1)}, f32[5,8,128]{2,1,0:T(8,128)S(1)}, u32[]{:S(2)}, u32[]{:S(2)}) collective-permute-start(f32[5,8,128]{2,1,0:T(8,128)S(1)} %bitcast.15), channel_id=1, source_target_pairs={{0,8},{8,0},{16,24},{24,16},{1,9},{9,1},{17,25},{25,17},{2,10},{10... | collective-permute-start | bytes 61448 | tf_op jit(solution)/shard_map/ppermute | solution.py:771
  7.5 6.1 %collective-permute-start.4 = (f32[13,8,128]{2,1,0:T(8,128)S(1)}, f32[13,8,128]{2,1,0:T(8,128)S(1)}, u32[]{:S(2)}, u32[]{:S(2)}) collective-permute-start(f32[13,8,128]{2,1,0:T(8,128)S(1)} %get-tuple-element.34), channel_id=1, source_target_pairs={{0,2},{1,3},{2,4},{3,5},{4,6},{5,7},{6,0},{7,1},{8,9},{9,10},{10,1... | collective-permute-start | bytes 159752 | tf_op jit(solution)/shard_map/ppermute | solution.py:761
  9.1 4.7 %collective-permute-start.3 = (f32[13,8,128]{2,1,0:T(8,128)S(1)}, f32[13,8,128]{2,1,0:T(8,128)S(1)}, u32[]{:S(2)}, u32[]{:S(2)}) collective-permute-start(f32[13,8,128]{2,1,0:T(8,128)S(1)} %get-tuple-element.33.mine_ref), channel_id=1, source_target_pairs={{0,6},{1,7},{2,0},{3,1},{4,2},{5,3},{6,4},{7,5},{8,15},{9,8},{10,9... | collective-permute-start | bytes 159752 | tf_op jit(solution)/shard_map/ppermute | solution.py:761
  13.8 1.2 %collective-permute-start.5 = (f32[13,8,128]{2,1,0:T(8,128)S(1)}, f32[13,8,128]{2,1,0:T(8,128)S(1)}, u32[]{:S(2)}, u32[]{:S(2)}) collective-permute-start(f32[13,8,128]{2,1,0:T(8,128)S(1)} %collective-permute-done.3.got_after), channel_id=1, source_target_pairs={{0,8},{8,0},{16,24},{24,16},{1,9},{9,1},{17,25},{25,17},{2,10},{10... | collective-permute-start | bytes 159752 | tf_op jit(solution)/shard_map/ppermute | solution.py:764
  13.8 1.4 %collective-permute-start.6 = (f32[13,8,128]{2,1,0:T(8,128)S(1)}, f32[13,8,128]{2,1,0:T(8,128)S(1)}, u32[]{:S(2)}, u32[]{:S(2)}) collective-permute-start(f32[13,8,128]{2,1,0:T(8,128)S(1)} %collective-permute-done.4.got_before), channel_id=1, source_target_pairs={{0,8},{8,0},{16,24},{24,16},{1,9},{9,1},{17,25},{25,17},{2,10},{10... | collective-permute-start | bytes 159752 | tf_op jit(solution)/shard_map/ppermute | solution.py:764
  20.0 1.3 %collective-permute-start.7 = (f32[13,8,128]{2,1,0:T(8,128)S(1)}, f32[13,8,128]{2,1,0:T(8,128)S(1)}, u32[]{:S(2)}, u32[]{:S(2)}) collective-permute-start(f32[13,8,128]{2,1,0:T(8,128)S(1)} %get-tuple-element.53), channel_id=1, source_target_pairs={{0,8},{8,0},{16,24},{24,16},{1,9},{9,1},{17,25},{25,17},{2,10},{10... | collective-permute-start | bytes 159752 | tf_op jit(solution)/shard_map/ppermute | solution.py:764
  20.4 1.2 %collective-permute-start.8 = (f32[13,8,128]{2,1,0:T(8,128)S(1)}, f32[13,8,128]{2,1,0:T(8,128)S(1)}, u32[]{:S(2)}, u32[]{:S(2)}) collective-permute-start(f32[13,8,128]{2,1,0:T(8,128)S(1)} %get-tuple-element.54), channel_id=1, source_target_pairs={{0,8},{8,0},{16,24},{24,16},{1,9},{9,1},{17,25},{25,17},{2,10},{10... | collective-permute-start | bytes 159752 | tf_op jit(solution)/shard_map/ppermute | solution.py:764
  21.7 6.1 %collective-permute-start.9 = (f32[13,8,128]{2,1,0:T(8,128)S(1)}, f32[13,8,128]{2,1,0:T(8,128)S(1)}, u32[]{:S(2)}, u32[]{:S(2)}) collective-permute-start(f32[13,8,128]{2,1,0:T(8,128)S(1)} %get-tuple-element.55), channel_id=1, source_target_pairs={{0,2},{1,3},{2,4},{3,5},{4,6},{5,7},{6,0},{7,1},{8,9},{9,10},{10,1... | collective-permute-start | bytes 159752 | tf_op jit(solution)/shard_map/ppermute | solution.py:761
  23.1 5.1 %collective-permute-start.10 = (f32[13,8,128]{2,1,0:T(8,128)S(1)}, f32[13,8,128]{2,1,0:T(8,128)S(1)}, u32[]{:S(2)}, u32[]{:S(2)}) collective-permute-start(f32[13,8,128]{2,1,0:T(8,128)S(1)} %get-tuple-element.56), channel_id=1, source_target_pairs={{0,6},{1,7},{2,0},{3,1},{4,2},{5,3},{6,4},{7,5},{8,15},{9,8},{10,9... | collective-permute-start | bytes 159752 | tf_op jit(solution)/shard_map/ppermute | solution.py:761
  28.3 1.9 %collective-permute-start.11 = (f32[5,8,128]{2,1,0:T(8,128)S(1)}, f32[5,8,128]{2,1,0:T(8,128)S(1)}, u32[]{:S(2)}, u32[]{:S(2)}) collective-permute-start(f32[5,8,128]{2,1,0:T(8,128)S(1)} %get-tuple-element.58), channel_id=1, source_target_pairs={{0,8},{8,0},{16,24},{24,16},{1,9},{9,1},{17,25},{25,17},{2,10},{10... | collective-permute-start | bytes 61448 | tf_op jit(solution)/shard_map/ppermute | solution.py:844
  28.4 3.9 %collective-permute-start.12 = (f32[5,8,128]{2,1,0:T(8,128)S(1)}, f32[5,8,128]{2,1,0:T(8,128)S(1)}, u32[]{:S(2)}, u32[]{:S(2)}) collective-permute-start(f32[5,8,128]{2,1,0:T(8,128)S(1)} %get-tuple-element.59), channel_id=1, source_target_pairs={{0,16},{8,24},{16,0},{24,8},{1,17},{9,25},{17,1},{25,9},{2,18},{10... | collective-permute-start | bytes 61448 | tf_op jit(solution)/shard_map/ppermute | solution.py:844
  29.2 3.3 %collective-permute-start.13 = (f32[5,8,128]{2,1,0:T(8,128)S(1)}, f32[5,8,128]{2,1,0:T(8,128)S(1)}, u32[]{:S(2)}, u32[]{:S(2)}) collective-permute-start(f32[5,8,128]{2,1,0:T(8,128)S(1)} %get-tuple-element.60), channel_id=1, source_target_pairs={{0,24},{8,16},{16,8},{24,0},{1,25},{9,17},{17,9},{25,1},{2,26},{10... | collective-permute-start | bytes 61448 | tf_op jit(solution)/shard_map/ppermute | solution.py:844

commit v5 on v4

--- a/solution.py
+++ b/solution.py
@@ -796,13 +796,13 @@
         limit=16 << 20,
         name="prepare",
     ))
+    *held[1:], prepared[3] = lax.optimization_barrier((*held[1:], prepared[3]))
     message = shape(chip.tiles, tall, cols)
     to_previous, to_following = call(
         functools.partial(pack_kernel, chip), (message, message), core, *held, scalars=1, name="pack"
     )
     from_a = along_y(to_previous, -2, -1)
     from_b = along_y(to_following, 2, 1)
-    from_a, from_b, prepared[3] = lax.optimization_barrier((from_a, from_b, prepared[3]))
     swap_a, swap_b = swap(from_a), swap(from_b)
 
     chunk = 4 * cols

time: 33.4 us -> 33.3 us (level)
    ppermute x4, waiting for transfers between devices: 3.01 us -> 5.11 us  [along_y(): return lax.ppermute(value, ('gx', 'gy'), pairs)]
    ppermute x3, waiting for transfers between devices: 3.02 us -> 1.05 us  [body(): lax.ppermute(packed, 'gx', chip.pairs(slot))]
  transfers between devices with their start and end apart: 14 -> 14, of which waited for: 12 -> 11; matrix products, arithmetic and copies ran while one was open for 0% -> 0% of each run, Pallas kernels for 6% -> 6%
where the time goes in v5:
time: 33.3 us; the launch traced here: 33.1 us
  starting transfers between devices  13.7 us (41%)
  waiting for transfers between devices  10.3 us (31%)
  Pallas kernels  8.15 us (24%)
  local copies, waits for them, and re-layouts  0.89 us (3%)
    pallas_call x7, Pallas kernels, call(): pl.pallas_call(kernel, out_shape=outs, in_specs=places, out_specs=out_pla...  8.15 us
    ppermute x4, starting transfers between devices, along_y(): return lax.ppermute(value, ('gx', 'gy'), pairs)  7.75 us
    ppermute x4, waiting for transfers between devices, along_y(): return lax.ppermute(value, ('gx', 'gy'), pairs)  5.11 us
    ppermute x3, starting transfers between devices, body(): lax.ppermute(packed, 'gx', chip.pairs(slot))  3.15 us
    ppermute x3, waiting for transfers between devices, body(): lax.ppermute(parts[slot], 'gx', chip.pairs(slot, back=True))  2.22 us
    ppermute x4, waiting for transfers between devices, swap(): return lax.ppermute(value, 'gx', [(s, s ^ 1) for s in range(gx)])  1.96 us
    ppermute x3, starting transfers between devices, body(): lax.ppermute(parts[slot], 'gx', chip.pairs(slot, back=True))  1.92 us
    ppermute x3, waiting for transfers between devices, body(): lax.ppermute(packed, 'gx', chip.pairs(slot))  1.05 us
  transfers between devices with their start and end apart: 14, of which 11 were waited for; matrix products, arithmetic and copies ran while one was open for 0% of the time, Pallas kernels for 6%

profile of v5, /device:TPU:0, one launch (start us, length us, event | category | flops | bytes accessed | tf_op | source)
XLA Modules:
  0.0 33.1 jit_solution(842091587773454150)
XLA Ops:
  0.0 0.9 %copy-done = f32[5,1,32,128]{3,2,1,0:T(8,128)S(1)} copy-done((f32[5,1,32,128]{3,2,1,0:T(8,128)S(1)}, f32[5,1,32,128]{3,2,1,0:T(8,128)}, u32[]{:S(2)}) %copy-start) | copy-done | bytes 81944
  0.9 0.1 pool.1
  1.0 2.5 %collective-permute-start.2 = (f32[5,8,128]{2,1,0:T(8,128)S(1)}, f32[5,8,128]{2,1,0:T(8,128)S(1)}, u32[]{:S(2)}, u32[]{:S(2)}) collective-permute-start(f32[5,8,128]{2,1,0:T(8,128)S(1)} %bitcast.13), channel_id=1, source_target_pairs={{0,24},{8,16},{16,8},{24,0},{1,25},{9,17},{17,9},{25,1},{2,26},{10... | collective-permute-start | bytes 61448 | tf_op jit(solution)/shard_map/ppermute | solution.py:771
  3.5 0.6 %collective-permute-start.1 = (f32[5,8,128]{2,1,0:T(8,128)S(1)}, f32[5,8,128]{2,1,0:T(8,128)S(1)}, u32[]{:S(2)}, u32[]{:S(2)}) collective-permute-start(f32[5,8,128]{2,1,0:T(8,128)S(1)} %bitcast.14), channel_id=1, source_target_pairs={{0,16},{8,24},{16,0},{24,8},{1,17},{9,25},{17,1},{25,9},{2,18},{10... | collective-permute-start | bytes 61448 | tf_op jit(solution)/shard_map/ppermute | solution.py:771
  4.2 0.0 collective-permute-start
  4.2 2.0 %prepare.1 = (bf16[1152,256]{1,0:T(8,128)(2,1)S(1)}, bf16[256,1152]{1,0:T(8,128)(2,1)S(1)}, f32[2,32,32,128]{3,2,1,0:T(8,128)S(1)}, f32[16,32]{1,0:T(8,128)S(1)}...) custom-call(f32[160,128]{1,0:T(8,128)} %bitcast.20, ...), custom_call_target="tpu_custom_call" | custom-call | tf_op jit(solution)/shard_map/prepare/pallas_call | solution.py:728
  6.2 0.0 collective-permute-done.2.refs_3_.last_ref
  6.3 1.0 %collective-permute-done.1.refs_2_ = f32[5,8,128]{2,1,0:T(8,128)S(1)} collective-permute-done((f32[5,8,128]{2,1,0:T(8,128)S(1)}, f32[5,8,128]{2,1,0:T(8,128)S(1)}, u32[]{:S(2)}, u32[]{:S(2)}) %collective-permute-start.1) | collective-permute-done | bytes 20512 | tf_op jit(solution)/shard_map/ppermute | solution.py:771
  7.3 0.2 pack.1
  7.5 1.6 %collective-permute-start.4 = (f32[13,8,128]{2,1,0:T(8,128)S(1)}, f32[13,8,128]{2,1,0:T(8,128)S(1)}, u32[]{:S(2)}, u32[]{:S(2)}) collective-permute-start(f32[13,8,128]{2,1,0:T(8,128)S(1)} %get-tuple-element.39), channel_id=1, source_target_pairs={{0,2},{1,3},{2,4},{3,5},{4,6},{5,7},{6,0},{7,1},{8,9},{9,10},{10,1... | collective-permute-start | bytes 159752 | tf_op jit(solution)/shard_map/ppermute | solution.py:761
  9.1 2.2 %collective-permute-start.3 = (f32[13,8,128]{2,1,0:T(8,128)S(1)}, f32[13,8,128]{2,1,0:T(8,128)S(1)}, u32[]{:S(2)}, u32[]{:S(2)}) collective-permute-start(f32[13,8,128]{2,1,0:T(8,128)S(1)} %get-tuple-element.38.mine_ref), channel_id=1, source_target_pairs={{0,6},{1,7},{2,0},{3,1},{4,2},{5,3},{6,4},{7,5},{8,15},{9,8},{10,9... | collective-permute-start | bytes 159752 | tf_op jit(solution)/shard_map/ppermute | solution.py:761
  11.3 2.2 %collective-permute-done.4.got_before = f32[13,8,128]{2,1,0:T(8,128)S(1)} collective-permute-done((f32[13,8,128]{2,1,0:T(8,128)S(1)}, f32[13,8,128]{2,1,0:T(8,128)S(1)}, u32[]{:S(2)}, u32[]{:S(2)}) %collective-permute-start.4) | collective-permute-done | bytes 53280 | tf_op jit(solution)/shard_map/ppermute | solution.py:761
  13.6 0.2 collective-permute-done.3.got_after
  13.8 0.3 collective-permute-start.5
  14.1 0.7 %collective-permute-done.6.other_before = f32[13,8,128]{2,1,0:T(8,128)S(1)} collective-permute-done((f32[13,8,128]{2,1,0:T(8,128)S(1)}, f32[13,8,128]{2,1,0:T(8,128)S(1)}, u32[]{:S(2)}, u32[]{:S(2)}) %collective-permute-start.6) | collective-permute-done | bytes 53280 | tf_op jit(solution)/shard_map/ppermute | solution.py:764
  14.8 0.2 collective-permute-done.5.other_after
  15.0 4.8 %network.1 = (f32[5,32,128]{2,1,0:T(8,128)S(1)}, f32[5,16,128]{2,1,0:T(8,128)S(1)}, f32[5,8,128]{2,1,0:T(8,128)S(1)}, f32[13,8,128]{2,1,0:T(8,128)S(1)}, f32[13,...) custom-call(s32[1]{0:T(128)} %bitcast.core_ref, f32[5,32,128]{2,1,0:T(8,128)S(1)} %bitcast.12, ...), custom_call_target="tpu_custom_call" | custom-call | tf_op jit(solution)/shard_map/network/pallas_call | solution.py:728
  19.9 0.3 %collective-permute-start.7 = (f32[13,8,128]{2,1,0:T(8,128)S(1)}, f32[13,8,128]{2,1,0:T(8,128)S(1)}, u32[]{:S(2)}, u32[]{:S(2)}) collective-permute-start(f32[13,8,128]{2,1,0:T(8,128)S(1)} %get-tuple-element.55), channel_id=1, source_target_pairs={{0,8},{8,0},{16,24},{24,16},{1,9},{9,1},{17,25},{25,17},{2,10},{10... | collective-permute-start | bytes 159752 | tf_op jit(solution)/shard_map/ppermute | solution.py:764
  20.2 0.2 collective-permute-start.8
  20.4 0.7 %collective-permute-done.7.got_b = f32[13,8,128]{2,1,0:T(8,128)S(1)} collective-permute-done((f32[13,8,128]{2,1,0:T(8,128)S(1)}, f32[13,8,128]{2,1,0:T(8,128)S(1)}, u32[]{:S(2)}, u32[]{:S(2)}) %collective-permute-start.7) | collective-permute-done | bytes 53280 | tf_op jit(solution)/shard_map/ppermute | solution.py:764
  21.2 0.3 collective-permute-done.8.got_a
  21.5 1.3 %collective-permute-start.9 = (f32[13,8,128]{2,1,0:T(8,128)S(1)}, f32[13,8,128]{2,1,0:T(8,128)S(1)}, u32[]{:S(2)}, u32[]{:S(2)}) collective-permute-start(f32[13,8,128]{2,1,0:T(8,128)S(1)} %get-tuple-element.57), channel_id=1, source_target_pairs={{0,2},{1,3},{2,4},{3,5},{4,6},{5,7},{6,0},{7,1},{8,9},{9,10},{10,1... | collective-permute-start | bytes 159752 | tf_op jit(solution)/shard_map/ppermute | solution.py:761
  22.7 2.6 %collective-permute-start.10 = (f32[13,8,128]{2,1,0:T(8,128)S(1)}, f32[13,8,128]{2,1,0:T(8,128)S(1)}, u32[]{:S(2)}, u32[]{:S(2)}) collective-permute-start(f32[13,8,128]{2,1,0:T(8,128)S(1)} %get-tuple-element.58), channel_id=1, source_target_pairs={{0,6},{1,7},{2,0},{3,1},{4,2},{5,3},{6,4},{7,5},{8,15},{9,8},{10,9... | collective-permute-start | bytes 159752 | tf_op jit(solution)/shard_map/ppermute | solution.py:761
  25.3 2.2 %collective-permute-done.9.from_before = f32[13,8,128]{2,1,0:T(8,128)S(1)} collective-permute-done((f32[13,8,128]{2,1,0:T(8,128)S(1)}, f32[13,8,128]{2,1,0:T(8,128)S(1)}, u32[]{:S(2)}, u32[]{:S(2)}) %collective-permute-start.9) | collective-permute-done | bytes 53280 | tf_op jit(solution)/shard_map/ppermute | solution.py:761
  27.5 0.4 %collective-permute-done.10.from_after = f32[13,8,128]{2,1,0:T(8,128)S(1)} collective-permute-done((f32[13,8,128]{2,1,0:T(8,128)S(1)}, f32[13,8,128]{2,1,0:T(8,128)S(1)}, u32[]{:S(2)}, u32[]{:S(2)}) %collective-permute-start.10) | collective-permute-done | bytes 53280 | tf_op jit(solution)/shard_map/ppermute | solution.py:761
  28.0 0.2 gather.1
  28.2 0.1 collective-permute-start.11
  28.2 0.8 %collective-permute-start.12 = (f32[5,8,128]{2,1,0:T(8,128)S(1)}, f32[5,8,128]{2,1,0:T(8,128)S(1)}, u32[]{:S(2)}, u32[]{:S(2)}) collective-permute-start(f32[5,8,128]{2,1,0:T(8,128)S(1)} %get-tuple-element.61), channel_id=1, source_target_pairs={{0,16},{8,24},{16,0},{24,8},{1,17},{9,25},{17,1},{25,9},{2,18},{10... | collective-permute-start | bytes 61448 | tf_op jit(solution)/shard_map/ppermute | solution.py:844
  29.1 1.0 %collective-permute-start.13 = (f32[5,8,128]{2,1,0:T(8,128)S(1)}, f32[5,8,128]{2,1,0:T(8,128)S(1)}, u32[]{:S(2)}, u32[]{:S(2)}) collective-permute-start(f32[5,8,128]{2,1,0:T(8,128)S(1)} %get-tuple-element.62), channel_id=1, source_target_pairs={{0,24},{8,16},{16,8},{24,0},{1,25},{9,17},{17,9},{25,1},{2,26},{10... | collective-permute-start | bytes 61448 | tf_op jit(solution)/shard_map/ppermute | solution.py:844
  30.1 2.0 %collective-permute-done.12.refs_2_ = f32[5,8,128]{2,1,0:T(8,128)S(1)} collective-permute-done((f32[5,8,128]{2,1,0:T(8,128)S(1)}, f32[5,8,128]{2,1,0:T(8,128)S(1)}, u32[]{:S(2)}, u32[]{:S(2)}) %collective-permute-start.12) | collective-permute-done | bytes 20512 | tf_op jit(solution)/shard_map/ppermute | solution.py:844
  32.1 0.2 collective-permute-done.13.refs_3_
  32.3 0.8 %final.1 = f32[160,128]{1,0:T(8,128)} custom-call(f32[160,128]{1,0:T(8,128)S(1)} %bitcast.18, f32[5,8,128]{2,1,0:T(8,128)S(1)} %get-tuple-element.59.refs_0_, f32[5,8,128]{2,1,0:T(8,128)S(1)} %collective-permute-done.11.refs_1_, f32[5,8,128]{2,1,0:T(8,128)S(1)} %collective-permute-done.12.refs_2_, f32[5,8,128]{2,1,0:T(8,128)S(1)} %collective-permute-done.13.refs_3_), custom_call_target="tpu_custom_call" | custom-call | tf_op jit(solution)/shard_map/final/pallas_call | solution.py:728
  (7 shorter events, 0.0 us)
Async XLA Ops:
  0.0 0.9 %copy-start = (f32[5,1,32,128]{3,2,1,0:T(8,128)S(1)}, f32[5,1,32,128]{3,2,1,0:T(8,128)}, u32[]{:S(2)}) copy-start(f32[5,1,32,128]{3,2,1,0:T(8,128)} %param.8) | copy-start | bytes 245764
  0.9 14.2 %copy-start.1 = (f32[5,1,32,128]{3,2,1,0:T(8,128)S(1)}, f32[5,1,32,128]{3,2,1,0:T(8,128)}, u32[]{:S(2)}) copy-start(f32[5,1,32,128]{3,2,1,0:T(8,128)} %param.8) | copy-start | bytes 245764
  1.0 5.2 %collective-permute-start.2 = (f32[5,8,128]{2,1,0:T(8,128)S(1)}, f32[5,8,128]{2,1,0:T(8,128)S(1)}, u32[]{:S(2)}, u32[]{:S(2)}) collective-permute-start(f32[5,8,128]{2,1,0:T(8,128)S(1)} %bitcast.13), channel_id=1, source_target_pairs={{0,24},{8,16},{16,8},{24,0},{1,25},{9,17},{17,9},{25,1},{2,26},{10... | collective-permute-start | bytes 61448 | tf_op jit(solution)/shard_map/ppermute | solution.py:771
  3.5 3.8 %collective-permute-start.1 = (f32[5,8,128]{2,1,0:T(8,128)S(1)}, f32[5,8,128]{2,1,0:T(8,128)S(1)}, u32[]{:S(2)}, u32[]{:S(2)}) collective-permute-start(f32[5,8,128]{2,1,0:T(8,128)S(1)} %bitcast.14), channel_id=1, source_target_pairs={{0,16},{8,24},{16,0},{24,8},{1,17},{9,25},{17,1},{25,9},{2,18},{10... | collective-permute-start | bytes 61448 | tf_op jit(solution)/shard_map/ppermute | solution.py:771
  4.2 3.1 %collective-permute-start = (f32[5,8,128]{2,1,0:T(8,128)S(1)}, f32[5,8,128]{2,1,0:T(8,128)S(1)}, u32[]{:S(2)}, u32[]{:S(2)}) collective-permute-start(f32[5,8,128]{2,1,0:T(8,128)S(1)} %bitcast.15), channel_id=1, source_target_pairs={{0,8},{8,0},{16,24},{24,16},{1,9},{9,1},{17,25},{25,17},{2,10},{10... | collective-permute-start | bytes 61448 | tf_op jit(solution)/shard_map/ppermute | solution.py:771
  7.5 6.1 %collective-permute-start.4 = (f32[13,8,128]{2,1,0:T(8,128)S(1)}, f32[13,8,128]{2,1,0:T(8,128)S(1)}, u32[]{:S(2)}, u32[]{:S(2)}) collective-permute-start(f32[13,8,128]{2,1,0:T(8,128)S(1)} %get-tuple-element.39), channel_id=1, source_target_pairs={{0,2},{1,3},{2,4},{3,5},{4,6},{5,7},{6,0},{7,1},{8,9},{9,10},{10,1... | collective-permute-start | bytes 159752 | tf_op jit(solution)/shard_map/ppermute | solution.py:761
  9.1 4.7 %collective-permute-start.3 = (f32[13,8,128]{2,1,0:T(8,128)S(1)}, f32[13,8,128]{2,1,0:T(8,128)S(1)}, u32[]{:S(2)}, u32[]{:S(2)}) collective-permute-start(f32[13,8,128]{2,1,0:T(8,128)S(1)} %get-tuple-element.38.mine_ref), channel_id=1, source_target_pairs={{0,6},{1,7},{2,0},{3,1},{4,2},{5,3},{6,4},{7,5},{8,15},{9,8},{10,9... | collective-permute-start | bytes 159752 | tf_op jit(solution)/shard_map/ppermute | solution.py:761
  13.6 1.2 %collective-permute-start.6 = (f32[13,8,128]{2,1,0:T(8,128)S(1)}, f32[13,8,128]{2,1,0:T(8,128)S(1)}, u32[]{:S(2)}, u32[]{:S(2)}) collective-permute-start(f32[13,8,128]{2,1,0:T(8,128)S(1)} %collective-permute-done.4.got_before), channel_id=1, source_target_pairs={{0,8},{8,0},{16,24},{24,16},{1,9},{9,1},{17,25},{25,17},{2,10},{10... | collective-permute-start | bytes 159752 | tf_op jit(solution)/shard_map/ppermute | solution.py:764
  13.8 1.2 %collective-permute-start.5 = (f32[13,8,128]{2,1,0:T(8,128)S(1)}, f32[13,8,128]{2,1,0:T(8,128)S(1)}, u32[]{:S(2)}, u32[]{:S(2)}) collective-permute-start(f32[13,8,128]{2,1,0:T(8,128)S(1)} %collective-permute-done.3.got_after), channel_id=1, source_target_pairs={{0,8},{8,0},{16,24},{24,16},{1,9},{9,1},{17,25},{25,17},{2,10},{10... | collective-permute-start | bytes 159752 | tf_op jit(solution)/shard_map/ppermute | solution.py:764
  19.9 1.3 %collective-permute-start.7 = (f32[13,8,128]{2,1,0:T(8,128)S(1)}, f32[13,8,128]{2,1,0:T(8,128)S(1)}, u32[]{:S(2)}, u32[]{:S(2)}) collective-permute-start(f32[13,8,128]{2,1,0:T(8,128)S(1)} %get-tuple-element.55), channel_id=1, source_target_pairs={{0,8},{8,0},{16,24},{24,16},{1,9},{9,1},{17,25},{25,17},{2,10},{10... | collective-permute-start | bytes 159752 | tf_op jit(solution)/shard_map/ppermute | solution.py:764
  20.2 1.2 %collective-permute-start.8 = (f32[13,8,128]{2,1,0:T(8,128)S(1)}, f32[13,8,128]{2,1,0:T(8,128)S(1)}, u32[]{:S(2)}, u32[]{:S(2)}) collective-permute-start(f32[13,8,128]{2,1,0:T(8,128)S(1)} %get-tuple-element.56), channel_id=1, source_target_pairs={{0,8},{8,0},{16,24},{24,16},{1,9},{9,1},{17,25},{25,17},{2,10},{10... | collective-permute-start | bytes 159752 | tf_op jit(solution)/shard_map/ppermute | solution.py:764
  21.5 6.1 %collective-permute-start.9 = (f32[13,8,128]{2,1,0:T(8,128)S(1)}, f32[13,8,128]{2,1,0:T(8,128)S(1)}, u32[]{:S(2)}, u32[]{:S(2)}) collective-permute-start(f32[13,8,128]{2,1,0:T(8,128)S(1)} %get-tuple-element.57), channel_id=1, source_target_pairs={{0,2},{1,3},{2,4},{3,5},{4,6},{5,7},{6,0},{7,1},{8,9},{9,10},{10,1... | collective-permute-start | bytes 159752 | tf_op jit(solution)/shard_map/ppermute | solution.py:761
  22.7 5.3 %collective-permute-start.10 = (f32[13,8,128]{2,1,0:T(8,128)S(1)}, f32[13,8,128]{2,1,0:T(8,128)S(1)}, u32[]{:S(2)}, u32[]{:S(2)}) collective-permute-start(f32[13,8,128]{2,1,0:T(8,128)S(1)} %get-tuple-element.58), channel_id=1, source_target_pairs={{0,6},{1,7},{2,0},{3,1},{4,2},{5,3},{6,4},{7,5},{8,15},{9,8},{10,9... | collective-permute-start | bytes 159752 | tf_op jit(solution)/shard_map/ppermute | solution.py:761
  28.2 1.9 %collective-permute-start.11 = (f32[5,8,128]{2,1,0:T(8,128)S(1)}, f32[5,8,128]{2,1,0:T(8,128)S(1)}, u32[]{:S(2)}, u32[]{:S(2)}) collective-permute-start(f32[5,8,128]{2,1,0:T(8,128)S(1)} %get-tuple-element.60), channel_id=1, source_target_pairs={{0,8},{8,0},{16,24},{24,16},{1,9},{9,1},{17,25},{25,17},{2,10},{10... | collective-permute-start | bytes 61448 | tf_op jit(solution)/shard_map/ppermute | solution.py:844
  28.2 3.9 %collective-permute-start.12 = (f32[5,8,128]{2,1,0:T(8,128)S(1)}, f32[5,8,128]{2,1,0:T(8,128)S(1)}, u32[]{:S(2)}, u32[]{:S(2)}) collective-permute-start(f32[5,8,128]{2,1,0:T(8,128)S(1)} %get-tuple-element.61), channel_id=1, source_target_pairs={{0,16},{8,24},{16,0},{24,8},{1,17},{9,25},{17,1},{25,9},{2,18},{10... | collective-permute-start | bytes 61448 | tf_op jit(solution)/shard_map/ppermute | solution.py:844
  29.1 3.2 %collective-permute-start.13 = (f32[5,8,128]{2,1,0:T(8,128)S(1)}, f32[5,8,128]{2,1,0:T(8,128)S(1)}, u32[]{:S(2)}, u32[]{:S(2)}) collective-permute-start(f32[5,8,128]{2,1,0:T(8,128)S(1)} %get-tuple-element.62), channel_id=1, source_target_pairs={{0,24},{8,16},{16,8},{24,0},{1,25},{9,17},{17,9},{25,1},{2,26},{10... | collective-permute-start | bytes 61448 | tf_op jit(solution)/shard_map/ppermute | solution.py:844

commit v6 on v5

--- a/solution.py
+++ b/solution.py
@@ -342,11 +342,11 @@
     lane = lax.broadcasted_iota(jnp.int32, (width, lanes), 1)
     swapped = pltpu.roll(coefficients, half, 1)
     signed = jnp.where(lane < half, coefficients, -coefficients)
-    total_real, total_imag = [None] * 2, [None] * 2
+    total_real, total_imag = [None] * 4, [None] * 4
     for w in range(width):
         block = weights[layer, w]
-        total_real[w % 2] = added(total_real[w % 2], block * signed[w : w + 1])
-        total_imag[w % 2] = added(total_imag[w % 2], block * swapped[w : w + 1])
+        total_real[w % 4] = added(total_real[w % 4], block * signed[w : w + 1])
+        total_imag[w % 4] = added(total_imag[w % 4], block * swapped[w : w + 1])
     total_real, total_imag = sum(total_real), sum(total_imag)
     total_real += pltpu.roll(total_real, half, 1)
     total_imag += pltpu.roll(total_imag, half, 1)

time: 33.3 us -> 33.3 us (level)
  no operation moved by 1% of the time
where the time goes in v6:
time: 33.3 us; the launch traced here: 33.1 us
  starting transfers between devices  13.7 us (41%)
  waiting for transfers between devices  10.3 us (31%)
  Pallas kernels  8.15 us (24%)
  local copies, waits for them, and re-layouts  0.89 us (3%)
    pallas_call x7, Pallas kernels, call(): pl.pallas_call(kernel, out_shape=outs, in_specs=places, out_specs=out_pla...  8.15 us
    ppermute x4, starting transfers between devices, along_y(): return lax.ppermute(value, ('gx', 'gy'), pairs)  7.75 us
    ppermute x4, waiting for transfers between devices, along_y(): return lax.ppermute(value, ('gx', 'gy'), pairs)  5.11 us
    ppermute x3, starting transfers between devices, body(): lax.ppermute(packed, 'gx', chip.pairs(slot))  3.15 us
    ppermute x3, waiting for transfers between devices, body(): lax.ppermute(parts[slot], 'gx', chip.pairs(slot, back=True))  2.22 us
    ppermute x4, waiting for transfers between devices, swap(): return lax.ppermute(value, 'gx', [(s, s ^ 1) for s in range(gx)])  1.96 us
    ppermute x3, starting transfers between devices, body(): lax.ppermute(parts[slot], 'gx', chip.pairs(slot, back=True))  1.92 us
    ppermute x3, waiting for transfers between devices, body(): lax.ppermute(packed, 'gx', chip.pairs(slot))  1.05 us
  transfers between devices with their start and end apart: 14, of which 11 were waited for; matrix products, arithmetic and copies ran while one was open for 0% of the time, Pallas kernels for 6%

profile of v6, /device:TPU:0, one launch (start us, length us, event | category | flops | bytes accessed | tf_op | source)
XLA Modules:
  0.0 33.1 jit_solution(4799233852863618023)
XLA Ops:
  0.0 0.9 %copy-done = f32[5,1,32,128]{3,2,1,0:T(8,128)S(1)} copy-done((f32[5,1,32,128]{3,2,1,0:T(8,128)S(1)}, f32[5,1,32,128]{3,2,1,0:T(8,128)}, u32[]{:S(2)}) %copy-start) | copy-done | bytes 81944
  0.9 0.1 pool.1
  1.0 2.5 %collective-permute-start.2 = (f32[5,8,128]{2,1,0:T(8,128)S(1)}, f32[5,8,128]{2,1,0:T(8,128)S(1)}, u32[]{:S(2)}, u32[]{:S(2)}) collective-permute-start(f32[5,8,128]{2,1,0:T(8,128)S(1)} %bitcast.13), channel_id=1, source_target_pairs={{0,24},{8,16},{16,8},{24,0},{1,25},{9,17},{17,9},{25,1},{2,26},{10... | collective-permute-start | bytes 61448 | tf_op jit(solution)/shard_map/ppermute | solution.py:771
  3.5 0.6 %collective-permute-start.1 = (f32[5,8,128]{2,1,0:T(8,128)S(1)}, f32[5,8,128]{2,1,0:T(8,128)S(1)}, u32[]{:S(2)}, u32[]{:S(2)}) collective-permute-start(f32[5,8,128]{2,1,0:T(8,128)S(1)} %bitcast.14), channel_id=1, source_target_pairs={{0,16},{8,24},{16,0},{24,8},{1,17},{9,25},{17,1},{25,9},{2,18},{10... | collective-permute-start | bytes 61448 | tf_op jit(solution)/shard_map/ppermute | solution.py:771
  4.2 0.0 collective-permute-start
  4.2 2.0 %prepare.1 = (bf16[1152,256]{1,0:T(8,128)(2,1)S(1)}, bf16[256,1152]{1,0:T(8,128)(2,1)S(1)}, f32[2,32,32,128]{3,2,1,0:T(8,128)S(1)}, f32[16,32]{1,0:T(8,128)S(1)}...) custom-call(f32[160,128]{1,0:T(8,128)} %bitcast.20, ...), custom_call_target="tpu_custom_call" | custom-call | tf_op jit(solution)/shard_map/prepare/pallas_call | solution.py:728
  6.3 1.0 %collective-permute-done.1.refs_2_ = f32[5,8,128]{2,1,0:T(8,128)S(1)} collective-permute-done((f32[5,8,128]{2,1,0:T(8,128)S(1)}, f32[5,8,128]{2,1,0:T(8,128)S(1)}, u32[]{:S(2)}, u32[]{:S(2)}) %collective-permute-start.1) | collective-permute-done | bytes 20512 | tf_op jit(solution)/shard_map/ppermute | solution.py:771
  7.3 0.0 collective-permute-done.refs_1_.next_ref
  7.3 0.2 pack.1
  7.5 1.6 %collective-permute-start.4 = (f32[13,8,128]{2,1,0:T(8,128)S(1)}, f32[13,8,128]{2,1,0:T(8,128)S(1)}, u32[]{:S(2)}, u32[]{:S(2)}) collective-permute-start(f32[13,8,128]{2,1,0:T(8,128)S(1)} %get-tuple-element.39), channel_id=1, source_target_pairs={{0,2},{1,3},{2,4},{3,5},{4,6},{5,7},{6,0},{7,1},{8,9},{9,10},{10,1... | collective-permute-start | bytes 159752 | tf_op jit(solution)/shard_map/ppermute | solution.py:761
  9.1 2.2 %collective-permute-start.3 = (f32[13,8,128]{2,1,0:T(8,128)S(1)}, f32[13,8,128]{2,1,0:T(8,128)S(1)}, u32[]{:S(2)}, u32[]{:S(2)}) collective-permute-start(f32[13,8,128]{2,1,0:T(8,128)S(1)} %get-tuple-element.38.mine_ref), channel_id=1, source_target_pairs={{0,6},{1,7},{2,0},{3,1},{4,2},{5,3},{6,4},{7,5},{8,15},{9,8},{10,9... | collective-permute-start | bytes 159752 | tf_op jit(solution)/shard_map/ppermute | solution.py:761
  11.3 2.2 %collective-permute-done.4.got_before = f32[13,8,128]{2,1,0:T(8,128)S(1)} collective-permute-done((f32[13,8,128]{2,1,0:T(8,128)S(1)}, f32[13,8,128]{2,1,0:T(8,128)S(1)}, u32[]{:S(2)}, u32[]{:S(2)}) %collective-permute-start.4) | collective-permute-done | bytes 53280 | tf_op jit(solution)/shard_map/ppermute | solution.py:761
  13.6 0.2 collective-permute-done.3.got_after
  13.8 0.3 collective-permute-start.5
  14.1 0.7 %collective-permute-done.6.other_before = f32[13,8,128]{2,1,0:T(8,128)S(1)} collective-permute-done((f32[13,8,128]{2,1,0:T(8,128)S(1)}, f32[13,8,128]{2,1,0:T(8,128)S(1)}, u32[]{:S(2)}, u32[]{:S(2)}) %collective-permute-start.6) | collective-permute-done | bytes 53280 | tf_op jit(solution)/shard_map/ppermute | solution.py:764
  14.8 0.2 collective-permute-done.5.other_after
  15.0 4.8 %network.1 = (f32[5,32,128]{2,1,0:T(8,128)S(1)}, f32[5,16,128]{2,1,0:T(8,128)S(1)}, f32[5,8,128]{2,1,0:T(8,128)S(1)}, f32[13,8,128]{2,1,0:T(8,128)S(1)}, f32[13,...) custom-call(s32[1]{0:T(128)} %bitcast.core_ref, f32[5,32,128]{2,1,0:T(8,128)S(1)} %bitcast.12, ...), custom_call_target="tpu_custom_call" | custom-call | tf_op jit(solution)/shard_map/network/pallas_call | solution.py:728
  19.9 0.3 %collective-permute-start.7 = (f32[13,8,128]{2,1,0:T(8,128)S(1)}, f32[13,8,128]{2,1,0:T(8,128)S(1)}, u32[]{:S(2)}, u32[]{:S(2)}) collective-permute-start(f32[13,8,128]{2,1,0:T(8,128)S(1)} %get-tuple-element.55), channel_id=1, source_target_pairs={{0,8},{8,0},{16,24},{24,16},{1,9},{9,1},{17,25},{25,17},{2,10},{10... | collective-permute-start | bytes 159752 | tf_op jit(solution)/shard_map/ppermute | solution.py:764
  20.2 0.2 collective-permute-start.8
  20.4 0.7 %collective-permute-done.7.got_b = f32[13,8,128]{2,1,0:T(8,128)S(1)} collective-permute-done((f32[13,8,128]{2,1,0:T(8,128)S(1)}, f32[13,8,128]{2,1,0:T(8,128)S(1)}, u32[]{:S(2)}, u32[]{:S(2)}) %collective-permute-start.7) | collective-permute-done | bytes 53280 | tf_op jit(solution)/shard_map/ppermute | solution.py:764
  21.2 0.3 collective-permute-done.8.got_a
  21.5 1.3 %collective-permute-start.9 = (f32[13,8,128]{2,1,0:T(8,128)S(1)}, f32[13,8,128]{2,1,0:T(8,128)S(1)}, u32[]{:S(2)}, u32[]{:S(2)}) collective-permute-start(f32[13,8,128]{2,1,0:T(8,128)S(1)} %get-tuple-element.57), channel_id=1, source_target_pairs={{0,2},{1,3},{2,4},{3,5},{4,6},{5,7},{6,0},{7,1},{8,9},{9,10},{10,1... | collective-permute-start | bytes 159752 | tf_op jit(solution)/shard_map/ppermute | solution.py:761
  22.7 2.6 %collective-permute-start.10 = (f32[13,8,128]{2,1,0:T(8,128)S(1)}, f32[13,8,128]{2,1,0:T(8,128)S(1)}, u32[]{:S(2)}, u32[]{:S(2)}) collective-permute-start(f32[13,8,128]{2,1,0:T(8,128)S(1)} %get-tuple-element.58), channel_id=1, source_target_pairs={{0,6},{1,7},{2,0},{3,1},{4,2},{5,3},{6,4},{7,5},{8,15},{9,8},{10,9... | collective-permute-start | bytes 159752 | tf_op jit(solution)/shard_map/ppermute | solution.py:761
  25.3 2.2 %collective-permute-done.9.from_before = f32[13,8,128]{2,1,0:T(8,128)S(1)} collective-permute-done((f32[13,8,128]{2,1,0:T(8,128)S(1)}, f32[13,8,128]{2,1,0:T(8,128)S(1)}, u32[]{:S(2)}, u32[]{:S(2)}) %collective-permute-start.9) | collective-permute-done | bytes 53280 | tf_op jit(solution)/shard_map/ppermute | solution.py:761
  27.5 0.4 %collective-permute-done.10.from_after = f32[13,8,128]{2,1,0:T(8,128)S(1)} collective-permute-done((f32[13,8,128]{2,1,0:T(8,128)S(1)}, f32[13,8,128]{2,1,0:T(8,128)S(1)}, u32[]{:S(2)}, u32[]{:S(2)}) %collective-permute-start.10) | collective-permute-done | bytes 53280 | tf_op jit(solution)/shard_map/ppermute | solution.py:761
  28.0 0.2 gather.1
  28.2 0.1 collective-permute-start.11
  28.2 0.8 %collective-permute-start.12 = (f32[5,8,128]{2,1,0:T(8,128)S(1)}, f32[5,8,128]{2,1,0:T(8,128)S(1)}, u32[]{:S(2)}, u32[]{:S(2)}) collective-permute-start(f32[5,8,128]{2,1,0:T(8,128)S(1)} %get-tuple-element.61), channel_id=1, source_target_pairs={{0,16},{8,24},{16,0},{24,8},{1,17},{9,25},{17,1},{25,9},{2,18},{10... | collective-permute-start | bytes 61448 | tf_op jit(solution)/shard_map/ppermute | solution.py:844
  29.1 1.0 %collective-permute-start.13 = (f32[5,8,128]{2,1,0:T(8,128)S(1)}, f32[5,8,128]{2,1,0:T(8,128)S(1)}, u32[]{:S(2)}, u32[]{:S(2)}) collective-permute-start(f32[5,8,128]{2,1,0:T(8,128)S(1)} %get-tuple-element.62), channel_id=1, source_target_pairs={{0,24},{8,16},{16,8},{24,0},{1,25},{9,17},{17,9},{25,1},{2,26},{10... | collective-permute-start | bytes 61448 | tf_op jit(solution)/shard_map/ppermute | solution.py:844
  30.1 2.0 %collective-permute-done.12.refs_2_ = f32[5,8,128]{2,1,0:T(8,128)S(1)} collective-permute-done((f32[5,8,128]{2,1,0:T(8,128)S(1)}, f32[5,8,128]{2,1,0:T(8,128)S(1)}, u32[]{:S(2)}, u32[]{:S(2)}) %collective-permute-start.12) | collective-permute-done | bytes 20512 | tf_op jit(solution)/shard_map/ppermute | solution.py:844
  32.1 0.2 collective-permute-done.13.refs_3_
  32.3 0.8 %final.1 = f32[160,128]{1,0:T(8,128)} custom-call(f32[160,128]{1,0:T(8,128)S(1)} %bitcast.18, f32[5,8,128]{2,1,0:T(8,128)S(1)} %get-tuple-element.59.refs_0_, f32[5,8,128]{2,1,0:T(8,128)S(1)} %collective-permute-done.11.refs_1_, f32[5,8,128]{2,1,0:T(8,128)S(1)} %collective-permute-done.12.refs_2_, f32[5,8,128]{2,1,0:T(8,128)S(1)} %collective-permute-done.13.refs_3_), custom_call_target="tpu_custom_call" | custom-call | tf_op jit(solution)/shard_map/final/pallas_call | solution.py:728
  (7 shorter events, 0.0 us)
Async XLA Ops:
  0.0 0.9 %copy-start = (f32[5,1,32,128]{3,2,1,0:T(8,128)S(1)}, f32[5,1,32,128]{3,2,1,0:T(8,128)}, u32[]{:S(2)}) copy-start(f32[5,1,32,128]{3,2,1,0:T(8,128)} %param.8) | copy-start | bytes 245764
  0.9 14.2 %copy-start.1 = (f32[5,1,32,128]{3,2,1,0:T(8,128)S(1)}, f32[5,1,32,128]{3,2,1,0:T(8,128)}, u32[]{:S(2)}) copy-start(f32[5,1,32,128]{3,2,1,0:T(8,128)} %param.8) | copy-start | bytes 245764
  1.0 5.2 %collective-permute-start.2 = (f32[5,8,128]{2,1,0:T(8,128)S(1)}, f32[5,8,128]{2,1,0:T(8,128)S(1)}, u32[]{:S(2)}, u32[]{:S(2)}) collective-permute-start(f32[5,8,128]{2,1,0:T(8,128)S(1)} %bitcast.13), channel_id=1, source_target_pairs={{0,24},{8,16},{16,8},{24,0},{1,25},{9,17},{17,9},{25,1},{2,26},{10... | collective-permute-start | bytes 61448 | tf_op jit(solution)/shard_map/ppermute | solution.py:771
  3.5 3.8 %collective-permute-start.1 = (f32[5,8,128]{2,1,0:T(8,128)S(1)}, f32[5,8,128]{2,1,0:T(8,128)S(1)}, u32[]{:S(2)}, u32[]{:S(2)}) collective-permute-start(f32[5,8,128]{2,1,0:T(8,128)S(1)} %bitcast.14), channel_id=1, source_target_pairs={{0,16},{8,24},{16,0},{24,8},{1,17},{9,25},{17,1},{25,9},{2,18},{10... | collective-permute-start | bytes 61448 | tf_op jit(solution)/shard_map/ppermute | solution.py:771
  4.2 3.1 %collective-permute-start = (f32[5,8,128]{2,1,0:T(8,128)S(1)}, f32[5,8,128]{2,1,0:T(8,128)S(1)}, u32[]{:S(2)}, u32[]{:S(2)}) collective-permute-start(f32[5,8,128]{2,1,0:T(8,128)S(1)} %bitcast.15), channel_id=1, source_target_pairs={{0,8},{8,0},{16,24},{24,16},{1,9},{9,1},{17,25},{25,17},{2,10},{10... | collective-permute-start | bytes 61448 | tf_op jit(solution)/shard_map/ppermute | solution.py:771
  7.5 6.1 %collective-permute-start.4 = (f32[13,8,128]{2,1,0:T(8,128)S(1)}, f32[13,8,128]{2,1,0:T(8,128)S(1)}, u32[]{:S(2)}, u32[]{:S(2)}) collective-permute-start(f32[13,8,128]{2,1,0:T(8,128)S(1)} %get-tuple-element.39), channel_id=1, source_target_pairs={{0,2},{1,3},{2,4},{3,5},{4,6},{5,7},{6,0},{7,1},{8,9},{9,10},{10,1... | collective-permute-start | bytes 159752 | tf_op jit(solution)/shard_map/ppermute | solution.py:761
  9.1 4.7 %collective-permute-start.3 = (f32[13,8,128]{2,1,0:T(8,128)S(1)}, f32[13,8,128]{2,1,0:T(8,128)S(1)}, u32[]{:S(2)}, u32[]{:S(2)}) collective-permute-start(f32[13,8,128]{2,1,0:T(8,128)S(1)} %get-tuple-element.38.mine_ref), channel_id=1, source_target_pairs={{0,6},{1,7},{2,0},{3,1},{4,2},{5,3},{6,4},{7,5},{8,15},{9,8},{10,9... | collective-permute-start | bytes 159752 | tf_op jit(solution)/shard_map/ppermute | solution.py:761
  13.6 1.2 %collective-permute-start.6 = (f32[13,8,128]{2,1,0:T(8,128)S(1)}, f32[13,8,128]{2,1,0:T(8,128)S(1)}, u32[]{:S(2)}, u32[]{:S(2)}) collective-permute-start(f32[13,8,128]{2,1,0:T(8,128)S(1)} %collective-permute-done.4.got_before), channel_id=1, source_target_pairs={{0,8},{8,0},{16,24},{24,16},{1,9},{9,1},{17,25},{25,17},{2,10},{10... | collective-permute-start | bytes 159752 | tf_op jit(solution)/shard_map/ppermute | solution.py:764
  13.8 1.2 %collective-permute-start.5 = (f32[13,8,128]{2,1,0:T(8,128)S(1)}, f32[13,8,128]{2,1,0:T(8,128)S(1)}, u32[]{:S(2)}, u32[]{:S(2)}) collective-permute-start(f32[13,8,128]{2,1,0:T(8,128)S(1)} %collective-permute-done.3.got_after), channel_id=1, source_target_pairs={{0,8},{8,0},{16,24},{24,16},{1,9},{9,1},{17,25},{25,17},{2,10},{10... | collective-permute-start | bytes 159752 | tf_op jit(solution)/shard_map/ppermute | solution.py:764
  19.9 1.3 %collective-permute-start.7 = (f32[13,8,128]{2,1,0:T(8,128)S(1)}, f32[13,8,128]{2,1,0:T(8,128)S(1)}, u32[]{:S(2)}, u32[]{:S(2)}) collective-permute-start(f32[13,8,128]{2,1,0:T(8,128)S(1)} %get-tuple-element.55), channel_id=1, source_target_pairs={{0,8},{8,0},{16,24},{24,16},{1,9},{9,1},{17,25},{25,17},{2,10},{10... | collective-permute-start | bytes 159752 | tf_op jit(solution)/shard_map/ppermute | solution.py:764
  20.2 1.2 %collective-permute-start.8 = (f32[13,8,128]{2,1,0:T(8,128)S(1)}, f32[13,8,128]{2,1,0:T(8,128)S(1)}, u32[]{:S(2)}, u32[]{:S(2)}) collective-permute-start(f32[13,8,128]{2,1,0:T(8,128)S(1)} %get-tuple-element.56), channel_id=1, source_target_pairs={{0,8},{8,0},{16,24},{24,16},{1,9},{9,1},{17,25},{25,17},{2,10},{10... | collective-permute-start | bytes 159752 | tf_op jit(solution)/shard_map/ppermute | solution.py:764
  21.5 6.1 %collective-permute-start.9 = (f32[13,8,128]{2,1,0:T(8,128)S(1)}, f32[13,8,128]{2,1,0:T(8,128)S(1)}, u32[]{:S(2)}, u32[]{:S(2)}) collective-permute-start(f32[13,8,128]{2,1,0:T(8,128)S(1)} %get-tuple-element.57), channel_id=1, source_target_pairs={{0,2},{1,3},{2,4},{3,5},{4,6},{5,7},{6,0},{7,1},{8,9},{9,10},{10,1... | collective-permute-start | bytes 159752 | tf_op jit(solution)/shard_map/ppermute | solution.py:761
  22.7 5.3 %collective-permute-start.10 = (f32[13,8,128]{2,1,0:T(8,128)S(1)}, f32[13,8,128]{2,1,0:T(8,128)S(1)}, u32[]{:S(2)}, u32[]{:S(2)}) collective-permute-start(f32[13,8,128]{2,1,0:T(8,128)S(1)} %get-tuple-element.58), channel_id=1, source_target_pairs={{0,6},{1,7},{2,0},{3,1},{4,2},{5,3},{6,4},{7,5},{8,15},{9,8},{10,9... | collective-permute-start | bytes 159752 | tf_op jit(solution)/shard_map/ppermute | solution.py:761
  28.2 1.9 %collective-permute-start.11 = (f32[5,8,128]{2,1,0:T(8,128)S(1)}, f32[5,8,128]{2,1,0:T(8,128)S(1)}, u32[]{:S(2)}, u32[]{:S(2)}) collective-permute-start(f32[5,8,128]{2,1,0:T(8,128)S(1)} %get-tuple-element.60), channel_id=1, source_target_pairs={{0,8},{8,0},{16,24},{24,16},{1,9},{9,1},{17,25},{25,17},{2,10},{10... | collective-permute-start | bytes 61448 | tf_op jit(solution)/shard_map/ppermute | solution.py:844
  28.2 3.9 %collective-permute-start.12 = (f32[5,8,128]{2,1,0:T(8,128)S(1)}, f32[5,8,128]{2,1,0:T(8,128)S(1)}, u32[]{:S(2)}, u32[]{:S(2)}) collective-permute-start(f32[5,8,128]{2,1,0:T(8,128)S(1)} %get-tuple-element.61), channel_id=1, source_target_pairs={{0,16},{8,24},{16,0},{24,8},{1,17},{9,25},{17,1},{25,9},{2,18},{10... | collective-permute-start | bytes 61448 | tf_op jit(solution)/shard_map/ppermute | solution.py:844
  29.1 3.2 %collective-permute-start.13 = (f32[5,8,128]{2,1,0:T(8,128)S(1)}, f32[5,8,128]{2,1,0:T(8,128)S(1)}, u32[]{:S(2)}, u32[]{:S(2)}) collective-permute-start(f32[5,8,128]{2,1,0:T(8,128)S(1)} %get-tuple-element.62), channel_id=1, source_target_pairs={{0,24},{8,16},{16,8},{24,0},{1,25},{9,17},{17,9},{25,1},{2,26},{10... | collective-permute-start | bytes 61448 | tf_op jit(solution)/shard_map/ppermute | solution.py:844
